TPU v7x, 256 devices: a whole 4x4x8 slice. The times are simulated.
256 devices in a mesh: crop: 2 (over y_hi), rows: 16 (over y_lo, x, core), hid: 8 (over z).
Axes of the slice: x: 4, y: 4 (y_hi: 2, y_lo: 2; y = y_hi * 2 + y_lo), z: 8, core: 2. Of those that a mesh axis runs over, the one named last changes fastest.
Arguments:
- tokens: bfloat16 [2, 32, 64, 4096], P('crop', 'rows', None, 'hid'), may hold values from -6 to 6
- cotangent: bfloat16 [2, 32, 64, 4096], P('crop', 'rows', None, 'hid'), may hold values from -6 to 6
- weight_in: bfloat16 [256, 64, 5, 256], P('rows', 'hid'), may hold values from -0.15625 to 0.15625
- weight_out: bfloat16 [256, 64, 5, 256], P('rows', 'hid'), may hold values from -0.078125 to 0.078125
- mix_kernel: float32 [9, 16384], P(None, 'hid'), may hold values from -4 to 4
- block_rows: int32 [64, 5], P('hid'), may hold values from 0 to 15, as said below
Outputs:
- grad_tokens: bfloat16 [2, 32, 64, 4096], P('crop', 'rows', None, 'hid')
- grad_w_in: float32 [256, 64, 5, 256], P(('crop', 'rows'), 'hid')
- grad_w_out: float32 [256, 64, 5, 256], P(('crop', 'rows'), 'hid')
- grad_kernel: float32 [9, 16384], P(None, 'hid')
Inputs may be any that keep to these rules, and one draw needn't show every extreme that they name: In each block column c, block_rows[c, 0] is a label L and block_rows[c, k] for k >= 1 is L with bit k - 1 flipped, so the 5 entries of a column differ; every value is the label of equally many block columns.
All inputs are finite; a program needn't handle non-finite values.
Results may differ from a plain program's by a relative error of at most 0.019.
Values may be sent and summed in bfloat16 or wider, within the bound.
No kernel may reach another device: no remote copies, remote signals or barrier semaphores. Data moves between devices by JAX's collectives and lax.ppermute only.
A program may use at most 128 MiB of HBM per device.

v0:
```python
import jax
import jax.numpy as jnp
from jax import lax
from jax.experimental import pallas as pl
from jax.experimental.pallas import tpu as pltpu
from jax.sharding import PartitionSpec as P

root_two_pi = 0.7978845608
cubic_coef = 0.044715
loss_scale = 0.03125

F32, BF16 = jnp.float32, jnp.bfloat16
NX, NY, NZ = 4, 4, 8
COLS, NNZ, BS, PW = 8, 5, 256, 64
TOK, KERN = 256, 20
CORE, XPOS, YPOS, YLO, ZPOS = 40, 41, 42, 43, 44
ANY = pl.BlockSpec(memory_space=pl.ANY)
VMEM = pl.BlockSpec(memory_space=pltpu.VMEM)
SMEM = pl.BlockSpec(memory_space=pltpu.SMEM)


def by_core(value, step0, step1):
    pairs = []
    for y in range(NY):
        for x in range(NX):
            for c, (dy, dx) in enumerate((step0, step1)):
                target = (y + dy) % NY * 8 + (x + dx) % NX * 2 + c
                pairs.append((y * 8 + x * 2 + c, target))
    return lax.ppermute(value, ("crop", "rows"), pairs)


def first(value, step):
    return by_core(value, (step, 0), (0, step))


def second(value, step):
    return by_core(value, (0, step), (step, 0))


def to_partner(value):
    return lax.ppermute(value, "rows", [(r, r ^ 1) for r in range(16)])


def to_next_chip(value, step):
    pairs = []
    for q in range(8):
        if 0 <= q + step < 8:
            pairs += [(q * 2 + c, (q + step) * 2 + 1 - c) for c in range(2)]
    return lax.ppermute(value, "rows", pairs)


def along_z(value, step):
    return lax.ppermute(value, "hid", [(z, (z + step) % NZ) for z in range(NZ)])


def dot(a, b, dims):
    return lax.dot_general(a, b, (dims, ((), ())), preferred_element_type=F32)


def local(kernel, name, outs, args, scratch=(), flops=2**20, hbm=()):
    shapes = [jax.ShapeDtypeStruct(s, t) for s, t in outs]
    size = sum(a.size * a.dtype.itemsize for a in args[1:])
    return pl.pallas_call(
        kernel,
        out_shape=shapes,
        in_specs=[SMEM] + [ANY if i in hbm else VMEM for i in range(1, len(args))],
        out_specs=[VMEM] * len(outs),
        scratch_shapes=list(scratch),
        compiler_params=pltpu.CompilerParams(vmem_limit_bytes=28 * 2**20),
        cost_estimate=pl.CostEstimate(flops=flops, transcendentals=0, bytes_accessed=size),
        name=name,
    )(*args)


def lanes(c):
    return pl.ds(pl.multiple_of(c * BS, BS), BS)


def start_tokens(meta, pieces, buf, sem):
    z = meta[ZPOS]
    own, r1, r2, r3, l1, l2, l3, r4, l4 = pieces
    plan = [(own, 0, 0), (r1, 7, 0), (r2, 6, 0), (r3, 5, 0), (l1, 1, 0), (l2, 2, 0), (l3, 3, 0)]
    for src, d, at in plan + [(r4, 4, 0), (l4, 4, 128)]:
        h = (z + d) % NZ
        for part in range(2):
            rows = pl.ds(at, src.shape[0])
            target = buf.at[2 * h + part, rows]
            pltpu.make_async_copy(src.at[:, pl.ds(part * BS, BS)], target, sem).start()


def weight_plan(meta, pieces):
    core, x, ylo = meta[CORE], meta[XPOS], meta[YLO]
    own, r1, r2, r3, r4, r5, r6, r7, r8, r9 = pieces
    here, there = ylo * NX, (1 - ylo) * NX
    at = lambda base, d: base + (x + d) % NX
    pick = lambda a, b: jnp.where(core == 0, a, b)
    slots = [
        (own, at(here, 0)),
        (r1, pick(at(here, 3), at(there, 0))),
        (r2, pick(at(here, 1), at(here, 3))),
        (r3, pick(at(there, 0), at(here, 1))),
        (r4, pick(at(there, 3), at(there, 1))),
        (r5, pick(at(there, 1), at(there, 3))),
    ]
    plan = [(src, s, 2 * j + s) for src, j in slots for s in range(2)]
    for j, a, b in ((at(here, 2), r6, r7), (at(there, 2), r8, r9)):
        plan += [(a, 0, 2 * j), (b, 0, 2 * j + 1)]
    return plan


def forward_kernel(meta, *refs):
    tokens, pieces, outs = refs[:9], refs[9:19], refs[19:]
    pre, out, top, bot, wts, tok, sem = outs
    start_tokens(meta, tokens, tok, sem)
    plan = weight_plan(meta, pieces)
    core = meta[CORE]

    @pl.loop(0, COLS)
    def _(c):
        for k in range(NNZ):
            for src, row, slot in plan:
                wts[c, k, slot] = src[row, c, k]

    pltpu.make_async_copy(tok, tok, sem).wait()

    def total(c, dims):
        acc = None
        for k in range(NNZ):
            part = dot(tok[meta[c * NNZ + k]], wts[c, k].reshape(BS, BS), dims)
            acc = part if acc is None else acc + part
        return acc

    @pl.when(core == 0)
    def _():
        @pl.loop(0, COLS)
        def _(c):
            p = total(c, ((1,), (0,)))
            pre[:, lanes(c)] = p
            t = jnp.tanh(root_two_pi * (p + cubic_coef * p * p * p))
            out[:, lanes(c)] = (0.5 * p * (1.0 + t)).astype(BF16)

    @pl.when(core != 0)
    def _():
        @pl.loop(0, COLS)
        def _(c):
            out[:, lanes(c)] = total(c, ((1,), (1,))).astype(BF16)

    top[...] = out[:PW]
    bot[...] = out[TOK - PW :]


def forward(meta, tokens, pieces):
    wide = COLS * BS
    outs = [((TOK, wide), F32), ((TOK, wide), BF16), ((PW, wide), BF16), ((PW, wide), BF16)]
    outs += [((COLS, NNZ, 16, 16, BS), BF16), ((16, TOK, BS), BF16)]
    return local(
        forward_kernel,
        "forward",
        outs,
        (meta, *tokens, *pieces),
        [pltpu.SemaphoreType.DMA],
        flops=2 * TOK * BS * BS * NNZ * COLS,
        hbm=range(1, 10),
    )


def shifted_rows(mid, up, down, cols):
    cells = lax.broadcasted_iota(jnp.int32, (PW, BS), 0)
    out = []
    for row in [up[:, cols]] + [mid[i * PW : (i + 1) * PW, cols] for i in range(4)] + [down[:, cols]]:
        row = row.astype(F32)
        left = jnp.where(cells == 0, 0.0, pltpu.roll(row, 1, 0))
        right = jnp.where(cells == PW - 1, 0.0, pltpu.roll(row, PW - 1, 0))
        out.append((left, row, right))
    return out


def backward_kernel(meta, tok, got, mine, up, down, pre, taps, *refs):
    g0, g1, g3, g2a, g2b, pgrad, conv, lhs, res, slab, moved = refs
    core, x, y = meta[CORE], meta[XPOS], meta[YPOS]
    is_in = core == 0
    slab[...] = jnp.zeros_like(slab)
    here = jnp.where(is_in, y, x)
    far = jnp.where(is_in, NX, 1)
    near = jnp.where(is_in, 1, NY)

    @pl.loop(0, COLS)
    def _(c):
        cols = lanes(c)
        for i, rows in enumerate(shifted_rows(got, up, down, cols)):
            for b in range(3):
                moved[3 * i + b] = rows[b]
        tap = [jnp.where(is_in, taps[8 - j : 9 - j, cols], taps[j : j + 1, cols]) for j in range(9)]
        for i in range(4):
            acc = jnp.zeros((PW, BS), F32)
            for a in range(3):
                for b in range(3):
                    acc += tap[3 * a + b] * moved[3 * (i + a) + b]
            conv[i * PW : (i + 1) * PW] = acc

        @pl.when(is_in)
        def _():
            p = pre[:, cols]
            t = jnp.tanh(root_two_pi * (p + cubic_coef * p * p * p))
            slope = 0.5 * (1.0 + t) + 0.5 * p * (1.0 - t * t) * root_two_pi * (
                1.0 + 3.0 * cubic_coef * p * p
            )
            lhs[...] = (conv[...] * slope).astype(BF16)
            pgrad[:, cols] = lhs[...]
            for k in range(NNZ):
                part = dot(tok[meta[c * NNZ + k]], lhs[...], ((0,), (0,))) * loss_scale
                res[k] = part.astype(BF16).reshape(16, 16, BS)

        @pl.when(core != 0)
        def _():
            lhs[...] = conv[...].astype(BF16)
            for k in range(NNZ):
                part = dot(lhs[...], tok[meta[c * NNZ + k]], ((0,), (0,))) * loss_scale
                res[k] = part.astype(BF16).reshape(16, 16, BS)
            sums = []
            for a in range(3):
                for b in range(3):
                    acc = jnp.zeros((PW, BS), F32)
                    for i in range(4):
                        acc += moved[3 * (i + a) + b] * mine[i * PW : (i + 1) * PW, cols].astype(F32)
                    sums.append(jnp.sum(acc, axis=0, keepdims=True))
            rows = jnp.concatenate(sums + [jnp.zeros((7, BS), F32)], axis=0) * loss_scale
            slab[...] = rows.astype(BF16)

        def emit(out, d, at):
            start = (here + d) % 4 * far
            for k in range(NNZ):
                for s in range(4):
                    out[at, k * 4 + s] = res[k, start + s * near]
            out[at, KERN] = slab[...]

        emit(g0, 0, c)
        emit(g1, 1, c)
        emit(g3, 3, c)

        @pl.when(c < COLS // 2)
        def _():
            emit(g2a, 2, c)

        @pl.when(c >= COLS // 2)
        def _():
            emit(g2b, 2, c - COLS // 2)


def backward(meta, tok, got, mine, up, down, pre, taps):
    full, part = (COLS, KERN + 1, 16, BS), (COLS // 2, KERN + 1, 16, BS)
    outs = [(full, BF16)] * 3 + [(part, BF16)] * 2 + [((TOK, COLS * BS), BF16)]
    scratch = [
        pltpu.VMEM((TOK, BS), F32),
        pltpu.VMEM((TOK, BS), BF16),
        pltpu.VMEM((NNZ, 16, 16, BS), BF16),
        pltpu.VMEM((16, BS), BF16),
        pltpu.VMEM((18, PW, BS), F32),
    ]
    args = (meta, tok, got, mine, up, down, pre, taps)
    return local(
        backward_kernel, "backward", outs, args, scratch, flops=2 * TOK * BS * BS * NNZ * COLS
    )


def token_grad_kernel(meta, pgrad, wts, keep, send, acc):
    @pl.when(meta[CORE] == 0)
    def _():
        acc[...] = jnp.zeros_like(acc)

        @pl.loop(0, COLS)
        def _(c):
            for k in range(NNZ):
                wt = wts[c, k].reshape(BS, BS)
                acc[meta[c * NNZ + k]] += dot(pgrad[:, lanes(c)], wt, ((1,), (1,)))

        @pl.loop(0, 16)
        def _(r):
            keep[r] = acc[r, :128].astype(BF16)
            send[r] = acc[r, 128:].astype(BF16)


def token_grad(meta, pgrad, wts):
    return local(
        token_grad_kernel,
        "tokengrad",
        [((16, 128, BS), BF16)] * 2,
        (meta, pgrad, wts),
        [pltpu.VMEM((16, TOK, BS), F32)],
        flops=2 * TOK * BS * BS * NNZ * COLS,
    )


def gather_sum_kernel(meta, parts, out):
    for b in range(2):
        total = parts[b].astype(F32)
        for z in range(1, NZ):
            total += parts[2 * z + b].astype(F32)
        out[:, b * BS : (b + 1) * BS] = total.astype(BF16)


def relay_kernel(meta, g1, g3, ra, rb, o1, o3):
    for out, own, got, first_half in ((o1, g1, ra, 0), (o3, g3, rb, COLS // 2)):

        @pl.loop(0, COLS // 2)
        def _(c):
            at, other = c + first_half, c + COLS // 2 - first_half
            for k in range(KERN):
                out[at, k] = (own[at, k].astype(F32) + got[c, k].astype(F32)).astype(BF16)
                out[other, k] = own[other, k]
            out[at, KERN] = own[at, KERN]
            out[other, KERN] = own[other, KERN]
            out[at, KERN + 1] = got[c, KERN]
            out[other, KERN + 1] = own[other, KERN]


def relay(meta, g1, g3, ra, rb):
    shape = ((COLS, KERN + 2, 16, BS), BF16)
    return local(relay_kernel, "relay", [shape] * 2, (meta, g1, g3, ra, rb))


def first_sum_kernel(meta, own, prev, nxt, *outs):
    here = jnp.where(meta[CORE] == 0, meta[XPOS], meta[YPOS])

    @pl.loop(0, COLS)
    def _(c):
        far = jnp.where(c < COLS // 2, prev[c, KERN + 1], nxt[c, KERN + 1]).astype(F32)
        near = prev[c, KERN].astype(F32) + nxt[c, KERN].astype(F32)
        slab = ((own[c, KERN].astype(F32) + far) + near).astype(BF16)
        for d in range(4):
            s = (here + d) % 4
            for k in range(NNZ):
                at = k * 4 + s
                total = own[c, at].astype(F32) + prev[c, at].astype(F32) + nxt[c, at].astype(F32)
                outs[d][c, k] = total.astype(BF16)
            outs[d][c, NNZ] = slab


def second_sum_kernel(meta, own, prev, nxt, far, keep, send):
    first_core = meta[CORE] == 0

    @pl.loop(0, COLS)
    def _(c):
        for k in range(NNZ + 1):
            a, b, e, f = (r[c, k].astype(F32) for r in (own, prev, nxt, far))
            total = ((a + f) + (b + e)).astype(BF16)
            low, high = total[:8], total[8:]
            if k < NNZ:
                keep[c, k] = jnp.where(first_core, low, high)
                send[c, k] = jnp.where(first_core, high, low)
            else:
                for out in (keep, send):
                    out[c, NNZ] = low
                    out[c, NNZ + 1] = high


def place_kernel(meta, keep, got, win, wout, kern):
    is_in = meta[CORE] == 0

    @pl.loop(0, NNZ)
    def _(k):
        mine = jnp.stack([keep[c, k].astype(F32) for c in range(COLS)], axis=0)
        its = jnp.stack([got[c, k].astype(F32) for c in range(COLS)], axis=0)
        mine, its = jnp.swapaxes(mine, 0, 1), jnp.swapaxes(its, 0, 1)
        win[:, k] = jnp.where(is_in, mine, its)
        wout[:, k] = jnp.where(is_in, its, mine)

    for c in range(COLS):
        rows = [jnp.where(is_in, got[c, NNZ + i], keep[c, NNZ + i]).astype(F32) for i in range(2)]
        kern[:, c * BS : (c + 1) * BS] = jnp.concatenate(rows, axis=0)[:9]


def on_device(tokens, cotangent, weight_in, weight_out, mix_kernel, block_rows):
    row, crop, z = lax.axis_index("rows"), lax.axis_index("crop"), lax.axis_index("hid")
    core, x, ylo = row % 2, row // 2 % NX, row // 8
    place = jnp.stack([core, x, crop * 2 + ylo, ylo, z]).astype(jnp.int32)
    meta = jnp.concatenate([block_rows.reshape(-1), place])
    is_in = core == 0

    def side(a, b):
        mine, theirs = jnp.where(is_in, a, b), jnp.where(is_in, b, a)
        got = to_partner(theirs)
        return jnp.where(is_in, mine, got), jnp.where(is_in, got, mine)

    own = jnp.stack(side(*(w.transpose(1, 2, 0, 3) for w in (weight_in, weight_out))))
    t0 = jnp.concatenate(side(tokens.reshape(128, 512), cotangent.reshape(128, 512)))

    r1 = by_core(own, (0, 1), (1, 0))
    r2 = by_core(own, (0, -1), (0, 1))
    r3 = by_core(own, (-1, 0), (0, -1))
    zr1, zl1 = along_z(t0, 1), along_z(t0, -1)
    r4 = by_core(r1, (1, 0), (0, -1))
    r5 = by_core(r2, (-1, 0), (-1, 0))
    zr2, zl2 = along_z(zr1, 1), along_z(zl1, -1)
    r6 = by_core(jnp.where(is_in, r1[:1], r2[:1]), (0, 1), (0, 1))
    r7 = by_core(jnp.where(is_in, r2[1:], r3[1:]), (0, -1), (0, -1))
    zr3, zl3 = along_z(zr2, 1), along_z(zl2, -1)
    r8 = by_core(r6, (1, 0), (1, 0))
    r9 = by_core(r7, (-1, 0), (-1, 0))
    zr4, zl4 = along_z(zr3[:128], 1), along_z(zl3[128:], -1)
    pieces = (own, r1, r2, r3, r4, r5, r6, r7, r8, r9)
    token_pieces = (t0, zr1, zr2, zr3, zl1, zl2, zl3, zr4, zl4)

    pre, out, top, bot, wts, tok = forward(meta, token_pieces, pieces)
    got = to_partner(out)
    up, down = to_next_chip(bot, 1), to_next_chip(top, -1)
    g0, g1, g3, g2a, g2b, pgrad = backward(meta, tok, got, out, up, down, pre, mix_kernel)
    ra, rb = first(g2a, 1), first(g2b, -1)

    keep, send = token_grad(meta, pgrad, wts)
    terms = jnp.where(is_in, keep, to_partner(send))
    terms = lax.all_to_all(terms, "hid", 0, 0, tiled=True)
    (grad_tokens,) = local(gather_sum_kernel, "gathersum", [((128, 512), BF16)], (meta, terms))

    g1, g3 = relay(meta, g1, g3, ra, rb)
    h = local(
        first_sum_kernel,
        "firstsum",
        [((COLS, NNZ + 1, 16, BS), BF16)] * 4,
        (meta, g0, first(g1, 1), first(g3, -1)),
    )
    last = (h[0], second(h[1], 1), second(h[3], -1), second(h[2], 2))
    shape = ((COLS, NNZ + 2, 8, BS), BF16)
    kept, sent = local(second_sum_kernel, "secondsum", [shape] * 2, (meta, *last))
    out_shape = ((8, NNZ, 8, BS), F32)
    win, wout, kern = local(
        place_kernel,
        "place",
        [out_shape, out_shape, ((9, 8 * BS), F32)],
        (meta, kept, to_partner(sent)),
    )
    grad_tokens = grad_tokens.reshape(1, 2, PW, 512)
    return grad_tokens, win.transpose(0, 2, 1, 3), wout.transpose(0, 2, 1, 3), kern


def solution(mesh):
    placed = (
        P("crop", "rows", None, "hid"),
        P("crop", "rows", None, "hid"),
        P("rows", "hid", None, None),
        P("rows", "hid", None, None),
        P(None, "hid"),
        P("hid", None),
    )
    return jax.shard_map(
        on_device,
        mesh=mesh,
        in_specs=placed,
        out_specs=(
            P("crop", "rows", None, "hid"),
            P(("crop", "rows"), "hid", None, None),
            P(("crop", "rows"), "hid", None, None),
            P(None, "hid"),
        ),
        check_vma=False,
    )
```

profile of v0, /device:TPU:1, one launch (start us, length us, event | category | flops | bytes accessed | tf_op | source)
XLA Modules:
  0.0 158.8 jit_solution(8663548821438267265)
XLA Ops:
  1.9 3.3 %collective-permute-start.9 = (bf16[8,5,16,256]{3,2,1,0:T(8,128)(2,1)S(1)}, bf16[8,5,16,256]{3,2,1,0:T(8,128)(2,1)S(1)}, u32[]{:S(2)}, u32[]{:S(2)}) collective-permute-start(bf16[8,5,16,256]{3,2,1,0:T(8,128)(2,1)S(1)} %select_bitcast_fusion), channel_id=1, source_target_pairs={{0,8},{8,0},{16,24},{24,16},{32,40},{40,32},{48,56},{56,48},{64,72... | collective-permute-start | bytes 983048 | tf_op jit(solution)/shard_map/ppermute | solution.py:41
  8.9 5.7 %collective-permute-start.4 = (bf16[256,512]{1,0:T(8,128)(2,1)S(1)}, bf16[256,512]{1,0:T(8,128)(2,1)S(1)}, u32[]{:S(2)}, u32[]{:S(2)}) collective-permute-start(bf16[256,512]{1,0:T(8,128)(2,1)S(1)} %pad_maximum_fusion.1.refs_0_), channel_id=1, source_target_pairs={{0,7},{1,0},{2,1},{3,2},{4,3},{5,4},{6,5},{7,6},{8,15},{9,8},{10,9... | collective-permute-start | bytes 786440 | tf_op jit(solution)/shard_map/ppermute | solution.py:53
  14.5 3.3 %collective-permute-done.4.refs_4_ = bf16[256,512]{1,0:T(8,128)(2,1)S(1)} collective-permute-done((bf16[256,512]{1,0:T(8,128)(2,1)S(1)}, bf16[256,512]{1,0:T(8,128)(2,1)S(1)}, u32[]{:S(2)}, u32[]{:S(2)}) %collective-permute-start.4) | collective-permute-done | bytes 262176 | tf_op jit(solution)/shard_map/ppermute | solution.py:53
  17.9 3.4 %collective-permute-start.5 = (bf16[256,512]{1,0:T(8,128)(2,1)S(1)}, bf16[256,512]{1,0:T(8,128)(2,1)S(1)}, u32[]{:S(2)}, u32[]{:S(2)}) collective-permute-start(bf16[256,512]{1,0:T(8,128)(2,1)S(1)} %collective-permute-done.4.refs_4_), channel_id=1, source_target_pairs={{0,7},{1,0},{2,1},{3,2},{4,3},{5,4},{6,5},{7,6},{8,15},{9,8},{10,9... | collective-permute-start | bytes 786440 | tf_op jit(solution)/shard_map/ppermute | solution.py:53
  22.0 2.6 %collective-permute-done.5.refs_5_ = bf16[256,512]{1,0:T(8,128)(2,1)S(1)} collective-permute-done((bf16[256,512]{1,0:T(8,128)(2,1)S(1)}, bf16[256,512]{1,0:T(8,128)(2,1)S(1)}, u32[]{:S(2)}, u32[]{:S(2)}) %collective-permute-start.5) | collective-permute-done | bytes 262176 | tf_op jit(solution)/shard_map/ppermute | solution.py:53
  24.6 3.4 %collective-permute-start.6 = (bf16[256,512]{1,0:T(8,128)(2,1)S(1)}, bf16[256,512]{1,0:T(8,128)(2,1)S(1)}, u32[]{:S(2)}, u32[]{:S(2)}) collective-permute-start(bf16[256,512]{1,0:T(8,128)(2,1)S(1)} %collective-permute-done.5.refs_5_), channel_id=1, source_target_pairs={{0,7},{1,0},{2,1},{3,2},{4,3},{5,4},{6,5},{7,6},{8,15},{9,8},{10,9... | collective-permute-start | bytes 786440 | tf_op jit(solution)/shard_map/ppermute | solution.py:53
  28.1 2.8 %collective-permute-start.16 = (bf16[1,8,5,16,256]{4,3,2,1,0:T(8,128)(2,1)S(1)}, bf16[1,8,5,16,256]{4,3,2,1,0:T(8,128)(2,1)}, u32[]{:S(2)}, u32[]{:S(2)}) collective-permute-start(bf16[1,8,5,16,256]{4,3,2,1,0:T(8,128)(2,1)S(1)} %get-tuple-element.56), channel_id=1, source_target_pairs={{0,48},{8,56},{16,0},{24,8},{32,16},{40,24},{48,32},{56,40},{64,11... | collective-permute-start | bytes 983048 | tf_op jit(solution)/shard_map/ppermute | solution.py:29
  32.9 2.7 %collective-permute-start.13 = (bf16[2,8,5,16,256]{4,3,2,1,0:T(8,128)(2,1)S(1)}, bf16[2,8,5,16,256]{4,3,2,1,0:T(8,128)(2,1)}, u32[]{:S(2)}, u32[]{:S(2)}) collective-permute-start(bf16[2,8,5,16,256]{4,3,2,1,0:T(8,128)(2,1)S(1)} %collective-permute-done.10.refs_10_), channel_id=1, source_target_pairs={{0,64},{8,56},{16,80},{24,8},{32,96},{40,24},{48,112},{56,40},{64,... | collective-permute-start | bytes 1966088 | tf_op jit(solution)/shard_map/ppermute | solution.py:29
  35.6 4.2 %collective-permute-start.18 = (bf16[1,8,5,16,256]{4,3,2,1,0:T(8,128)(2,1)}, bf16[1,8,5,16,256]{4,3,2,1,0:T(8,128)(2,1)}, u32[]{:S(2)}, u32[]{:S(2)}) collective-permute-start(bf16[1,8,5,16,256]{4,3,2,1,0:T(8,128)(2,1)} %collective-permute-done.16.refs_16_), channel_id=1, source_target_pairs={{0,192},{8,200},{16,208},{24,216},{32,224},{40,232},{48,240},{56,2... | collective-permute-start | bytes 983048 | tf_op jit(solution)/shard_map/ppermute | solution.py:29
  40.1 4.0 %collective-permute-start.17 = (bf16[1,8,5,16,256]{4,3,2,1,0:T(8,128)(2,1)}, bf16[1,8,5,16,256]{4,3,2,1,0:T(8,128)(2,1)}, u32[]{:S(2)}, u32[]{:S(2)}) collective-permute-start(bf16[1,8,5,16,256]{4,3,2,1,0:T(8,128)(2,1)} %collective-permute-done.15.refs_15_), channel_id=1, source_target_pairs={{0,64},{8,72},{16,80},{24,88},{32,96},{40,104},{48,112},{56,120},{... | collective-permute-start | bytes 983048 | tf_op jit(solution)/shard_map/ppermute | solution.py:29
  49.9 5.5 %collective-permute-done.7.refs_7_ = bf16[128,512]{1,0:T(8,128)(2,1)} collective-permute-done((bf16[128,512]{1,0:T(8,128)(2,1)}, bf16[128,512]{1,0:T(8,128)(2,1)}, u32[]{:S(2)}, u32[]{:S(2)}) %collective-permute-start.7) | collective-permute-done | bytes 131104 | tf_op jit(solution)/shard_map/ppermute | solution.py:53
  62.4 5.6 %forward.1 = (f32[256,2048]{1,0:T(8,128)S(1)}, bf16[256,2048]{1,0:T(8,128)(2,1)S(1)}, bf16[64,2048]{1,0:T(8,128)(2,1)S(1)}, bf16[64,2048]{1,0:T(8,128)(2,1)S(1)}...) custom-call(s32[45]{0:T(128)S(1)} %concatenate.6.meta, ...), custom_call_target="tpu_custom_call" | custom-call | flops 1342177280 | bytes 7340032 | tf_op jit(solution)/shard_map/forward/pallas_call | solution.py:63
  68.0 4.9 %collective-permute-start.19 = (bf16[256,2048]{1,0:T(8,128)(2,1)S(1)}, bf16[256,2048]{1,0:T(8,128)(2,1)S(1)}, u32[]{:S(2)}, u32[]{:S(2)}) collective-permute-start(bf16[256,2048]{1,0:T(8,128)(2,1)S(1)} %get-tuple-element.30.mine), channel_id=1, source_target_pairs={{0,8},{8,0},{16,24},{24,16},{32,40},{40,32},{48,56},{56,48},{64,72... | collective-permute-start | bytes 3145736 | tf_op jit(solution)/shard_map/ppermute | solution.py:41
  75.5 4.6 %collective-permute-done.20.up = bf16[64,2048]{1,0:T(8,128)(2,1)S(1)} collective-permute-done((bf16[64,2048]{1,0:T(8,128)(2,1)S(1)}, bf16[64,2048]{1,0:T(8,128)(2,1)S(1)}, u32[]{:S(2)}, u32[]{:S(2)}) %collective-permute-start.20) | collective-permute-done | bytes 262176 | tf_op jit(solution)/shard_map/ppermute | solution.py:49
  80.1 4.0 %collective-permute-done.21.down = bf16[64,2048]{1,0:T(8,128)(2,1)S(1)} collective-permute-done((bf16[64,2048]{1,0:T(8,128)(2,1)S(1)}, bf16[64,2048]{1,0:T(8,128)(2,1)S(1)}, u32[]{:S(2)}, u32[]{:S(2)}) %collective-permute-start.21) | collective-permute-done | bytes 262176 | tf_op jit(solution)/shard_map/ppermute | solution.py:49
  84.0 7.2 %backward.1 = (bf16[8,21,16,256]{3,2,1,0:T(8,128)(2,1)S(1)}, bf16[8,21,16,256]{3,2,1,0:T(8,128)(2,1)S(1)}, bf16[8,21,16,256]{3,2,1,0:T(8,128)(2,1)S(1)}, bf16[4,...) custom-call(s32[45]{0:T(128)S(1)} %concatenate.6.meta, ...), custom_call_target="tpu_custom_call" | custom-call | flops 1342177280 | bytes 6889472 | tf_op jit(solution)/shard_map/backward/pallas_call | solution.py:63
  92.9 3.4 %collective-permute-start.22 = (bf16[16,128,256]{2,1,0:T(8,128)(2,1)S(1)}, bf16[16,128,256]{2,1,0:T(8,128)(2,1)S(1)}, u32[]{:S(2)}, u32[]{:S(2)}) collective-permute-start(bf16[16,128,256]{2,1,0:T(8,128)(2,1)S(1)} %get-tuple-element.37), channel_id=1, source_target_pairs={{0,8},{8,0},{16,24},{24,16},{32,40},{40,32},{48,56},{56,48},{64,72... | collective-permute-start | bytes 3145736 | tf_op jit(solution)/shard_map/ppermute | solution.py:41
  98.9 4.8 %collective-permute-start.24 = (bf16[4,21,16,256]{3,2,1,0:T(8,128)(2,1)S(1)}, bf16[4,21,16,256]{3,2,1,0:T(8,128)(2,1)S(1)}, u32[]{:S(2)}, u32[]{:S(2)}) collective-permute-start(bf16[4,21,16,256]{3,2,1,0:T(8,128)(2,1)S(1)} %get-tuple-element.42), channel_id=1, source_target_pairs={{0,192},{8,56},{16,208},{24,8},{32,224},{40,24},{48,240},{56,40},{... | collective-permute-start | bytes 2064392 | tf_op jit(solution)/shard_map/ppermute | solution.py:29
  103.7 8.3 %collective-permute-done.23.ra = bf16[4,21,16,256]{3,2,1,0:T(8,128)(2,1)S(1)} collective-permute-done((bf16[4,21,16,256]{3,2,1,0:T(8,128)(2,1)S(1)}, bf16[4,21,16,256]{3,2,1,0:T(8,128)(2,1)S(1)}, u32[]{:S(2)}, u32[]{:S(2)}) %collective-permute-start.23) | collective-permute-done | bytes 688160 | tf_op jit(solution)/shard_map/ppermute | solution.py:29
  118.5 3.6 %all-to-all-start = ((bf16[16,128,256]{2,1,0:T(8,128)(2,1)}), bf16[16,128,256]{2,1,0:T(8,128)(2,1)S(1)}, u32[]{:S(2)}, u32[]{:S(2)}) async-start(bf16[16,128,256]{2,1,0:T(8,128)(2,1)} %broadcast_select_fusion), calls=%async_computation | async-start | bytes 2097152 | tf_op jit(solution)/shard_map/all_to_all | solution.py:412
  122.1 12.3 %collective-permute-done.25.prev = bf16[8,22,16,256]{3,2,1,0:T(8,128)(2,1)S(1)} collective-permute-done((bf16[8,22,16,256]{3,2,1,0:T(8,128)(2,1)}, bf16[8,22,16,256]{3,2,1,0:T(8,128)(2,1)S(1)}, u32[]{:S(2)}, u32[]{:S(2)}) %collective-permute-start.25) | collective-permute-done | bytes 1441824 | tf_op jit(solution)/shard_map/ppermute | solution.py:29
  137.7 2.7 %collective-permute-start.28 = (bf16[8,6,16,256]{3,2,1,0:T(8,128)(2,1)S(1)}, bf16[8,6,16,256]{3,2,1,0:T(8,128)(2,1)S(1)}, u32[]{:S(2)}, u32[]{:S(2)}) collective-permute-start(bf16[8,6,16,256]{3,2,1,0:T(8,128)(2,1)S(1)} %get-tuple-element.47), channel_id=1, source_target_pairs={{0,48},{8,200},{16,0},{24,216},{32,16},{40,232},{48,32},{56,248},{... | collective-permute-start | bytes 1179656 | tf_op jit(solution)/shard_map/ppermute | solution.py:29
  140.4 9.7 %collective-permute-done.27.prev = bf16[8,6,16,256]{3,2,1,0:T(8,128)(2,1)S(1)} collective-permute-done((bf16[8,6,16,256]{3,2,1,0:T(8,128)(2,1)S(1)}, bf16[8,6,16,256]{3,2,1,0:T(8,128)(2,1)S(1)}, u32[]{:S(2)}, u32[]{:S(2)}) %collective-permute-start.27) | collective-permute-done | bytes 393248 | tf_op jit(solution)/shard_map/ppermute | solution.py:29
  150.9 3.9 %collective-permute-start.30 = (bf16[8,7,8,256]{3,2,1,0:T(8,128)(2,1)S(1)}, bf16[8,7,8,256]{3,2,1,0:T(8,128)(2,1)S(1)}, u32[]{:S(2)}, u32[]{:S(2)}) collective-permute-start(bf16[8,7,8,256]{3,2,1,0:T(8,128)(2,1)S(1)} %get-tuple-element.50), channel_id=1, source_target_pairs={{0,8},{8,0},{16,24},{24,16},{32,40},{40,32},{48,56},{56,48},{64,72... | collective-permute-start | bytes 688136 | tf_op jit(solution)/shard_map/ppermute | solution.py:41
  (100 shorter events, 42.5 us)
Async XLA Ops:
  6.7 21.3 %collective-permute-start.12 = (bf16[2,8,5,16,256]{4,3,2,1,0:T(8,128)(2,1)S(1)}, bf16[2,8,5,16,256]{4,3,2,1,0:T(8,128)(2,1)S(1)}, u32[]{:S(2)}, u32[]{:S(2)}) collective-permute-start(bf16[2,8,5,16,256]{4,3,2,1,0:T(8,128)(2,1)S(1)} %pad_maximum_fusion.refs_9_), channel_id=1, source_target_pairs={{0,192},{8,56},{16,208},{24,8},{32,224},{40,24},{48,240},{56,40},{... | collective-permute-start | bytes 1966088 | tf_op jit(solution)/shard_map/ppermute | solution.py:29
  7.5 20.5 %collective-permute-start.11 = (bf16[2,8,5,16,256]{4,3,2,1,0:T(8,128)(2,1)S(1)}, bf16[2,8,5,16,256]{4,3,2,1,0:T(8,128)(2,1)S(1)}, u32[]{:S(2)}, u32[]{:S(2)}) collective-permute-start(bf16[2,8,5,16,256]{4,3,2,1,0:T(8,128)(2,1)S(1)} %pad_maximum_fusion.refs_9_), channel_id=1, source_target_pairs={{0,48},{8,24},{16,0},{24,40},{32,16},{40,56},{48,32},{56,8},{64,11... | collective-permute-start | bytes 1966088 | tf_op jit(solution)/shard_map/ppermute | solution.py:29
  8.2 19.8 %collective-permute-start.10 = (bf16[2,8,5,16,256]{4,3,2,1,0:T(8,128)(2,1)S(1)}, bf16[2,8,5,16,256]{4,3,2,1,0:T(8,128)(2,1)S(1)}, u32[]{:S(2)}, u32[]{:S(2)}) collective-permute-start(bf16[2,8,5,16,256]{4,3,2,1,0:T(8,128)(2,1)S(1)} %pad_maximum_fusion.refs_9_), channel_id=1, source_target_pairs={{0,16},{8,72},{16,32},{24,88},{32,48},{40,104},{48,0},{56,120},{64... | collective-permute-start | bytes 1966088 | tf_op jit(solution)/shard_map/ppermute | solution.py:29
  8.9 9.0 %collective-permute-start.4 = (bf16[256,512]{1,0:T(8,128)(2,1)S(1)}, bf16[256,512]{1,0:T(8,128)(2,1)S(1)}, u32[]{:S(2)}, u32[]{:S(2)}) collective-permute-start(bf16[256,512]{1,0:T(8,128)(2,1)S(1)} %pad_maximum_fusion.1.refs_0_), channel_id=1, source_target_pairs={{0,7},{1,0},{2,1},{3,2},{4,3},{5,4},{6,5},{7,6},{8,15},{9,8},{10,9... | collective-permute-start | bytes 786440 | tf_op jit(solution)/shard_map/ppermute | solution.py:53
  14.5 7.4 %collective-permute-start.1 = (bf16[256,512]{1,0:T(8,128)(2,1)S(1)}, bf16[256,512]{1,0:T(8,128)(2,1)S(1)}, u32[]{:S(2)}, u32[]{:S(2)}) collective-permute-start(bf16[256,512]{1,0:T(8,128)(2,1)S(1)} %pad_maximum_fusion.1.refs_0_), channel_id=1, source_target_pairs={{0,1},{1,2},{2,3},{3,4},{4,5},{5,6},{6,7},{7,0},{8,9},{9,10},{10,1... | collective-permute-start | bytes 786440 | tf_op jit(solution)/shard_map/ppermute | solution.py:53
  22.0 10.9 %collective-permute-start.2 = (bf16[256,512]{1,0:T(8,128)(2,1)S(1)}, bf16[256,512]{1,0:T(8,128)(2,1)S(1)}, u32[]{:S(2)}, u32[]{:S(2)}) collective-permute-start(bf16[256,512]{1,0:T(8,128)(2,1)S(1)} %collective-permute-done.1.refs_1_), channel_id=1, source_target_pairs={{0,1},{1,2},{2,3},{3,4},{4,5},{5,6},{6,7},{7,0},{8,9},{9,10},{10,1... | collective-permute-start | bytes 786440 | tf_op jit(solution)/shard_map/ppermute | solution.py:53
  24.6 11.0 %collective-permute-start.6 = (bf16[256,512]{1,0:T(8,128)(2,1)S(1)}, bf16[256,512]{1,0:T(8,128)(2,1)S(1)}, u32[]{:S(2)}, u32[]{:S(2)}) collective-permute-start(bf16[256,512]{1,0:T(8,128)(2,1)S(1)} %collective-permute-done.5.refs_5_), channel_id=1, source_target_pairs={{0,7},{1,0},{2,1},{3,2},{4,3},{5,4},{6,5},{7,6},{8,15},{9,8},{10,9... | collective-permute-start | bytes 786440 | tf_op jit(solution)/shard_map/ppermute | solution.py:53
  28.1 7.5 %collective-permute-start.16 = (bf16[1,8,5,16,256]{4,3,2,1,0:T(8,128)(2,1)S(1)}, bf16[1,8,5,16,256]{4,3,2,1,0:T(8,128)(2,1)}, u32[]{:S(2)}, u32[]{:S(2)}) collective-permute-start(bf16[1,8,5,16,256]{4,3,2,1,0:T(8,128)(2,1)S(1)} %get-tuple-element.56), channel_id=1, source_target_pairs={{0,48},{8,56},{16,0},{24,8},{32,16},{40,24},{48,32},{56,40},{64,11... | collective-permute-start | bytes 983048 | tf_op jit(solution)/shard_map/ppermute | solution.py:29
  30.8 24.5 %collective-permute-start.14 = (bf16[2,8,5,16,256]{4,3,2,1,0:T(8,128)(2,1)S(1)}, bf16[2,8,5,16,256]{4,3,2,1,0:T(8,128)(2,1)S(1)}, u32[]{:S(2)}, u32[]{:S(2)}) collective-permute-start(bf16[2,8,5,16,256]{4,3,2,1,0:T(8,128)(2,1)S(1)} %collective-permute-done.11.refs_11_), channel_id=1, source_target_pairs={{0,192},{8,200},{16,208},{24,216},{32,224},{40,232},{48,240},{56,2... | collective-permute-start | bytes 1966088 | tf_op jit(solution)/shard_map/ppermute | solution.py:29
  32.9 22.9 %collective-permute-start.13 = (bf16[2,8,5,16,256]{4,3,2,1,0:T(8,128)(2,1)S(1)}, bf16[2,8,5,16,256]{4,3,2,1,0:T(8,128)(2,1)}, u32[]{:S(2)}, u32[]{:S(2)}) collective-permute-start(bf16[2,8,5,16,256]{4,3,2,1,0:T(8,128)(2,1)S(1)} %collective-permute-done.10.refs_10_), channel_id=1, source_target_pairs={{0,64},{8,56},{16,80},{24,8},{32,96},{40,24},{48,112},{56,40},{64,... | collective-permute-start | bytes 1966088 | tf_op jit(solution)/shard_map/ppermute | solution.py:29
  35.6 9.3 %collective-permute-start.3 = (bf16[256,512]{1,0:T(8,128)(2,1)S(1)}, bf16[256,512]{1,0:T(8,128)(2,1)S(1)}, u32[]{:S(2)}, u32[]{:S(2)}) collective-permute-start(bf16[256,512]{1,0:T(8,128)(2,1)S(1)} %collective-permute-done.2.refs_2_), channel_id=1, source_target_pairs={{0,1},{1,2},{2,3},{3,4},{4,5},{5,6},{6,7},{7,0},{8,9},{9,10},{10,1... | collective-permute-start | bytes 786440 | tf_op jit(solution)/shard_map/ppermute | solution.py:53
  35.6 20.2 %collective-permute-start.18 = (bf16[1,8,5,16,256]{4,3,2,1,0:T(8,128)(2,1)}, bf16[1,8,5,16,256]{4,3,2,1,0:T(8,128)(2,1)}, u32[]{:S(2)}, u32[]{:S(2)}) collective-permute-start(bf16[1,8,5,16,256]{4,3,2,1,0:T(8,128)(2,1)} %collective-permute-done.16.refs_16_), channel_id=1, source_target_pairs={{0,192},{8,200},{16,208},{24,216},{32,224},{40,232},{48,240},{56,2... | collective-permute-start | bytes 983048 | tf_op jit(solution)/shard_map/ppermute | solution.py:29
  40.1 15.6 %collective-permute-start.17 = (bf16[1,8,5,16,256]{4,3,2,1,0:T(8,128)(2,1)}, bf16[1,8,5,16,256]{4,3,2,1,0:T(8,128)(2,1)}, u32[]{:S(2)}, u32[]{:S(2)}) collective-permute-start(bf16[1,8,5,16,256]{4,3,2,1,0:T(8,128)(2,1)} %collective-permute-done.15.refs_15_), channel_id=1, source_target_pairs={{0,64},{8,72},{16,80},{24,88},{32,96},{40,104},{48,112},{56,120},{... | collective-permute-start | bytes 983048 | tf_op jit(solution)/shard_map/ppermute | solution.py:29
  68.0 16.0 %collective-permute-start.19 = (bf16[256,2048]{1,0:T(8,128)(2,1)S(1)}, bf16[256,2048]{1,0:T(8,128)(2,1)S(1)}, u32[]{:S(2)}, u32[]{:S(2)}) collective-permute-start(bf16[256,2048]{1,0:T(8,128)(2,1)S(1)} %get-tuple-element.30.mine), channel_id=1, source_target_pairs={{0,8},{8,0},{16,24},{24,16},{32,40},{40,32},{48,56},{56,48},{64,72... | collective-permute-start | bytes 3145736 | tf_op jit(solution)/shard_map/ppermute | solution.py:41
  74.2 9.8 %collective-permute-start.21 = (bf16[64,2048]{1,0:T(8,128)(2,1)S(1)}, bf16[64,2048]{1,0:T(8,128)(2,1)S(1)}, u32[]{:S(2)}, u32[]{:S(2)}) collective-permute-start(bf16[64,2048]{1,0:T(8,128)(2,1)S(1)} %get-tuple-element.32), channel_id=1, source_target_pairs={{16,8},{24,0},{32,24},{40,16},{48,40},{56,32},{64,56},{72,48},{80,... | collective-permute-start | bytes 786440 | tf_op jit(solution)/shard_map/ppermute | solution.py:49
  92.9 24.5 %collective-permute-start.22 = (bf16[16,128,256]{2,1,0:T(8,128)(2,1)S(1)}, bf16[16,128,256]{2,1,0:T(8,128)(2,1)S(1)}, u32[]{:S(2)}, u32[]{:S(2)}) collective-permute-start(bf16[16,128,256]{2,1,0:T(8,128)(2,1)S(1)} %get-tuple-element.37), channel_id=1, source_target_pairs={{0,8},{8,0},{16,24},{24,16},{32,40},{40,32},{48,56},{56,48},{64,72... | collective-permute-start | bytes 3145736 | tf_op jit(solution)/shard_map/ppermute | solution.py:41
  96.3 15.7 %collective-permute-start.23 = (bf16[4,21,16,256]{3,2,1,0:T(8,128)(2,1)S(1)}, bf16[4,21,16,256]{3,2,1,0:T(8,128)(2,1)S(1)}, u32[]{:S(2)}, u32[]{:S(2)}) collective-permute-start(bf16[4,21,16,256]{3,2,1,0:T(8,128)(2,1)S(1)} %get-tuple-element.41), channel_id=1, source_target_pairs={{0,64},{8,24},{16,80},{24,40},{32,96},{40,56},{48,112},{56,8},{64,... | collective-permute-start | bytes 2064392 | tf_op jit(solution)/shard_map/ppermute | solution.py:29
  98.9 13.1 %collective-permute-start.24 = (bf16[4,21,16,256]{3,2,1,0:T(8,128)(2,1)S(1)}, bf16[4,21,16,256]{3,2,1,0:T(8,128)(2,1)S(1)}, u32[]{:S(2)}, u32[]{:S(2)}) collective-permute-start(bf16[4,21,16,256]{3,2,1,0:T(8,128)(2,1)S(1)} %get-tuple-element.42), channel_id=1, source_target_pairs={{0,192},{8,56},{16,208},{24,8},{32,224},{40,24},{48,240},{56,40},{... | collective-permute-start | bytes 2064392 | tf_op jit(solution)/shard_map/ppermute | solution.py:29
  114.4 19.9 %collective-permute-start.25 = (bf16[8,22,16,256]{3,2,1,0:T(8,128)(2,1)}, bf16[8,22,16,256]{3,2,1,0:T(8,128)(2,1)S(1)}, u32[]{:S(2)}, u32[]{:S(2)}) collective-permute-start(bf16[8,22,16,256]{3,2,1,0:T(8,128)(2,1)} %get-tuple-element.43), channel_id=1, source_target_pairs={{0,64},{8,24},{16,80},{24,40},{32,96},{40,56},{48,112},{56,8},{64,... | collective-permute-start | bytes 4325384 | tf_op jit(solution)/shard_map/ppermute | solution.py:29
  115.3 19.0 %collective-permute-start.26 = (bf16[8,22,16,256]{3,2,1,0:T(8,128)(2,1)}, bf16[8,22,16,256]{3,2,1,0:T(8,128)(2,1)}, u32[]{:S(2)}, u32[]{:S(2)}) collective-permute-start(bf16[8,22,16,256]{3,2,1,0:T(8,128)(2,1)} %get-tuple-element.44), channel_id=1, source_target_pairs={{0,192},{8,56},{16,208},{24,8},{32,224},{40,24},{48,240},{56,40},{... | collective-permute-start | bytes 4325384 | tf_op jit(solution)/shard_map/ppermute | solution.py:29
  118.5 39.0 %all-to-all-start = ((bf16[16,128,256]{2,1,0:T(8,128)(2,1)}), bf16[16,128,256]{2,1,0:T(8,128)(2,1)S(1)}, u32[]{:S(2)}, u32[]{:S(2)}) async-start(bf16[16,128,256]{2,1,0:T(8,128)(2,1)} %broadcast_select_fusion), calls=%async_computation | async-start | bytes 2097152 | tf_op jit(solution)/shard_map/all_to_all | solution.py:412
  137.6 12.4 %collective-permute-start.27 = (bf16[8,6,16,256]{3,2,1,0:T(8,128)(2,1)S(1)}, bf16[8,6,16,256]{3,2,1,0:T(8,128)(2,1)S(1)}, u32[]{:S(2)}, u32[]{:S(2)}) collective-permute-start(bf16[8,6,16,256]{3,2,1,0:T(8,128)(2,1)S(1)} %get-tuple-element.46), channel_id=1, source_target_pairs={{0,16},{8,72},{16,32},{24,88},{32,48},{40,104},{48,0},{56,120},{64... | collective-permute-start | bytes 1179656 | tf_op jit(solution)/shard_map/ppermute | solution.py:29
  137.7 12.3 %collective-permute-start.28 = (bf16[8,6,16,256]{3,2,1,0:T(8,128)(2,1)S(1)}, bf16[8,6,16,256]{3,2,1,0:T(8,128)(2,1)S(1)}, u32[]{:S(2)}, u32[]{:S(2)}) collective-permute-start(bf16[8,6,16,256]{3,2,1,0:T(8,128)(2,1)S(1)} %get-tuple-element.47), channel_id=1, source_target_pairs={{0,48},{8,200},{16,0},{24,216},{32,16},{40,232},{48,32},{56,248},{... | collective-permute-start | bytes 1179656 | tf_op jit(solution)/shard_map/ppermute | solution.py:29
  140.4 9.7 %collective-permute-start.29 = (bf16[8,6,16,256]{3,2,1,0:T(8,128)(2,1)S(1)}, bf16[8,6,16,256]{3,2,1,0:T(8,128)(2,1)S(1)}, u32[]{:S(2)}, u32[]{:S(2)}) collective-permute-start(bf16[8,6,16,256]{3,2,1,0:T(8,128)(2,1)S(1)} %get-tuple-element.48), channel_id=1, source_target_pairs={{0,32},{8,136},{16,48},{24,152},{32,0},{40,168},{48,16},{56,184},{... | collective-permute-start | bytes 1179656 | tf_op jit(solution)/shard_map/ppermute | solution.py:29
  (28 other events, 193.7 us)
where the time goes:
time: 159 us
  starting transfers between devices  65.4 us (41%)
  waiting for transfers between devices  54.8 us (34%)
  Pallas kernels  21.5 us (14%)
  local copies, waits for them, and re-layouts  12.7 us (8%)
  other arithmetic  3.61 us (2%)
    ppermute x16, waiting for transfers between devices, by_core(): return lax.ppermute(value, ('crop', 'rows'), pairs)  31.1 us
    ppermute x16, starting transfers between devices, by_core(): return lax.ppermute(value, ('crop', 'rows'), pairs)  30.8 us
    pallas_call x8, Pallas kernels, local(): pl.pallas_call(kernel, out_shape=shapes, in_specs=[SMEM] + [ANY if i in h...  21.5 us
    ppermute x5, starting transfers between devices, to_partner(): return lax.ppermute(value, 'rows', [(r, r ^ 1) for r in range(16)])  15.6 us
    ppermute x8, waiting for transfers between devices, along_z(): return lax.ppermute(value, 'hid', [(z, (z + step) % NZ) for z in range(NZ)])  14 us
    ppermute x8, starting transfers between devices, along_z(): return lax.ppermute(value, 'hid', [(z, (z + step) % NZ) for z in range(NZ)])  12.8 us
    unnamed x40, local copies, waits for them, and re-layouts  11.8 us
    ppermute x2, waiting for transfers between devices, to_next_chip(): return lax.ppermute(value, 'rows', pairs)  8.54 us
  transfers between devices with their start and end apart: 32, of which 13 were waited for; matrix products, arithmetic and copies ran while one was open for 2% of the time, Pallas kernels for 4%

commit v1 on v0

--- a/solution.py
+++ b/solution.py
@@ -12,9 +12,9 @@
 F32, BF16 = jnp.float32, jnp.bfloat16
 NX, NY, NZ = 4, 4, 8
 COLS, NNZ, BS, PW = 8, 5, 256, 64
-TOK, KERN = 256, 20
+TOK, KERN, SPLIT = 256, 20, 4
 CORE, XPOS, YPOS, YLO, ZPOS = 40, 41, 42, 43, 44
-ANY = pl.BlockSpec(memory_space=pl.ANY)
+HBM = pl.BlockSpec(memory_space=pltpu.MemorySpace.HBM)
 VMEM = pl.BlockSpec(memory_space=pltpu.VMEM)
 SMEM = pl.BlockSpec(memory_space=pltpu.SMEM)
 
@@ -63,10 +63,10 @@
     return pl.pallas_call(
         kernel,
         out_shape=shapes,
-        in_specs=[SMEM] + [ANY if i in hbm else VMEM for i in range(1, len(args))],
+        in_specs=[SMEM] + [HBM if i in hbm else VMEM for i in range(1, len(args))],
         out_specs=[VMEM] * len(outs),
         scratch_shapes=list(scratch),
-        compiler_params=pltpu.CompilerParams(vmem_limit_bytes=28 * 2**20),
+        compiler_params=pltpu.CompilerParams(vmem_limit_bytes=14 * 2**20),
         cost_estimate=pl.CostEstimate(flops=flops, transcendentals=0, bytes_accessed=size),
         name=name,
     )(*args)
@@ -90,22 +90,36 @@
 
 def weight_plan(meta, pieces):
     core, x, ylo = meta[CORE], meta[XPOS], meta[YLO]
-    own, r1, r2, r3, r4, r5, r6, r7, r8, r9 = pieces
+    own, a, b, c, d, e, f, g, h, i = pieces
     here, there = ylo * NX, (1 - ylo) * NX
-    at = lambda base, d: base + (x + d) % NX
-    pick = lambda a, b: jnp.where(core == 0, a, b)
+    side = jnp.where(core == 0, NX - 1, 1)
+    at = lambda base, step: base + (x + step) % NX
     slots = [
         (own, at(here, 0)),
-        (r1, pick(at(here, 3), at(there, 0))),
-        (r2, pick(at(here, 1), at(here, 3))),
-        (r3, pick(at(there, 0), at(here, 1))),
-        (r4, pick(at(there, 3), at(there, 1))),
-        (r5, pick(at(there, 1), at(there, 3))),
+        (a, at(here, side)),
+        (b, at(there, 0)),
+        (c, at(here, NX - side)),
+        (d, at(there, side)),
+        (e, at(there, NX - side)),
     ]
     plan = [(src, s, 2 * j + s) for src, j in slots for s in range(2)]
-    for j, a, b in ((at(here, 2), r6, r7), (at(there, 2), r8, r9)):
-        plan += [(a, 0, 2 * j), (b, 0, 2 * j + 1)]
+    for j, low, high in ((at(here, 2), f, g), (at(there, 2), h, i)):
+        plan += [(low, 0, 2 * j), (high, 0, 2 * j + 1)]
     return plan
+
+
+def hold(meta, value, *others):
+    def kernel(meta, src, *refs):
+        refs[-1][...] = src[...]
+
+    outs = [(value.shape, value.dtype)]
+    return local(kernel, "hold", outs, (meta, value, *others))[0]
+
+
+def cut_kernel(meta, a, c, *refs):
+    low, high = refs[-2:]
+    low[...] = a[:1]
+    high[...] = c[1:]
 
 
 def forward_kernel(meta, *refs):
@@ -176,7 +190,7 @@
 
 
 def backward_kernel(meta, tok, got, mine, up, down, pre, taps, *refs):
-    g0, g1, g3, g2a, g2b, pgrad, conv, lhs, res, slab, moved = refs
+    g0, m1, m3, g1, g3, pgrad, conv, lhs, res, slab, moved = refs
     core, x, y = meta[CORE], meta[XPOS], meta[YPOS]
     is_in = core == 0
     slab[...] = jnp.zeros_like(slab)
@@ -235,20 +249,22 @@
             out[at, KERN] = slab[...]
 
         emit(g0, 0, c)
-        emit(g1, 1, c)
-        emit(g3, 3, c)
-
-        @pl.when(c < COLS // 2)
+
+        @pl.when(c < SPLIT)
         def _():
-            emit(g2a, 2, c)
-
-        @pl.when(c >= COLS // 2)
+            emit(m1, 2, c)
+            emit(g1, 1, c)
+            emit(m3, 3, c + SPLIT)
+
+        @pl.when(c >= SPLIT)
         def _():
-            emit(g2b, 2, c - COLS // 2)
+            emit(m3, 2, c - SPLIT)
+            emit(m1, 1, c)
+            emit(g3, 3, c - SPLIT)
 
 
 def backward(meta, tok, got, mine, up, down, pre, taps):
-    full, part = (COLS, KERN + 1, 16, BS), (COLS // 2, KERN + 1, 16, BS)
+    full, part = (COLS, KERN + 1, 16, BS), (SPLIT, KERN + 1, 16, BS)
     outs = [(full, BF16)] * 3 + [(part, BF16)] * 2 + [((TOK, COLS * BS), BF16)]
     scratch = [
         pltpu.VMEM((TOK, BS), F32),
@@ -299,41 +315,33 @@
         out[:, b * BS : (b + 1) * BS] = total.astype(BF16)
 
 
-def relay_kernel(meta, g1, g3, ra, rb, o1, o3):
-    for out, own, got, first_half in ((o1, g1, ra, 0), (o3, g3, rb, COLS // 2)):
-
-        @pl.loop(0, COLS // 2)
+def relay_kernel(meta, g1, g3, m1, m3, _, o1, o3):
+    for out, own, got in ((o1, g1, m1), (o3, g3, m3)):
+
+        @pl.loop(0, SPLIT)
         def _(c):
-            at, other = c + first_half, c + COLS // 2 - first_half
             for k in range(KERN):
-                out[at, k] = (own[at, k].astype(F32) + got[c, k].astype(F32)).astype(BF16)
-                out[other, k] = own[other, k]
-            out[at, KERN] = own[at, KERN]
-            out[other, KERN] = own[other, KERN]
-            out[at, KERN + 1] = got[c, KERN]
-            out[other, KERN + 1] = own[other, KERN]
-
-
-def relay(meta, g1, g3, ra, rb):
-    shape = ((COLS, KERN + 2, 16, BS), BF16)
-    return local(relay_kernel, "relay", [shape] * 2, (meta, g1, g3, ra, rb))
-
-
-def first_sum_kernel(meta, own, prev, nxt, *outs):
+                out[c, k] = (own[c, k].astype(F32) + got[c, k].astype(F32)).astype(BF16)
+            out[c, KERN] = own[c, KERN]
+            out[c, KERN + 1] = got[c, KERN]
+
+
+def first_sum_kernel(meta, own, m1, m3, p1, p3, *outs):
     here = jnp.where(meta[CORE] == 0, meta[XPOS], meta[YPOS])
 
-    @pl.loop(0, COLS)
-    def _(c):
-        far = jnp.where(c < COLS // 2, prev[c, KERN + 1], nxt[c, KERN + 1]).astype(F32)
-        near = prev[c, KERN].astype(F32) + nxt[c, KERN].astype(F32)
-        slab = ((own[c, KERN].astype(F32) + far) + near).astype(BF16)
-        for d in range(4):
-            s = (here + d) % 4
-            for k in range(NNZ):
-                at = k * 4 + s
-                total = own[c, at].astype(F32) + prev[c, at].astype(F32) + nxt[c, at].astype(F32)
-                outs[d][c, k] = total.astype(BF16)
-            outs[d][c, NNZ] = slab
+    for shift, relayed, direct in ((0, p1, m3), (SPLIT, p3, m1)):
+
+        @pl.loop(0, SPLIT)
+        def _(c):
+            at, got = c + shift, c + SPLIT
+            near = relayed[c, KERN].astype(F32) + direct[got, KERN].astype(F32)
+            far = own[at, KERN].astype(F32) + relayed[c, KERN + 1].astype(F32)
+            for d in range(4):
+                s = (here + d) % 4
+                for k in range(NNZ):
+                    total = own[at, k * 4 + s].astype(F32) + relayed[c, k * 4 + s].astype(F32)
+                    outs[d][at, k] = (total + direct[got, k * 4 + s].astype(F32)).astype(BF16)
+                outs[d][at, NNZ] = (far + near).astype(BF16)
 
 
 def second_sum_kernel(meta, own, prev, nxt, far, keep, send):
@@ -354,7 +362,7 @@
                     out[c, NNZ + 1] = high
 
 
-def place_kernel(meta, keep, got, win, wout, kern):
+def place_kernel(meta, keep, got, _, win, wout, kern):
     is_in = meta[CORE] == 0
 
     @pl.loop(0, NNZ)
@@ -385,39 +393,42 @@
     own = jnp.stack(side(*(w.transpose(1, 2, 0, 3) for w in (weight_in, weight_out))))
     t0 = jnp.concatenate(side(tokens.reshape(128, 512), cotangent.reshape(128, 512)))
 
-    r1 = by_core(own, (0, 1), (1, 0))
-    r2 = by_core(own, (0, -1), (0, 1))
-    r3 = by_core(own, (-1, 0), (0, -1))
+    wa = by_core(own, (0, 1), (0, -1))
+    wb = by_core(own, (-1, 0), (1, 0))
     zr1, zl1 = along_z(t0, 1), along_z(t0, -1)
-    r4 = by_core(r1, (1, 0), (0, -1))
-    r5 = by_core(r2, (-1, 0), (-1, 0))
+    wc = by_core(hold(meta, own, wa, wb, zr1, zl1), (0, -1), (0, 1))
+    wd = by_core(wa, (1, 0), (-1, 0))
     zr2, zl2 = along_z(zr1, 1), along_z(zl1, -1)
-    r6 = by_core(jnp.where(is_in, r1[:1], r2[:1]), (0, 1), (0, 1))
-    r7 = by_core(jnp.where(is_in, r2[1:], r3[1:]), (0, -1), (0, -1))
+    cuts = [((1, *own.shape[1:]), BF16)] * 2
+    low, high = local(cut_kernel, "cut", cuts, (meta, wa, wc, wd, zr2, zl2))
+    wf = by_core(low, (0, 1), (0, -1))
+    wg = by_core(high, (0, -1), (0, 1))
+    we = by_core(wc, (-1, 0), (1, 0))
     zr3, zl3 = along_z(zr2, 1), along_z(zl2, -1)
-    r8 = by_core(r6, (1, 0), (1, 0))
-    r9 = by_core(r7, (-1, 0), (-1, 0))
+    wh = by_core(wf, (1, 0), (-1, 0))
+    wi = by_core(wg, (-1, 0), (1, 0))
     zr4, zl4 = along_z(zr3[:128], 1), along_z(zl3[128:], -1)
-    pieces = (own, r1, r2, r3, r4, r5, r6, r7, r8, r9)
+    pieces = (own, wa, wb, wc, wd, we, wf, wg, wh, wi)
     token_pieces = (t0, zr1, zr2, zr3, zl1, zl2, zl3, zr4, zl4)
 
     pre, out, top, bot, wts, tok = forward(meta, token_pieces, pieces)
     got = to_partner(out)
     up, down = to_next_chip(bot, 1), to_next_chip(top, -1)
-    g0, g1, g3, g2a, g2b, pgrad = backward(meta, tok, got, out, up, down, pre, mix_kernel)
-    ra, rb = first(g2a, 1), first(g2b, -1)
+    g0, m1, m3, g1, g3, pgrad = backward(meta, tok, got, out, up, down, pre, mix_kernel)
+    m1, m3 = first(m1, 1), first(m3, -1)
 
     keep, send = token_grad(meta, pgrad, wts)
     terms = jnp.where(is_in, keep, to_partner(send))
+    relayed = [((SPLIT, KERN + 2, 16, BS), BF16)] * 2
+    r1, r3 = local(relay_kernel, "relay", relayed, (meta, g1, g3, m1, m3, terms), hbm=(5,))
     terms = lax.all_to_all(terms, "hid", 0, 0, tiled=True)
     (grad_tokens,) = local(gather_sum_kernel, "gathersum", [((128, 512), BF16)], (meta, terms))
 
-    g1, g3 = relay(meta, g1, g3, ra, rb)
     h = local(
         first_sum_kernel,
         "firstsum",
         [((COLS, NNZ + 1, 16, BS), BF16)] * 4,
-        (meta, g0, first(g1, 1), first(g3, -1)),
+        (meta, g0, m1, m3, first(r1, 1), first(r3, -1)),
     )
     last = (h[0], second(h[1], 1), second(h[3], -1), second(h[2], 2))
     shape = ((COLS, NNZ + 2, 8, BS), BF16)
@@ -427,7 +438,7 @@
         place_kernel,
         "place",
         [out_shape, out_shape, ((9, 8 * BS), F32)],
-        (meta, kept, to_partner(sent)),
+        (meta, kept, to_partner(sent), grad_tokens),
     )
     grad_tokens = grad_tokens.reshape(1, 2, PW, 512)
     return grad_tokens, win.transpose(0, 2, 1, 3), wout.transpose(0, 2, 1, 3), kern

time: 159 us -> 148 us (0.931)
  starting transfers between devices: 65.4 us -> 54.6 us
  waiting for transfers between devices: 54.8 us -> 64.4 us
  local copies, waits for them, and re-layouts: 12.7 us -> 3.63 us
    unnamed x40 -> x18, local copies, waits for them, and re-layouts: 11.8 us -> 3.44 us
    ppermute x16, waiting for transfers between devices: 31.1 us -> 38.5 us  [by_core(): return lax.ppermute(value, ('crop', 'rows'), pairs)]
    ppermute x16, starting transfers between devices: 30.8 us -> 24.7 us  [by_core(): return lax.ppermute(value, ('crop', 'rows'), pairs)]
    ppermute x8, waiting for transfers between devices: 14 us -> 17.1 us  [along_z(): return lax.ppermute(value, 'hid', [(z, (z + step) % NZ) for z in range(NZ)])]
    ppermute x5, starting transfers between devices: 15.6 us -> 12.8 us  [to_partner(): return lax.ppermute(value, 'rows', [(r, r ^ 1) for r in range(16)])]
    ppermute x8, starting transfers between devices: 12.8 us -> 10.2 us  [along_z(): return lax.ppermute(value, 'hid', [(z, (z + step) % NZ) for z in range(NZ)])]
    pallas_call x8 -> x10, Pallas kernels: 21.5 us -> 21.1 us  [local(): pl.pallas_call(kernel, out_shape=shapes, in_specs=[SMEM] + [HBM if i in h...]
  transfers between devices with their start and end apart: 32 -> 32, of which waited for: 13 -> 16; matrix products, arithmetic and copies ran while one was open for 2% -> 2% of each run, Pallas kernels for 4% -> 3%
where the time goes in v1:
time: 148 us
  waiting for transfers between devices  64.4 us (44%)
  starting transfers between devices  54.6 us (37%)
  Pallas kernels  21.1 us (14%)
  local copies, waits for them, and re-layouts  3.63 us (2%)
  other arithmetic  3.54 us (2%)
    ppermute x16, waiting for transfers between devices, by_core(): return lax.ppermute(value, ('crop', 'rows'), pairs)  38.5 us
    ppermute x16, starting transfers between devices, by_core(): return lax.ppermute(value, ('crop', 'rows'), pairs)  24.7 us
    pallas_call x10, Pallas kernels, local(): pl.pallas_call(kernel, out_shape=shapes, in_specs=[SMEM] + [HBM if i in h...  21.1 us
    ppermute x8, waiting for transfers between devices, along_z(): return lax.ppermute(value, 'hid', [(z, (z + step) % NZ) for z in range(NZ)])  17.1 us
    ppermute x5, starting transfers between devices, to_partner(): return lax.ppermute(value, 'rows', [(r, r ^ 1) for r in range(16)])  12.8 us
    ppermute x8, starting transfers between devices, along_z(): return lax.ppermute(value, 'hid', [(z, (z + step) % NZ) for z in range(NZ)])  10.2 us
    ppermute x2, waiting for transfers between devices, to_next_chip(): return lax.ppermute(value, 'rows', pairs)  8.54 us
    all_to_all x1, starting transfers between devices, on_device(): terms = lax.all_to_all(terms, 'hid', 0, 0, tiled=True)  4.24 us
  transfers between devices with their start and end apart: 32, of which 16 were waited for; matrix products, arithmetic and copies ran while one was open for 2% of the time, Pallas kernels for 3%

profile of v1, /device:TPU:1, one launch (start us, length us, event | category | flops | bytes accessed | tf_op | source)
XLA Modules:
  0.0 148.1 jit_solution(10972512866539439569)
XLA Ops:
  1.9 3.3 %collective-permute-start.9 = (bf16[8,5,16,256]{3,2,1,0:T(8,128)(2,1)S(1)}, bf16[8,5,16,256]{3,2,1,0:T(8,128)(2,1)S(1)}, u32[]{:S(2)}, u32[]{:S(2)}) collective-permute-start(bf16[8,5,16,256]{3,2,1,0:T(8,128)(2,1)S(1)} %select_bitcast_fusion), channel_id=1, source_target_pairs={{0,8},{8,0},{16,24},{24,16},{32,40},{40,32},{48,56},{56,48},{64,72... | collective-permute-start | bytes 983048 | tf_op jit(solution)/shard_map/ppermute | solution.py:41
  8.9 5.7 %collective-permute-start.4 = (bf16[256,512]{1,0:T(8,128)(2,1)S(1)}, bf16[256,512]{1,0:T(8,128)(2,1)S(1)}, u32[]{:S(2)}, u32[]{:S(2)}) collective-permute-start(bf16[256,512]{1,0:T(8,128)(2,1)S(1)} %pad_maximum_fusion.1.refs_0_), channel_id=1, source_target_pairs={{0,7},{1,0},{2,1},{3,2},{4,3},{5,4},{6,5},{7,6},{8,15},{9,8},{10,9... | collective-permute-start | bytes 786440 | tf_op jit(solution)/shard_map/ppermute | solution.py:53
  14.7 4.3 %collective-permute-done.4.refs_3_.refs_4_ = bf16[256,512]{1,0:T(8,128)(2,1)S(1)} collective-permute-done((bf16[256,512]{1,0:T(8,128)(2,1)S(1)}, bf16[256,512]{1,0:T(8,128)(2,1)S(1)}, u32[]{:S(2)}, u32[]{:S(2)}) %collective-permute-start.4) | collective-permute-done | bytes 262176 | tf_op jit(solution)/shard_map/ppermute | solution.py:53
  19.0 3.1 %collective-permute-done.1.refs_2_.refs_1_ = bf16[256,512]{1,0:T(8,128)(2,1)S(1)} collective-permute-done((bf16[256,512]{1,0:T(8,128)(2,1)S(1)}, bf16[256,512]{1,0:T(8,128)(2,1)S(1)}, u32[]{:S(2)}, u32[]{:S(2)}) %collective-permute-start.1) | collective-permute-done | bytes 262176 | tf_op jit(solution)/shard_map/ppermute | solution.py:53
  22.9 2.8 %collective-permute-start.13 = (bf16[2,8,5,16,256]{4,3,2,1,0:T(8,128)(2,1)S(1)}, bf16[2,8,5,16,256]{4,3,2,1,0:T(8,128)(2,1)S(1)}, u32[]{:S(2)}, u32[]{:S(2)}) collective-permute-start(bf16[2,8,5,16,256]{4,3,2,1,0:T(8,128)(2,1)S(1)} %collective-permute-done.10.refs_0_.a.refs_10_), channel_id=1, source_target_pairs={{0,64},{8,200},{16,80},{24,216},{32,96},{40,232},{48,112},{56,248}... | collective-permute-start | bytes 1966088 | tf_op jit(solution)/shard_map/ppermute | solution.py:29
  27.1 4.4 %collective-permute-done.5.refs_2_.refs_5_ = bf16[256,512]{1,0:T(8,128)(2,1)S(1)} collective-permute-done((bf16[256,512]{1,0:T(8,128)(2,1)S(1)}, bf16[256,512]{1,0:T(8,128)(2,1)S(1)}, u32[]{:S(2)}, u32[]{:S(2)}) %collective-permute-start.5) | collective-permute-done | bytes 262176 | tf_op jit(solution)/shard_map/ppermute | solution.py:53
  34.4 3.6 %collective-permute-start.15 = (bf16[1,8,5,16,256]{4,3,2,1,0:T(8,128)(2,1)S(1)}, bf16[1,8,5,16,256]{4,3,2,1,0:T(8,128)(2,1)S(1)}, u32[]{:S(2)}, u32[]{:S(2)}) collective-permute-start(bf16[1,8,5,16,256]{4,3,2,1,0:T(8,128)(2,1)S(1)} %get-tuple-element.31), channel_id=1, source_target_pairs={{0,16},{8,56},{16,32},{24,8},{32,48},{40,24},{48,0},{56,40},{64,80... | collective-permute-start | bytes 983048 | tf_op jit(solution)/shard_map/ppermute | solution.py:29
  39.6 2.4 %collective-permute-done.15.refs_15_ = bf16[1,8,5,16,256]{4,3,2,1,0:T(8,128)(2,1)S(1)} collective-permute-done((bf16[1,8,5,16,256]{4,3,2,1,0:T(8,128)(2,1)S(1)}, bf16[1,8,5,16,256]{4,3,2,1,0:T(8,128)(2,1)S(1)}, u32[]{:S(2)}, u32[]{:S(2)}) %collective-permute-start.15) | collective-permute-done | bytes 327712 | tf_op jit(solution)/shard_map/ppermute | solution.py:29
  43.8 4.5 %collective-permute-done.16.refs_16_ = bf16[1,8,5,16,256]{4,3,2,1,0:T(8,128)(2,1)S(1)} collective-permute-done((bf16[1,8,5,16,256]{4,3,2,1,0:T(8,128)(2,1)S(1)}, bf16[1,8,5,16,256]{4,3,2,1,0:T(8,128)(2,1)S(1)}, u32[]{:S(2)}, u32[]{:S(2)}) %collective-permute-start.16) | collective-permute-done | bytes 327712 | tf_op jit(solution)/shard_map/ppermute | solution.py:29
  51.3 2.5 %collective-permute-done.8.refs_8_ = bf16[128,512]{1,0:T(8,128)(2,1)S(1)} collective-permute-done((bf16[128,512]{1,0:T(8,128)(2,1)S(1)}, bf16[128,512]{1,0:T(8,128)(2,1)S(1)}, u32[]{:S(2)}, u32[]{:S(2)}) %collective-permute-start.8) | collective-permute-done | bytes 131104 | tf_op jit(solution)/shard_map/ppermute | solution.py:53
  55.4 2.1 %collective-permute-done.18.refs_18_ = bf16[1,8,5,16,256]{4,3,2,1,0:T(8,128)(2,1)S(1)} collective-permute-done((bf16[1,8,5,16,256]{4,3,2,1,0:T(8,128)(2,1)S(1)}, bf16[1,8,5,16,256]{4,3,2,1,0:T(8,128)(2,1)S(1)}, u32[]{:S(2)}, u32[]{:S(2)}) %collective-permute-start.18) | collective-permute-done | bytes 327712 | tf_op jit(solution)/shard_map/ppermute | solution.py:29
  57.6 4.3 %forward.1 = (f32[256,2048]{1,0:T(8,128)S(1)}, bf16[256,2048]{1,0:T(8,128)(2,1)S(1)}, bf16[64,2048]{1,0:T(8,128)(2,1)S(1)}, bf16[64,2048]{1,0:T(8,128)(2,1)S(1)}...) custom-call(s32[45]{0:T(128)S(1)} %concatenate.6.meta, ...), custom_call_target="tpu_custom_call" | custom-call | flops 1342177280 | bytes 7340032 | tf_op jit(solution)/shard_map/forward/pallas_call | solution.py:63
  61.8 2.2 %collective-permute-start.19 = (bf16[256,2048]{1,0:T(8,128)(2,1)S(1)}, bf16[256,2048]{1,0:T(8,128)(2,1)S(1)}, u32[]{:S(2)}, u32[]{:S(2)}) collective-permute-start(bf16[256,2048]{1,0:T(8,128)(2,1)S(1)} %get-tuple-element.34.mine), channel_id=1, source_target_pairs={{0,8},{8,0},{16,24},{24,16},{32,40},{40,32},{48,56},{56,48},{64,72... | collective-permute-start | bytes 3145736 | tf_op jit(solution)/shard_map/ppermute | solution.py:41
  66.7 4.6 %collective-permute-done.20.up = bf16[64,2048]{1,0:T(8,128)(2,1)S(1)} collective-permute-done((bf16[64,2048]{1,0:T(8,128)(2,1)S(1)}, bf16[64,2048]{1,0:T(8,128)(2,1)S(1)}, u32[]{:S(2)}, u32[]{:S(2)}) %collective-permute-start.20) | collective-permute-done | bytes 262176 | tf_op jit(solution)/shard_map/ppermute | solution.py:49
  71.3 4.0 %collective-permute-done.21.down = bf16[64,2048]{1,0:T(8,128)(2,1)S(1)} collective-permute-done((bf16[64,2048]{1,0:T(8,128)(2,1)S(1)}, bf16[64,2048]{1,0:T(8,128)(2,1)S(1)}, u32[]{:S(2)}, u32[]{:S(2)}) %collective-permute-start.21) | collective-permute-done | bytes 262176 | tf_op jit(solution)/shard_map/ppermute | solution.py:49
  75.2 8.7 %backward.1 = (bf16[8,21,16,256]{3,2,1,0:T(8,128)(2,1)S(1)}, bf16[8,21,16,256]{3,2,1,0:T(8,128)(2,1)}, bf16[8,21,16,256]{3,2,1,0:T(8,128)(2,1)}, bf16[4,21,16,25...) custom-call(s32[45]{0:T(128)S(1)} %concatenate.6.meta, ...), custom_call_target="tpu_custom_call" | custom-call | flops 1342177280 | bytes 6889472 | tf_op jit(solution)/shard_map/backward/pallas_call | solution.py:63
  85.9 3.2 %collective-permute-start.22 = (bf16[16,128,256]{2,1,0:T(8,128)(2,1)S(1)}, bf16[16,128,256]{2,1,0:T(8,128)(2,1)S(1)}, u32[]{:S(2)}, u32[]{:S(2)}) collective-permute-start(bf16[16,128,256]{2,1,0:T(8,128)(2,1)S(1)} %get-tuple-element.41), channel_id=1, source_target_pairs={{0,8},{8,0},{16,24},{24,16},{32,40},{40,32},{48,56},{56,48},{64,72... | collective-permute-start | bytes 3145736 | tf_op jit(solution)/shard_map/ppermute | solution.py:41
  89.8 5.3 %collective-permute-start.24 = (bf16[8,21,16,256]{3,2,1,0:T(8,128)(2,1)}, bf16[8,21,16,256]{3,2,1,0:T(8,128)(2,1)S(1)}, u32[]{:S(2)}, u32[]{:S(2)}) collective-permute-start(bf16[8,21,16,256]{3,2,1,0:T(8,128)(2,1)} %get-tuple-element.44), channel_id=1, source_target_pairs={{0,192},{8,56},{16,208},{24,8},{32,224},{40,24},{48,240},{56,40},{... | collective-permute-start | bytes 4128776 | tf_op jit(solution)/shard_map/ppermute | solution.py:29
  96.2 4.2 %all-to-all-start = ((bf16[16,128,256]{2,1,0:T(8,128)(2,1)}), bf16[16,128,256]{2,1,0:T(8,128)(2,1)}, u32[]{:S(2)}, u32[]{:S(2)}) async-start(bf16[16,128,256]{2,1,0:T(8,128)(2,1)} %broadcast_select_fusion._), calls=%async_computation | async-start | bytes 2097152 | tf_op jit(solution)/shard_map/all_to_all | solution.py:424
  100.4 11.0 %collective-permute-done.23.m1 = bf16[8,21,16,256]{3,2,1,0:T(8,128)(2,1)S(1)} collective-permute-done((bf16[8,21,16,256]{3,2,1,0:T(8,128)(2,1)}, bf16[8,21,16,256]{3,2,1,0:T(8,128)(2,1)S(1)}, u32[]{:S(2)}, u32[]{:S(2)}) %collective-permute-start.23) | collective-permute-done | bytes 1376288 | tf_op jit(solution)/shard_map/ppermute | solution.py:29
  116.2 9.0 %collective-permute-done.25.p1 = bf16[4,22,16,256]{3,2,1,0:T(8,128)(2,1)S(1)} collective-permute-done((bf16[4,22,16,256]{3,2,1,0:T(8,128)(2,1)S(1)}, bf16[4,22,16,256]{3,2,1,0:T(8,128)(2,1)S(1)}, u32[]{:S(2)}, u32[]{:S(2)}) %collective-permute-start.25) | collective-permute-done | bytes 720928 | tf_op jit(solution)/shard_map/ppermute | solution.py:29
  126.4 2.7 %collective-permute-start.28 = (bf16[8,6,16,256]{3,2,1,0:T(8,128)(2,1)S(1)}, bf16[8,6,16,256]{3,2,1,0:T(8,128)(2,1)S(1)}, u32[]{:S(2)}, u32[]{:S(2)}) collective-permute-start(bf16[8,6,16,256]{3,2,1,0:T(8,128)(2,1)S(1)} %get-tuple-element.51), channel_id=1, source_target_pairs={{0,48},{8,200},{16,0},{24,216},{32,16},{40,232},{48,32},{56,248},{... | collective-permute-start | bytes 1179656 | tf_op jit(solution)/shard_map/ppermute | solution.py:29
  130.3 8.4 %collective-permute-done.27.prev = bf16[8,6,16,256]{3,2,1,0:T(8,128)(2,1)S(1)} collective-permute-done((bf16[8,6,16,256]{3,2,1,0:T(8,128)(2,1)S(1)}, bf16[8,6,16,256]{3,2,1,0:T(8,128)(2,1)S(1)}, u32[]{:S(2)}, u32[]{:S(2)}) %collective-permute-start.27) | collective-permute-done | bytes 393248 | tf_op jit(solution)/shard_map/ppermute | solution.py:29
  139.6 4.0 %collective-permute-start.30 = (bf16[8,7,8,256]{3,2,1,0:T(8,128)(2,1)S(1)}, bf16[8,7,8,256]{3,2,1,0:T(8,128)(2,1)S(1)}, u32[]{:S(2)}, u32[]{:S(2)}) collective-permute-start(bf16[8,7,8,256]{3,2,1,0:T(8,128)(2,1)S(1)} %get-tuple-element.54), channel_id=1, source_target_pairs={{0,8},{8,0},{16,24},{24,16},{32,40},{40,32},{48,56},{56,48},{64,72... | collective-permute-start | bytes 688136 | tf_op jit(solution)/shard_map/ppermute | solution.py:41
  (79 shorter events, 37.0 us)
Async XLA Ops:
  6.7 15.5 %collective-permute-start.11 = (bf16[2,8,5,16,256]{4,3,2,1,0:T(8,128)(2,1)S(1)}, bf16[2,8,5,16,256]{4,3,2,1,0:T(8,128)(2,1)S(1)}, u32[]{:S(2)}, u32[]{:S(2)}) collective-permute-start(bf16[2,8,5,16,256]{4,3,2,1,0:T(8,128)(2,1)S(1)} %pad_maximum_fusion.src.refs_9_), channel_id=1, source_target_pairs={{0,192},{8,72},{16,208},{24,88},{32,224},{40,104},{48,240},{56,120... | collective-permute-start | bytes 1966088 | tf_op jit(solution)/shard_map/ppermute | solution.py:29
  6.8 15.4 %collective-permute-start.10 = (bf16[2,8,5,16,256]{4,3,2,1,0:T(8,128)(2,1)S(1)}, bf16[2,8,5,16,256]{4,3,2,1,0:T(8,128)(2,1)S(1)}, u32[]{:S(2)}, u32[]{:S(2)}) collective-permute-start(bf16[2,8,5,16,256]{4,3,2,1,0:T(8,128)(2,1)S(1)} %pad_maximum_fusion.src.refs_9_), channel_id=1, source_target_pairs={{0,16},{8,56},{16,32},{24,8},{32,48},{40,24},{48,0},{56,40},{64,80... | collective-permute-start | bytes 1966088 | tf_op jit(solution)/shard_map/ppermute | solution.py:29
  8.9 10.1 %collective-permute-start.4 = (bf16[256,512]{1,0:T(8,128)(2,1)S(1)}, bf16[256,512]{1,0:T(8,128)(2,1)S(1)}, u32[]{:S(2)}, u32[]{:S(2)}) collective-permute-start(bf16[256,512]{1,0:T(8,128)(2,1)S(1)} %pad_maximum_fusion.1.refs_0_), channel_id=1, source_target_pairs={{0,7},{1,0},{2,1},{3,2},{4,3},{5,4},{6,5},{7,6},{8,15},{9,8},{10,9... | collective-permute-start | bytes 786440 | tf_op jit(solution)/shard_map/ppermute | solution.py:53
  14.5 7.6 %collective-permute-start.1 = (bf16[256,512]{1,0:T(8,128)(2,1)S(1)}, bf16[256,512]{1,0:T(8,128)(2,1)S(1)}, u32[]{:S(2)}, u32[]{:S(2)}) collective-permute-start(bf16[256,512]{1,0:T(8,128)(2,1)S(1)} %pad_maximum_fusion.1.refs_0_), channel_id=1, source_target_pairs={{0,1},{1,2},{2,3},{3,4},{4,5},{5,6},{6,7},{7,0},{8,9},{9,10},{10,1... | collective-permute-start | bytes 786440 | tf_op jit(solution)/shard_map/ppermute | solution.py:53
  22.8 11.0 %collective-permute-start.12 = (bf16[2,8,5,16,256]{4,3,2,1,0:T(8,128)(2,1)S(1)}, bf16[2,8,5,16,256]{4,3,2,1,0:T(8,128)(2,1)S(1)}, u32[]{:S(2)}, u32[]{:S(2)}) collective-permute-start(bf16[2,8,5,16,256]{4,3,2,1,0:T(8,128)(2,1)S(1)} %hold.1), channel_id=1, source_target_pairs={{0,48},{8,24},{16,0},{24,40},{32,16},{40,56},{48,32},{56,8},{64,11... | collective-permute-start | bytes 1966088 | tf_op jit(solution)/shard_map/ppermute | solution.py:29
  22.9 10.9 %collective-permute-start.13 = (bf16[2,8,5,16,256]{4,3,2,1,0:T(8,128)(2,1)S(1)}, bf16[2,8,5,16,256]{4,3,2,1,0:T(8,128)(2,1)S(1)}, u32[]{:S(2)}, u32[]{:S(2)}) collective-permute-start(bf16[2,8,5,16,256]{4,3,2,1,0:T(8,128)(2,1)S(1)} %collective-permute-done.10.refs_0_.a.refs_10_), channel_id=1, source_target_pairs={{0,64},{8,200},{16,80},{24,216},{32,96},{40,232},{48,112},{56,248}... | collective-permute-start | bytes 1966088 | tf_op jit(solution)/shard_map/ppermute | solution.py:29
  34.4 7.6 %collective-permute-start.15 = (bf16[1,8,5,16,256]{4,3,2,1,0:T(8,128)(2,1)S(1)}, bf16[1,8,5,16,256]{4,3,2,1,0:T(8,128)(2,1)S(1)}, u32[]{:S(2)}, u32[]{:S(2)}) collective-permute-start(bf16[1,8,5,16,256]{4,3,2,1,0:T(8,128)(2,1)S(1)} %get-tuple-element.31), channel_id=1, source_target_pairs={{0,16},{8,56},{16,32},{24,8},{32,48},{40,24},{48,0},{56,40},{64,80... | collective-permute-start | bytes 983048 | tf_op jit(solution)/shard_map/ppermute | solution.py:29
  38.0 17.4 %collective-permute-start.14 = (bf16[2,8,5,16,256]{4,3,2,1,0:T(8,128)(2,1)S(1)}, bf16[2,8,5,16,256]{4,3,2,1,0:T(8,128)(2,1)S(1)}, u32[]{:S(2)}, u32[]{:S(2)}) collective-permute-start(bf16[2,8,5,16,256]{4,3,2,1,0:T(8,128)(2,1)S(1)} %collective-permute-done.12.c.refs_12_), channel_id=1, source_target_pairs={{0,192},{8,72},{16,208},{24,88},{32,224},{40,104},{48,240},{56,120... | collective-permute-start | bytes 1966088 | tf_op jit(solution)/shard_map/ppermute | solution.py:29
  38.1 10.2 %collective-permute-start.16 = (bf16[1,8,5,16,256]{4,3,2,1,0:T(8,128)(2,1)S(1)}, bf16[1,8,5,16,256]{4,3,2,1,0:T(8,128)(2,1)S(1)}, u32[]{:S(2)}, u32[]{:S(2)}) collective-permute-start(bf16[1,8,5,16,256]{4,3,2,1,0:T(8,128)(2,1)S(1)} %get-tuple-element.32), channel_id=1, source_target_pairs={{0,48},{8,24},{16,0},{24,40},{32,16},{40,56},{48,32},{56,8},{64,11... | collective-permute-start | bytes 983048 | tf_op jit(solution)/shard_map/ppermute | solution.py:29
  38.1 11.5 %collective-permute-start.6 = (bf16[256,512]{1,0:T(8,128)(2,1)S(1)}, bf16[256,512]{1,0:T(8,128)(2,1)S(1)}, u32[]{:S(2)}, u32[]{:S(2)}) collective-permute-start(bf16[256,512]{1,0:T(8,128)(2,1)S(1)} %collective-permute-done.5.refs_2_.refs_5_), channel_id=1, source_target_pairs={{0,7},{1,0},{2,1},{3,2},{4,3},{5,4},{6,5},{7,6},{8,15},{9,8},{10,9... | collective-permute-start | bytes 786440 | tf_op jit(solution)/shard_map/ppermute | solution.py:53
  38.3 11.7 %collective-permute-start.3 = (bf16[256,512]{1,0:T(8,128)(2,1)S(1)}, bf16[256,512]{1,0:T(8,128)(2,1)S(1)}, u32[]{:S(2)}, u32[]{:S(2)}) collective-permute-start(bf16[256,512]{1,0:T(8,128)(2,1)S(1)} %collective-permute-done.2.refs_1_.refs_2_), channel_id=1, source_target_pairs={{0,1},{1,2},{2,3},{3,4},{4,5},{5,6},{6,7},{7,0},{8,9},{9,10},{10,1... | collective-permute-start | bytes 786440 | tf_op jit(solution)/shard_map/ppermute | solution.py:53
  42.0 13.4 %collective-permute-start.17 = (bf16[1,8,5,16,256]{4,3,2,1,0:T(8,128)(2,1)S(1)}, bf16[1,8,5,16,256]{4,3,2,1,0:T(8,128)(2,1)S(1)}, u32[]{:S(2)}, u32[]{:S(2)}) collective-permute-start(bf16[1,8,5,16,256]{4,3,2,1,0:T(8,128)(2,1)S(1)} %collective-permute-done.15.refs_15_), channel_id=1, source_target_pairs={{0,64},{8,200},{16,80},{24,216},{32,96},{40,232},{48,112},{56,248}... | collective-permute-start | bytes 983048 | tf_op jit(solution)/shard_map/ppermute | solution.py:29
  48.3 9.3 %collective-permute-start.18 = (bf16[1,8,5,16,256]{4,3,2,1,0:T(8,128)(2,1)S(1)}, bf16[1,8,5,16,256]{4,3,2,1,0:T(8,128)(2,1)S(1)}, u32[]{:S(2)}, u32[]{:S(2)}) collective-permute-start(bf16[1,8,5,16,256]{4,3,2,1,0:T(8,128)(2,1)S(1)} %collective-permute-done.16.refs_16_), channel_id=1, source_target_pairs={{0,192},{8,72},{16,208},{24,88},{32,224},{40,104},{48,240},{56,120... | collective-permute-start | bytes 983048 | tf_op jit(solution)/shard_map/ppermute | solution.py:29
  61.8 13.4 %collective-permute-start.19 = (bf16[256,2048]{1,0:T(8,128)(2,1)S(1)}, bf16[256,2048]{1,0:T(8,128)(2,1)S(1)}, u32[]{:S(2)}, u32[]{:S(2)}) collective-permute-start(bf16[256,2048]{1,0:T(8,128)(2,1)S(1)} %get-tuple-element.34.mine), channel_id=1, source_target_pairs={{0,8},{8,0},{16,24},{24,16},{32,40},{40,32},{48,56},{56,48},{64,72... | collective-permute-start | bytes 3145736 | tf_op jit(solution)/shard_map/ppermute | solution.py:41
  65.4 9.8 %collective-permute-start.21 = (bf16[64,2048]{1,0:T(8,128)(2,1)S(1)}, bf16[64,2048]{1,0:T(8,128)(2,1)S(1)}, u32[]{:S(2)}, u32[]{:S(2)}) collective-permute-start(bf16[64,2048]{1,0:T(8,128)(2,1)S(1)} %get-tuple-element.36), channel_id=1, source_target_pairs={{16,8},{24,0},{32,24},{40,16},{48,40},{56,32},{64,56},{72,48},{80,... | collective-permute-start | bytes 786440 | tf_op jit(solution)/shard_map/ppermute | solution.py:49
  85.9 9.2 %collective-permute-start.22 = (bf16[16,128,256]{2,1,0:T(8,128)(2,1)S(1)}, bf16[16,128,256]{2,1,0:T(8,128)(2,1)S(1)}, u32[]{:S(2)}, u32[]{:S(2)}) collective-permute-start(bf16[16,128,256]{2,1,0:T(8,128)(2,1)S(1)} %get-tuple-element.41), channel_id=1, source_target_pairs={{0,8},{8,0},{16,24},{24,16},{32,40},{40,32},{48,56},{56,48},{64,72... | collective-permute-start | bytes 3145736 | tf_op jit(solution)/shard_map/ppermute | solution.py:41
  89.1 22.3 %collective-permute-start.23 = (bf16[8,21,16,256]{3,2,1,0:T(8,128)(2,1)}, bf16[8,21,16,256]{3,2,1,0:T(8,128)(2,1)S(1)}, u32[]{:S(2)}, u32[]{:S(2)}) collective-permute-start(bf16[8,21,16,256]{3,2,1,0:T(8,128)(2,1)} %get-tuple-element.43), channel_id=1, source_target_pairs={{0,64},{8,24},{16,80},{24,40},{32,96},{40,56},{48,112},{56,8},{64,... | collective-permute-start | bytes 4128776 | tf_op jit(solution)/shard_map/ppermute | solution.py:29
  89.8 21.6 %collective-permute-start.24 = (bf16[8,21,16,256]{3,2,1,0:T(8,128)(2,1)}, bf16[8,21,16,256]{3,2,1,0:T(8,128)(2,1)S(1)}, u32[]{:S(2)}, u32[]{:S(2)}) collective-permute-start(bf16[8,21,16,256]{3,2,1,0:T(8,128)(2,1)} %get-tuple-element.44), channel_id=1, source_target_pairs={{0,192},{8,56},{16,208},{24,8},{32,224},{40,24},{48,240},{56,40},{... | collective-permute-start | bytes 4128776 | tf_op jit(solution)/shard_map/ppermute | solution.py:29
  96.2 47.4 %all-to-all-start = ((bf16[16,128,256]{2,1,0:T(8,128)(2,1)}), bf16[16,128,256]{2,1,0:T(8,128)(2,1)}, u32[]{:S(2)}, u32[]{:S(2)}) async-start(bf16[16,128,256]{2,1,0:T(8,128)(2,1)} %broadcast_select_fusion._), calls=%async_computation | async-start | bytes 2097152 | tf_op jit(solution)/shard_map/all_to_all | solution.py:424
  113.4 11.8 %collective-permute-start.25 = (bf16[4,22,16,256]{3,2,1,0:T(8,128)(2,1)S(1)}, bf16[4,22,16,256]{3,2,1,0:T(8,128)(2,1)S(1)}, u32[]{:S(2)}, u32[]{:S(2)}) collective-permute-start(bf16[4,22,16,256]{3,2,1,0:T(8,128)(2,1)S(1)} %get-tuple-element.47), channel_id=1, source_target_pairs={{0,64},{8,24},{16,80},{24,40},{32,96},{40,56},{48,112},{56,8},{64,... | collective-permute-start | bytes 2162696 | tf_op jit(solution)/shard_map/ppermute | solution.py:29
  114.3 10.9 %collective-permute-start.26 = (bf16[4,22,16,256]{3,2,1,0:T(8,128)(2,1)S(1)}, bf16[4,22,16,256]{3,2,1,0:T(8,128)(2,1)S(1)}, u32[]{:S(2)}, u32[]{:S(2)}) collective-permute-start(bf16[4,22,16,256]{3,2,1,0:T(8,128)(2,1)S(1)} %get-tuple-element.48), channel_id=1, source_target_pairs={{0,192},{8,56},{16,208},{24,8},{32,224},{40,24},{48,240},{56,40},{... | collective-permute-start | bytes 2162696 | tf_op jit(solution)/shard_map/ppermute | solution.py:29
  126.3 12.4 %collective-permute-start.27 = (bf16[8,6,16,256]{3,2,1,0:T(8,128)(2,1)S(1)}, bf16[8,6,16,256]{3,2,1,0:T(8,128)(2,1)S(1)}, u32[]{:S(2)}, u32[]{:S(2)}) collective-permute-start(bf16[8,6,16,256]{3,2,1,0:T(8,128)(2,1)S(1)} %get-tuple-element.50), channel_id=1, source_target_pairs={{0,16},{8,72},{16,32},{24,88},{32,48},{40,104},{48,0},{56,120},{64... | collective-permute-start | bytes 1179656 | tf_op jit(solution)/shard_map/ppermute | solution.py:29
  126.4 12.3 %collective-permute-start.28 = (bf16[8,6,16,256]{3,2,1,0:T(8,128)(2,1)S(1)}, bf16[8,6,16,256]{3,2,1,0:T(8,128)(2,1)S(1)}, u32[]{:S(2)}, u32[]{:S(2)}) collective-permute-start(bf16[8,6,16,256]{3,2,1,0:T(8,128)(2,1)S(1)} %get-tuple-element.51), channel_id=1, source_target_pairs={{0,48},{8,200},{16,0},{24,216},{32,16},{40,232},{48,32},{56,248},{... | collective-permute-start | bytes 1179656 | tf_op jit(solution)/shard_map/ppermute | solution.py:29
  129.1 9.7 %collective-permute-start.29 = (bf16[8,6,16,256]{3,2,1,0:T(8,128)(2,1)S(1)}, bf16[8,6,16,256]{3,2,1,0:T(8,128)(2,1)S(1)}, u32[]{:S(2)}, u32[]{:S(2)}) collective-permute-start(bf16[8,6,16,256]{3,2,1,0:T(8,128)(2,1)S(1)} %get-tuple-element.52), channel_id=1, source_target_pairs={{0,32},{8,136},{16,48},{24,152},{32,0},{40,168},{48,16},{56,184},{... | collective-permute-start | bytes 1179656 | tf_op jit(solution)/shard_map/ppermute | solution.py:29
  (17 other events, 104.1 us)

commit v2 on v1

--- a/solution.py
+++ b/solution.py
@@ -1,3 +1,5 @@
+import functools
+
 import jax
 import jax.numpy as jnp
 from jax import lax
@@ -124,7 +126,8 @@
 
 def forward_kernel(meta, *refs):
     tokens, pieces, outs = refs[:9], refs[9:19], refs[19:]
-    pre, out, top, bot, wts, tok, sem = outs
+    pre, *halves, wts, tok, sem = outs
+    rows, tops, bots = halves[:2], halves[2:4], halves[4:]
     start_tokens(meta, tokens, tok, sem)
     plan = weight_plan(meta, pieces)
     core = meta[CORE]
@@ -144,28 +147,31 @@
             acc = part if acc is None else acc + part
         return acc
 
-    @pl.when(core == 0)
-    def _():
-        @pl.loop(0, COLS)
-        def _(c):
-            p = total(c, ((1,), (0,)))
-            pre[:, lanes(c)] = p
-            t = jnp.tanh(root_two_pi * (p + cubic_coef * p * p * p))
-            out[:, lanes(c)] = (0.5 * p * (1.0 + t)).astype(BF16)
-
-    @pl.when(core != 0)
-    def _():
-        @pl.loop(0, COLS)
-        def _(c):
-            out[:, lanes(c)] = total(c, ((1,), (1,))).astype(BF16)
-
-    top[...] = out[:PW]
-    bot[...] = out[TOK - PW :]
+    for half, out in enumerate(rows):
+        first_col = half * SPLIT
+
+        @pl.when(core == 0)
+        def _():
+            @pl.loop(0, SPLIT)
+            def _(c):
+                p = total(c + first_col, ((1,), (0,)))
+                pre[:, lanes(c + first_col)] = p
+                t = jnp.tanh(root_two_pi * (p + cubic_coef * p * p * p))
+                out[:, lanes(c)] = (0.5 * p * (1.0 + t)).astype(BF16)
+
+        @pl.when(core != 0)
+        def _():
+            @pl.loop(0, SPLIT)
+            def _(c):
+                out[:, lanes(c)] = total(c + first_col, ((1,), (1,))).astype(BF16)
+
+        tops[half][...] = out[:PW]
+        bots[half][...] = out[TOK - PW :]
 
 
 def forward(meta, tokens, pieces):
-    wide = COLS * BS
-    outs = [((TOK, wide), F32), ((TOK, wide), BF16), ((PW, wide), BF16), ((PW, wide), BF16)]
+    wide = SPLIT * BS
+    outs = [((TOK, COLS * BS), F32)] + [((TOK, wide), BF16)] * 2 + [((PW, wide), BF16)] * 4
     outs += [((COLS, NNZ, 16, 16, BS), BF16), ((16, TOK, BS), BF16)]
     return local(
         forward_kernel,
@@ -189,8 +195,9 @@
     return out
 
 
-def backward_kernel(meta, tok, got, mine, up, down, pre, taps, *refs):
-    g0, m1, m3, g1, g3, pgrad, conv, lhs, res, slab, moved = refs
+def backward_kernel(half, meta, tok, got, mine, up, down, pre, taps, *refs):
+    refs = refs[-10:]
+    g0, far_out, direct, through, pgrad, conv, lhs, res, slab, moved = refs
     core, x, y = meta[CORE], meta[XPOS], meta[YPOS]
     is_in = core == 0
     slab[...] = jnp.zeros_like(slab)
@@ -198,13 +205,15 @@
     far = jnp.where(is_in, NX, 1)
     near = jnp.where(is_in, 1, NY)
 
-    @pl.loop(0, COLS)
+    @pl.loop(0, SPLIT)
     def _(c):
         cols = lanes(c)
+        wide = lanes(c + half * SPLIT)
+        first_row = (c + half * SPLIT) * NNZ
         for i, rows in enumerate(shifted_rows(got, up, down, cols)):
             for b in range(3):
                 moved[3 * i + b] = rows[b]
-        tap = [jnp.where(is_in, taps[8 - j : 9 - j, cols], taps[j : j + 1, cols]) for j in range(9)]
+        tap = [jnp.where(is_in, taps[8 - j : 9 - j, wide], taps[j : j + 1, wide]) for j in range(9)]
         for i in range(4):
             acc = jnp.zeros((PW, BS), F32)
             for a in range(3):
@@ -214,7 +223,7 @@
 
         @pl.when(is_in)
         def _():
-            p = pre[:, cols]
+            p = pre[:, wide]
             t = jnp.tanh(root_two_pi * (p + cubic_coef * p * p * p))
             slope = 0.5 * (1.0 + t) + 0.5 * p * (1.0 - t * t) * root_two_pi * (
                 1.0 + 3.0 * cubic_coef * p * p
@@ -222,14 +231,14 @@
             lhs[...] = (conv[...] * slope).astype(BF16)
             pgrad[:, cols] = lhs[...]
             for k in range(NNZ):
-                part = dot(tok[meta[c * NNZ + k]], lhs[...], ((0,), (0,))) * loss_scale
+                part = dot(tok[meta[first_row + k]], lhs[...], ((0,), (0,))) * loss_scale
                 res[k] = part.astype(BF16).reshape(16, 16, BS)
 
         @pl.when(core != 0)
         def _():
             lhs[...] = conv[...].astype(BF16)
             for k in range(NNZ):
-                part = dot(lhs[...], tok[meta[c * NNZ + k]], ((0,), (0,))) * loss_scale
+                part = dot(lhs[...], tok[meta[first_row + k]], ((0,), (0,))) * loss_scale
                 res[k] = part.astype(BF16).reshape(16, 16, BS)
             sums = []
             for a in range(3):
@@ -241,31 +250,16 @@
             rows = jnp.concatenate(sums + [jnp.zeros((7, BS), F32)], axis=0) * loss_scale
             slab[...] = rows.astype(BF16)
 
-        def emit(out, d, at):
+        for out, d in ((g0, 0), (far_out, 2), (direct, 1 if half else 3), (through, 3 if half else 1)):
             start = (here + d) % 4 * far
             for k in range(NNZ):
                 for s in range(4):
-                    out[at, k * 4 + s] = res[k, start + s * near]
-            out[at, KERN] = slab[...]
-
-        emit(g0, 0, c)
-
-        @pl.when(c < SPLIT)
-        def _():
-            emit(m1, 2, c)
-            emit(g1, 1, c)
-            emit(m3, 3, c + SPLIT)
-
-        @pl.when(c >= SPLIT)
-        def _():
-            emit(m3, 2, c - SPLIT)
-            emit(m1, 1, c)
-            emit(g3, 3, c - SPLIT)
-
-
-def backward(meta, tok, got, mine, up, down, pre, taps):
-    full, part = (COLS, KERN + 1, 16, BS), (SPLIT, KERN + 1, 16, BS)
-    outs = [(full, BF16)] * 3 + [(part, BF16)] * 2 + [((TOK, COLS * BS), BF16)]
+                    out[c, k * 4 + s] = res[k, start + s * near]
+            out[c, KERN] = slab[...]
+
+
+def backward(half, meta, tok, got, mine, up, down, pre, taps, before):
+    outs = [((SPLIT, KERN + 1, 16, BS), BF16)] * 4 + [((TOK, SPLIT * BS), BF16)]
     scratch = [
         pltpu.VMEM((TOK, BS), F32),
         pltpu.VMEM((TOK, BS), BF16),
@@ -273,22 +267,24 @@
         pltpu.VMEM((16, BS), BF16),
         pltpu.VMEM((18, PW, BS), F32),
     ]
-    args = (meta, tok, got, mine, up, down, pre, taps)
-    return local(
-        backward_kernel, "backward", outs, args, scratch, flops=2 * TOK * BS * BS * NNZ * COLS
-    )
-
-
-def token_grad_kernel(meta, pgrad, wts, keep, send, acc):
+    kernel = functools.partial(backward_kernel, half)
+    args = (meta, tok, got, mine, up, down, pre, taps, *before)
+    return local(kernel, "backward", outs, args, scratch, flops=2 * TOK * BS * BS * NNZ * SPLIT)
+
+
+def token_grad_kernel(meta, pg0, pg1, wts, _, keep, send, acc):
     @pl.when(meta[CORE] == 0)
     def _():
         acc[...] = jnp.zeros_like(acc)
 
-        @pl.loop(0, COLS)
-        def _(c):
-            for k in range(NNZ):
-                wt = wts[c, k].reshape(BS, BS)
-                acc[meta[c * NNZ + k]] += dot(pgrad[:, lanes(c)], wt, ((1,), (1,)))
+        for half, pgrad in enumerate((pg0, pg1)):
+
+            @pl.loop(0, SPLIT)
+            def _(c):
+                for k in range(NNZ):
+                    wt = wts[c + half * SPLIT, k].reshape(BS, BS)
+                    row = meta[(c + half * SPLIT) * NNZ + k]
+                    acc[row] += dot(pgrad[:, lanes(c)], wt, ((1,), (1,)))
 
         @pl.loop(0, 16)
         def _(r):
@@ -296,12 +292,12 @@
             send[r] = acc[r, 128:].astype(BF16)
 
 
-def token_grad(meta, pgrad, wts):
+def token_grad(meta, pg0, pg1, wts, before):
     return local(
         token_grad_kernel,
         "tokengrad",
         [((16, 128, BS), BF16)] * 2,
-        (meta, pgrad, wts),
+        (meta, pg0, pg1, wts, before),
         [pltpu.VMEM((16, TOK, BS), F32)],
         flops=2 * TOK * BS * BS * NNZ * COLS,
     )
@@ -315,32 +311,39 @@
         out[:, b * BS : (b + 1) * BS] = total.astype(BF16)
 
 
-def relay_kernel(meta, g1, g3, m1, m3, _, o1, o3):
-    for out, own, got in ((o1, g1, m1), (o3, g3, m3)):
+def relay_kernel(meta, own, got, *refs):
+    out = refs[-1]
+
+    @pl.loop(0, SPLIT)
+    def _(c):
+        for k in range(KERN):
+            out[c, k] = (own[c, k].astype(F32) + got[c, k].astype(F32)).astype(BF16)
+        out[c, KERN] = own[c, KERN]
+        out[c, KERN + 1] = got[c, KERN]
+
+
+def relay(meta, own, got, *others):
+    outs = [((SPLIT, KERN + 2, 16, BS), BF16)]
+    return local(relay_kernel, "relay", outs, (meta, own, got, *others), hbm=(4,))[0]
+
+
+def first_sum_kernel(meta, *refs):
+    outs = refs[6:]
+    here = jnp.where(meta[CORE] == 0, meta[XPOS], meta[YPOS])
+
+    for half in range(2):
+        own, direct, relayed = refs[3 * half : 3 * half + 3]
 
         @pl.loop(0, SPLIT)
         def _(c):
-            for k in range(KERN):
-                out[c, k] = (own[c, k].astype(F32) + got[c, k].astype(F32)).astype(BF16)
-            out[c, KERN] = own[c, KERN]
-            out[c, KERN + 1] = got[c, KERN]
-
-
-def first_sum_kernel(meta, own, m1, m3, p1, p3, *outs):
-    here = jnp.where(meta[CORE] == 0, meta[XPOS], meta[YPOS])
-
-    for shift, relayed, direct in ((0, p1, m3), (SPLIT, p3, m1)):
-
-        @pl.loop(0, SPLIT)
-        def _(c):
-            at, got = c + shift, c + SPLIT
-            near = relayed[c, KERN].astype(F32) + direct[got, KERN].astype(F32)
-            far = own[at, KERN].astype(F32) + relayed[c, KERN + 1].astype(F32)
+            at = c + half * SPLIT
+            near = relayed[c, KERN].astype(F32) + direct[c, KERN].astype(F32)
+            far = own[c, KERN].astype(F32) + relayed[c, KERN + 1].astype(F32)
             for d in range(4):
                 s = (here + d) % 4
                 for k in range(NNZ):
-                    total = own[at, k * 4 + s].astype(F32) + relayed[c, k * 4 + s].astype(F32)
-                    outs[d][at, k] = (total + direct[got, k * 4 + s].astype(F32)).astype(BF16)
+                    total = own[c, k * 4 + s].astype(F32) + relayed[c, k * 4 + s].astype(F32)
+                    outs[d][at, k] = (total + direct[c, k * 4 + s].astype(F32)).astype(BF16)
                 outs[d][at, NNZ] = (far + near).astype(BF16)
 
 
@@ -411,16 +414,22 @@
     pieces = (own, wa, wb, wc, wd, we, wf, wg, wh, wi)
     token_pieces = (t0, zr1, zr2, zr3, zl1, zl2, zl3, zr4, zl4)
 
-    pre, out, top, bot, wts, tok = forward(meta, token_pieces, pieces)
-    got = to_partner(out)
-    up, down = to_next_chip(bot, 1), to_next_chip(top, -1)
-    g0, m1, m3, g1, g3, pgrad = backward(meta, tok, got, out, up, down, pre, mix_kernel)
-    m1, m3 = first(m1, 1), first(m3, -1)
-
-    keep, send = token_grad(meta, pgrad, wts)
+    pre, *halves, wts, tok = forward(meta, token_pieces, pieces)
+    out, top, bot = halves[:2], halves[2:4], halves[4:]
+    got = [to_partner(o) for o in out]
+    edges = [(to_next_chip(b, 1), to_next_chip(t, -1)) for t, b in zip(top, bot)]
+    signs = (1, -1)
+    half0 = backward(0, meta, tok, got[0], out[0], *edges[0], pre, mix_kernel, ())
+    half1 = backward(1, meta, tok, got[1], out[1], *edges[1], pre, mix_kernel, ())
+    g0, far, direct, through, pgrad = zip(half0, half1)
+    far = [first(f, s) for f, s in zip(far, signs)]
+    direct = [first(d, -s) for d, s in zip(direct, signs)]
+
+    relayed = [relay(meta, through[0], far[0], direct[0])]
+    keep, send = token_grad(meta, *pgrad, wts, relayed[0])
     terms = jnp.where(is_in, keep, to_partner(send))
-    relayed = [((SPLIT, KERN + 2, 16, BS), BF16)] * 2
-    r1, r3 = local(relay_kernel, "relay", relayed, (meta, g1, g3, m1, m3, terms), hbm=(5,))
+    relayed.append(relay(meta, through[1], far[1], direct[1], terms))
+    relayed = [first(r, s) for r, s in zip(relayed, signs)]
     terms = lax.all_to_all(terms, "hid", 0, 0, tiled=True)
     (grad_tokens,) = local(gather_sum_kernel, "gathersum", [((128, 512), BF16)], (meta, terms))
 
@@ -428,7 +437,7 @@
         first_sum_kernel,
         "firstsum",
         [((COLS, NNZ + 1, 16, BS), BF16)] * 4,
-        (meta, g0, m1, m3, first(r1, 1), first(r3, -1)),
+        (meta, g0[0], direct[0], relayed[0], g0[1], direct[1], relayed[1]),
     )
     last = (h[0], second(h[1], 1), second(h[3], -1), second(h[2], 2))
     shape = ((COLS, NNZ + 2, 8, BS), BF16)

time: 148 us -> 153 us (1.034)
  starting transfers between devices: 54.6 us -> 61.1 us
  waiting for transfers between devices: 64.4 us -> 61.5 us
    ppermute x16 -> x18, waiting for transfers between devices: 38.5 us -> 32.1 us  [by_core(): return lax.ppermute(value, ('crop', 'rows'), pairs)]
    ppermute x16 -> x18, starting transfers between devices: 24.7 us -> 29.4 us  [by_core(): return lax.ppermute(value, ('crop', 'rows'), pairs)]
    ppermute x2 -> x4, waiting for transfers between devices: 8.54 us -> 12.1 us  [to_next_chip(): return lax.ppermute(value, 'rows', pairs)]
    ppermute x2 -> x4, starting transfers between devices: 2.59 us -> 5.16 us  [to_next_chip(): return lax.ppermute(value, 'rows', pairs)]
    pallas_call x10 -> x12, Pallas kernels: 21.1 us -> 21.7 us  [local(): pl.pallas_call(kernel, out_shape=shapes, in_specs=[SMEM] + [HBM if i in h...]
    ppermute x5 -> x6, starting transfers between devices: 12.8 us -> 12.8 us  [to_partner(): return lax.ppermute(value, 'rows', [(r, r ^ 1) for r in range(16)])]
  transfers between devices with their start and end apart: 32 -> 37, of which waited for: 16 -> 21; matrix products, arithmetic and copies ran while one was open for 2% -> 2% of each run, Pallas kernels for 3% -> 6%
where the time goes in v2:
time: 153 us
  waiting for transfers between devices  61.5 us (40%)
  starting transfers between devices  61.1 us (40%)
  Pallas kernels  21.7 us (14%)
  other arithmetic  4.6 us (3%)
  local copies, waits for them, and re-layouts  3.18 us (2%)
    ppermute x18, waiting for transfers between devices, by_core(): return lax.ppermute(value, ('crop', 'rows'), pairs)  32.1 us
    ppermute x18, starting transfers between devices, by_core(): return lax.ppermute(value, ('crop', 'rows'), pairs)  29.4 us
    pallas_call x12, Pallas kernels, local(): pl.pallas_call(kernel, out_shape=shapes, in_specs=[SMEM] + [HBM if i in h...  21.7 us
    ppermute x8, waiting for transfers between devices, along_z(): return lax.ppermute(value, 'hid', [(z, (z + step) % NZ) for z in range(NZ)])  17.1 us
    ppermute x6, starting transfers between devices, to_partner(): return lax.ppermute(value, 'rows', [(r, r ^ 1) for r in range(16)])  12.8 us
    ppermute x4, waiting for transfers between devices, to_next_chip(): return lax.ppermute(value, 'rows', pairs)  12.1 us
    ppermute x8, starting transfers between devices, along_z(): return lax.ppermute(value, 'hid', [(z, (z + step) % NZ) for z in range(NZ)])  10.2 us
    ppermute x4, starting transfers between devices, to_next_chip(): return lax.ppermute(value, 'rows', pairs)  5.16 us
  transfers between devices with their start and end apart: 37, of which 21 were waited for; matrix products, arithmetic and copies ran while one was open for 2% of the time, Pallas kernels for 6%

profile of v2, /device:TPU:1, one launch (start us, length us, event | category | flops | bytes accessed | tf_op | source)
XLA Modules:
  0.0 153.0 jit_solution(10221311415482854540)
XLA Ops:
  1.8 3.3 %collective-permute-start.9 = (bf16[8,5,16,256]{3,2,1,0:T(8,128)(2,1)S(1)}, bf16[8,5,16,256]{3,2,1,0:T(8,128)(2,1)S(1)}, u32[]{:S(2)}, u32[]{:S(2)}) collective-permute-start(bf16[8,5,16,256]{3,2,1,0:T(8,128)(2,1)S(1)} %select_bitcast_fusion), channel_id=1, source_target_pairs={{0,8},{8,0},{16,24},{24,16},{32,40},{40,32},{48,56},{56,48},{64,72... | collective-permute-start | bytes 983048 | tf_op jit(solution)/shard_map/ppermute | solution.py:43
  9.9 5.7 %collective-permute-start.4 = (bf16[256,512]{1,0:T(8,128)(2,1)S(1)}, bf16[256,512]{1,0:T(8,128)(2,1)S(1)}, u32[]{:S(2)}, u32[]{:S(2)}) collective-permute-start(bf16[256,512]{1,0:T(8,128)(2,1)S(1)} %pad_maximum_fusion.1.refs_0_), channel_id=1, source_target_pairs={{0,7},{1,0},{2,1},{3,2},{4,3},{5,4},{6,5},{7,6},{8,15},{9,8},{10,9... | collective-permute-start | bytes 786440 | tf_op jit(solution)/shard_map/ppermute | solution.py:55
  15.7 4.3 %collective-permute-done.4.refs_3_.refs_4_ = bf16[256,512]{1,0:T(8,128)(2,1)S(1)} collective-permute-done((bf16[256,512]{1,0:T(8,128)(2,1)S(1)}, bf16[256,512]{1,0:T(8,128)(2,1)S(1)}, u32[]{:S(2)}, u32[]{:S(2)}) %collective-permute-start.4) | collective-permute-done | bytes 262176 | tf_op jit(solution)/shard_map/ppermute | solution.py:55
  20.0 3.1 %collective-permute-done.1.refs_2_.refs_1_ = bf16[256,512]{1,0:T(8,128)(2,1)S(1)} collective-permute-done((bf16[256,512]{1,0:T(8,128)(2,1)S(1)}, bf16[256,512]{1,0:T(8,128)(2,1)S(1)}, u32[]{:S(2)}, u32[]{:S(2)}) %collective-permute-start.1) | collective-permute-done | bytes 262176 | tf_op jit(solution)/shard_map/ppermute | solution.py:55
  23.8 2.8 %collective-permute-start.13 = (bf16[2,8,5,16,256]{4,3,2,1,0:T(8,128)(2,1)S(1)}, bf16[2,8,5,16,256]{4,3,2,1,0:T(8,128)(2,1)S(1)}, u32[]{:S(2)}, u32[]{:S(2)}) collective-permute-start(bf16[2,8,5,16,256]{4,3,2,1,0:T(8,128)(2,1)S(1)} %collective-permute-done.10.refs_0_.a.refs_10_), channel_id=1, source_target_pairs={{0,64},{8,200},{16,80},{24,216},{32,96},{40,232},{48,112},{56,248}... | collective-permute-start | bytes 1966088 | tf_op jit(solution)/shard_map/ppermute | solution.py:31
  28.1 4.4 %collective-permute-done.5.refs_2_.refs_5_ = bf16[256,512]{1,0:T(8,128)(2,1)S(1)} collective-permute-done((bf16[256,512]{1,0:T(8,128)(2,1)S(1)}, bf16[256,512]{1,0:T(8,128)(2,1)S(1)}, u32[]{:S(2)}, u32[]{:S(2)}) %collective-permute-start.5) | collective-permute-done | bytes 262176 | tf_op jit(solution)/shard_map/ppermute | solution.py:55
  35.4 3.6 %collective-permute-start.15 = (bf16[1,8,5,16,256]{4,3,2,1,0:T(8,128)(2,1)S(1)}, bf16[1,8,5,16,256]{4,3,2,1,0:T(8,128)(2,1)S(1)}, u32[]{:S(2)}, u32[]{:S(2)}) collective-permute-start(bf16[1,8,5,16,256]{4,3,2,1,0:T(8,128)(2,1)S(1)} %get-tuple-element.36), channel_id=1, source_target_pairs={{0,16},{8,56},{16,32},{24,8},{32,48},{40,24},{48,0},{56,40},{64,80... | collective-permute-start | bytes 983048 | tf_op jit(solution)/shard_map/ppermute | solution.py:31
  44.8 4.5 %collective-permute-done.16.refs_16_ = bf16[1,8,5,16,256]{4,3,2,1,0:T(8,128)(2,1)S(1)} collective-permute-done((bf16[1,8,5,16,256]{4,3,2,1,0:T(8,128)(2,1)S(1)}, bf16[1,8,5,16,256]{4,3,2,1,0:T(8,128)(2,1)S(1)}, u32[]{:S(2)}, u32[]{:S(2)}) %collective-permute-start.16) | collective-permute-done | bytes 327712 | tf_op jit(solution)/shard_map/ppermute | solution.py:31
  58.5 4.3 %forward.1 = (f32[256,2048]{1,0:T(8,128)S(1)}, bf16[256,1024]{1,0:T(8,128)(2,1)S(1)}, bf16[256,1024]{1,0:T(8,128)(2,1)S(1)}, bf16[64,1024]{1,0:T(8,128)(2,1)S(1)...) custom-call(s32[45]{0:T(128)S(1)} %concatenate.6.meta, ...), custom_call_target="tpu_custom_call" | custom-call | flops 1342177280 | bytes 7340032 | tf_op jit(solution)/shard_map/forward/pallas_call | solution.py:65
  69.4 3.9 %collective-permute-done.21.down = bf16[64,1024]{1,0:T(8,128)(2,1)S(1)} collective-permute-done((bf16[64,1024]{1,0:T(8,128)(2,1)S(1)}, bf16[64,1024]{1,0:T(8,128)(2,1)S(1)}, u32[]{:S(2)}, u32[]{:S(2)}) %collective-permute-start.21) | collective-permute-done | bytes 131104 | tf_op jit(solution)/shard_map/ppermute | solution.py:51
  73.4 3.8 %backward.2 = (bf16[4,21,16,256]{3,2,1,0:T(8,128)(2,1)S(1)}, bf16[4,21,16,256]{3,2,1,0:T(8,128)(2,1)S(1)}, bf16[4,21,16,256]{3,2,1,0:T(8,128)(2,1)S(1)}, bf16[4,...) custom-call(s32[45]{0:T(128)S(1)} %concatenate.6.meta, bf16[16,256,256]{2,1,0:T(8,128)(2,1)S(1)} %get-tuple-element.38.tok, ...), custom_call_target="tpu_custom_call" | custom-call | flops 671088640 | bytes 5578752 | tf_op jit(solution)/shard_map/backward/pallas_call | solution.py:65
  78.4 5.3 %collective-permute-start.26 = (bf16[4,21,16,256]{3,2,1,0:T(8,128)(2,1)S(1)}, bf16[4,21,16,256]{3,2,1,0:T(8,128)(2,1)S(1)}, u32[]{:S(2)}, u32[]{:S(2)}) collective-permute-start(bf16[4,21,16,256]{3,2,1,0:T(8,128)(2,1)S(1)} %get-tuple-element.51), channel_id=1, source_target_pairs={{0,192},{8,56},{16,208},{24,8},{32,224},{40,24},{48,240},{56,40},{... | collective-permute-start | bytes 2064392 | tf_op jit(solution)/shard_map/ppermute | solution.py:31
  86.4 2.8 %collective-permute-done.23.up = bf16[64,1024]{1,0:T(8,128)(2,1)S(1)} collective-permute-done((bf16[64,1024]{1,0:T(8,128)(2,1)S(1)}, bf16[64,1024]{1,0:T(8,128)(2,1)S(1)}, u32[]{:S(2)}, u32[]{:S(2)}) %collective-permute-start.23) | collective-permute-done | bytes 131104 | tf_op jit(solution)/shard_map/ppermute | solution.py:51
  89.2 3.5 %collective-permute-done.24.down = bf16[64,1024]{1,0:T(8,128)(2,1)S(1)} collective-permute-done((bf16[64,1024]{1,0:T(8,128)(2,1)S(1)}, bf16[64,1024]{1,0:T(8,128)(2,1)S(1)}, u32[]{:S(2)}, u32[]{:S(2)}) %collective-permute-start.24) | collective-permute-done | bytes 131104 | tf_op jit(solution)/shard_map/ppermute | solution.py:51
  92.7 4.9 %backward.3 = (bf16[4,21,16,256]{3,2,1,0:T(8,128)(2,1)S(1)}, bf16[4,21,16,256]{3,2,1,0:T(8,128)(2,1)}, bf16[4,21,16,256]{3,2,1,0:T(8,128)(2,1)}, bf16[4,21,16,25...) custom-call(s32[45]{0:T(128)S(1)} %concatenate.6.meta, bf16[16,256,256]{2,1,0:T(8,128)(2,1)S(1)} %get-tuple-element.38.tok, ...), custom_call_target="tpu_custom_call" | custom-call | flops 671088640 | bytes 5578752 | tf_op jit(solution)/shard_map/backward/pallas_call | solution.py:65
  99.1 3.9 %collective-permute-start.27 = (bf16[16,128,256]{2,1,0:T(8,128)(2,1)S(1)}, bf16[16,128,256]{2,1,0:T(8,128)(2,1)S(1)}, u32[]{:S(2)}, u32[]{:S(2)}) collective-permute-start(bf16[16,128,256]{2,1,0:T(8,128)(2,1)S(1)} %get-tuple-element.53), channel_id=1, source_target_pairs={{0,8},{8,0},{16,24},{24,16},{32,40},{40,32},{48,56},{56,48},{64,72... | collective-permute-start | bytes 3145736 | tf_op jit(solution)/shard_map/ppermute | solution.py:43
  102.9 2.8 %collective-permute-start.29 = (bf16[4,21,16,256]{3,2,1,0:T(8,128)(2,1)}, bf16[4,21,16,256]{3,2,1,0:T(8,128)(2,1)S(1)}, u32[]{:S(2)}, u32[]{:S(2)}) collective-permute-start(bf16[4,21,16,256]{3,2,1,0:T(8,128)(2,1)} %get-tuple-element.56), channel_id=1, source_target_pairs={{0,64},{8,24},{16,80},{24,40},{32,96},{40,56},{48,112},{56,8},{64,... | collective-permute-start | bytes 2064392 | tf_op jit(solution)/shard_map/ppermute | solution.py:31
  109.3 3.6 %all-to-all-start = ((bf16[16,128,256]{2,1,0:T(8,128)(2,1)}), bf16[16,128,256]{2,1,0:T(8,128)(2,1)S(1)}, u32[]{:S(2)}, u32[]{:S(2)}) async-start(bf16[16,128,256]{2,1,0:T(8,128)(2,1)} %broadcast_select_fusion.refs_1_), calls=%async_computation | async-start | bytes 2097152 | tf_op jit(solution)/shard_map/all_to_all | solution.py:433
  112.9 4.0 %collective-permute-done.29.refs_0_.refs_4_ = bf16[4,21,16,256]{3,2,1,0:T(8,128)(2,1)S(1)} collective-permute-done((bf16[4,21,16,256]{3,2,1,0:T(8,128)(2,1)}, bf16[4,21,16,256]{3,2,1,0:T(8,128)(2,1)S(1)}, u32[]{:S(2)}, u32[]{:S(2)}) %collective-permute-start.29) | collective-permute-done | bytes 688160 | tf_op jit(solution)/shard_map/ppermute | solution.py:31
  119.5 2.8 %collective-permute-start.31 = (bf16[4,22,16,256]{3,2,1,0:T(8,128)(2,1)S(1)}, bf16[4,22,16,256]{3,2,1,0:T(8,128)(2,1)S(1)}, u32[]{:S(2)}, u32[]{:S(2)}) collective-permute-start(bf16[4,22,16,256]{3,2,1,0:T(8,128)(2,1)S(1)} %relay.3), channel_id=1, source_target_pairs={{0,192},{8,56},{16,208},{24,8},{32,224},{40,24},{48,240},{56,40},{... | collective-permute-start | bytes 2162696 | tf_op jit(solution)/shard_map/ppermute | solution.py:31
  124.7 5.8 %collective-permute-done.31.refs_5_ = bf16[4,22,16,256]{3,2,1,0:T(8,128)(2,1)S(1)} collective-permute-done((bf16[4,22,16,256]{3,2,1,0:T(8,128)(2,1)S(1)}, bf16[4,22,16,256]{3,2,1,0:T(8,128)(2,1)S(1)}, u32[]{:S(2)}, u32[]{:S(2)}) %collective-permute-start.31) | collective-permute-done | bytes 720928 | tf_op jit(solution)/shard_map/ppermute | solution.py:31
  135.4 4.4 %collective-permute-done.32.prev = bf16[8,6,16,256]{3,2,1,0:T(8,128)(2,1)S(1)} collective-permute-done((bf16[8,6,16,256]{3,2,1,0:T(8,128)(2,1)S(1)}, bf16[8,6,16,256]{3,2,1,0:T(8,128)(2,1)S(1)}, u32[]{:S(2)}, u32[]{:S(2)}) %collective-permute-start.32) | collective-permute-done | bytes 393248 | tf_op jit(solution)/shard_map/ppermute | solution.py:31
  139.8 3.5 %collective-permute-done.33.nxt = bf16[8,6,16,256]{3,2,1,0:T(8,128)(2,1)S(1)} collective-permute-done((bf16[8,6,16,256]{3,2,1,0:T(8,128)(2,1)S(1)}, bf16[8,6,16,256]{3,2,1,0:T(8,128)(2,1)S(1)}, u32[]{:S(2)}, u32[]{:S(2)}) %collective-permute-start.33) | collective-permute-done | bytes 393248 | tf_op jit(solution)/shard_map/ppermute | solution.py:31
  145.9 3.3 %collective-permute-start.35 = (bf16[8,7,8,256]{3,2,1,0:T(8,128)(2,1)S(1)}, bf16[8,7,8,256]{3,2,1,0:T(8,128)(2,1)S(1)}, u32[]{:S(2)}, u32[]{:S(2)}) collective-permute-start(bf16[8,7,8,256]{3,2,1,0:T(8,128)(2,1)S(1)} %get-tuple-element.64), channel_id=1, source_target_pairs={{0,8},{8,0},{16,24},{24,16},{32,40},{40,32},{48,56},{56,48},{64,72... | collective-permute-start | bytes 688136 | tf_op jit(solution)/shard_map/ppermute | solution.py:43
  (91 shorter events, 57.8 us)
Async XLA Ops:
  7.7 15.5 %collective-permute-start.11 = (bf16[2,8,5,16,256]{4,3,2,1,0:T(8,128)(2,1)S(1)}, bf16[2,8,5,16,256]{4,3,2,1,0:T(8,128)(2,1)S(1)}, u32[]{:S(2)}, u32[]{:S(2)}) collective-permute-start(bf16[2,8,5,16,256]{4,3,2,1,0:T(8,128)(2,1)S(1)} %pad_maximum_fusion.src.refs_9_), channel_id=1, source_target_pairs={{0,192},{8,72},{16,208},{24,88},{32,224},{40,104},{48,240},{56,120... | collective-permute-start | bytes 1966088 | tf_op jit(solution)/shard_map/ppermute | solution.py:31
  7.8 15.4 %collective-permute-start.10 = (bf16[2,8,5,16,256]{4,3,2,1,0:T(8,128)(2,1)S(1)}, bf16[2,8,5,16,256]{4,3,2,1,0:T(8,128)(2,1)S(1)}, u32[]{:S(2)}, u32[]{:S(2)}) collective-permute-start(bf16[2,8,5,16,256]{4,3,2,1,0:T(8,128)(2,1)S(1)} %pad_maximum_fusion.src.refs_9_), channel_id=1, source_target_pairs={{0,16},{8,56},{16,32},{24,8},{32,48},{40,24},{48,0},{56,40},{64,80... | collective-permute-start | bytes 1966088 | tf_op jit(solution)/shard_map/ppermute | solution.py:31
  9.9 10.1 %collective-permute-start.4 = (bf16[256,512]{1,0:T(8,128)(2,1)S(1)}, bf16[256,512]{1,0:T(8,128)(2,1)S(1)}, u32[]{:S(2)}, u32[]{:S(2)}) collective-permute-start(bf16[256,512]{1,0:T(8,128)(2,1)S(1)} %pad_maximum_fusion.1.refs_0_), channel_id=1, source_target_pairs={{0,7},{1,0},{2,1},{3,2},{4,3},{5,4},{6,5},{7,6},{8,15},{9,8},{10,9... | collective-permute-start | bytes 786440 | tf_op jit(solution)/shard_map/ppermute | solution.py:55
  23.7 11.0 %collective-permute-start.12 = (bf16[2,8,5,16,256]{4,3,2,1,0:T(8,128)(2,1)S(1)}, bf16[2,8,5,16,256]{4,3,2,1,0:T(8,128)(2,1)S(1)}, u32[]{:S(2)}, u32[]{:S(2)}) collective-permute-start(bf16[2,8,5,16,256]{4,3,2,1,0:T(8,128)(2,1)S(1)} %hold.1), channel_id=1, source_target_pairs={{0,48},{8,24},{16,0},{24,40},{32,16},{40,56},{48,32},{56,8},{64,11... | collective-permute-start | bytes 1966088 | tf_op jit(solution)/shard_map/ppermute | solution.py:31
  23.8 10.9 %collective-permute-start.13 = (bf16[2,8,5,16,256]{4,3,2,1,0:T(8,128)(2,1)S(1)}, bf16[2,8,5,16,256]{4,3,2,1,0:T(8,128)(2,1)S(1)}, u32[]{:S(2)}, u32[]{:S(2)}) collective-permute-start(bf16[2,8,5,16,256]{4,3,2,1,0:T(8,128)(2,1)S(1)} %collective-permute-done.10.refs_0_.a.refs_10_), channel_id=1, source_target_pairs={{0,64},{8,200},{16,80},{24,216},{32,96},{40,232},{48,112},{56,248}... | collective-permute-start | bytes 1966088 | tf_op jit(solution)/shard_map/ppermute | solution.py:31
  39.0 17.4 %collective-permute-start.14 = (bf16[2,8,5,16,256]{4,3,2,1,0:T(8,128)(2,1)S(1)}, bf16[2,8,5,16,256]{4,3,2,1,0:T(8,128)(2,1)S(1)}, u32[]{:S(2)}, u32[]{:S(2)}) collective-permute-start(bf16[2,8,5,16,256]{4,3,2,1,0:T(8,128)(2,1)S(1)} %collective-permute-done.12.c.refs_12_), channel_id=1, source_target_pairs={{0,192},{8,72},{16,208},{24,88},{32,224},{40,104},{48,240},{56,120... | collective-permute-start | bytes 1966088 | tf_op jit(solution)/shard_map/ppermute | solution.py:31
  39.1 10.2 %collective-permute-start.16 = (bf16[1,8,5,16,256]{4,3,2,1,0:T(8,128)(2,1)S(1)}, bf16[1,8,5,16,256]{4,3,2,1,0:T(8,128)(2,1)S(1)}, u32[]{:S(2)}, u32[]{:S(2)}) collective-permute-start(bf16[1,8,5,16,256]{4,3,2,1,0:T(8,128)(2,1)S(1)} %get-tuple-element.37), channel_id=1, source_target_pairs={{0,48},{8,24},{16,0},{24,40},{32,16},{40,56},{48,32},{56,8},{64,11... | collective-permute-start | bytes 983048 | tf_op jit(solution)/shard_map/ppermute | solution.py:31
  39.1 11.5 %collective-permute-start.6 = (bf16[256,512]{1,0:T(8,128)(2,1)S(1)}, bf16[256,512]{1,0:T(8,128)(2,1)S(1)}, u32[]{:S(2)}, u32[]{:S(2)}) collective-permute-start(bf16[256,512]{1,0:T(8,128)(2,1)S(1)} %collective-permute-done.5.refs_2_.refs_5_), channel_id=1, source_target_pairs={{0,7},{1,0},{2,1},{3,2},{4,3},{5,4},{6,5},{7,6},{8,15},{9,8},{10,9... | collective-permute-start | bytes 786440 | tf_op jit(solution)/shard_map/ppermute | solution.py:55
  39.3 11.7 %collective-permute-start.3 = (bf16[256,512]{1,0:T(8,128)(2,1)S(1)}, bf16[256,512]{1,0:T(8,128)(2,1)S(1)}, u32[]{:S(2)}, u32[]{:S(2)}) collective-permute-start(bf16[256,512]{1,0:T(8,128)(2,1)S(1)} %collective-permute-done.2.refs_1_.refs_2_), channel_id=1, source_target_pairs={{0,1},{1,2},{2,3},{3,4},{4,5},{5,6},{6,7},{7,0},{8,9},{9,10},{10,1... | collective-permute-start | bytes 786440 | tf_op jit(solution)/shard_map/ppermute | solution.py:55
  43.0 13.4 %collective-permute-start.17 = (bf16[1,8,5,16,256]{4,3,2,1,0:T(8,128)(2,1)S(1)}, bf16[1,8,5,16,256]{4,3,2,1,0:T(8,128)(2,1)S(1)}, u32[]{:S(2)}, u32[]{:S(2)}) collective-permute-start(bf16[1,8,5,16,256]{4,3,2,1,0:T(8,128)(2,1)S(1)} %collective-permute-done.15.refs_15_), channel_id=1, source_target_pairs={{0,64},{8,200},{16,80},{24,216},{32,96},{40,232},{48,112},{56,248}... | collective-permute-start | bytes 983048 | tf_op jit(solution)/shard_map/ppermute | solution.py:31
  49.3 9.3 %collective-permute-start.18 = (bf16[1,8,5,16,256]{4,3,2,1,0:T(8,128)(2,1)S(1)}, bf16[1,8,5,16,256]{4,3,2,1,0:T(8,128)(2,1)S(1)}, u32[]{:S(2)}, u32[]{:S(2)}) collective-permute-start(bf16[1,8,5,16,256]{4,3,2,1,0:T(8,128)(2,1)S(1)} %collective-permute-done.16.refs_16_), channel_id=1, source_target_pairs={{0,192},{8,72},{16,208},{24,88},{32,224},{40,104},{48,240},{56,120... | collective-permute-start | bytes 983048 | tf_op jit(solution)/shard_map/ppermute | solution.py:31
  62.8 10.6 %collective-permute-start.19 = (bf16[256,1024]{1,0:T(8,128)(2,1)S(1)}, bf16[256,1024]{1,0:T(8,128)(2,1)S(1)}, u32[]{:S(2)}, u32[]{:S(2)}) collective-permute-start(bf16[256,1024]{1,0:T(8,128)(2,1)S(1)} %get-tuple-element.39.mine), channel_id=1, source_target_pairs={{0,8},{8,0},{16,24},{24,16},{32,40},{40,32},{48,56},{56,48},{64,72... | collective-permute-start | bytes 1572872 | tf_op jit(solution)/shard_map/ppermute | solution.py:43
  78.1 19.6 %collective-permute-start.25 = (bf16[4,21,16,256]{3,2,1,0:T(8,128)(2,1)S(1)}, bf16[4,21,16,256]{3,2,1,0:T(8,128)(2,1)S(1)}, u32[]{:S(2)}, u32[]{:S(2)}) collective-permute-start(bf16[4,21,16,256]{3,2,1,0:T(8,128)(2,1)S(1)} %get-tuple-element.50), channel_id=1, source_target_pairs={{0,64},{8,24},{16,80},{24,40},{32,96},{40,56},{48,112},{56,8},{64,... | collective-permute-start | bytes 2064392 | tf_op jit(solution)/shard_map/ppermute | solution.py:31
  78.4 19.2 %collective-permute-start.26 = (bf16[4,21,16,256]{3,2,1,0:T(8,128)(2,1)S(1)}, bf16[4,21,16,256]{3,2,1,0:T(8,128)(2,1)S(1)}, u32[]{:S(2)}, u32[]{:S(2)}) collective-permute-start(bf16[4,21,16,256]{3,2,1,0:T(8,128)(2,1)S(1)} %get-tuple-element.51), channel_id=1, source_target_pairs={{0,192},{8,56},{16,208},{24,8},{32,224},{40,24},{48,240},{56,40},{... | collective-permute-start | bytes 2064392 | tf_op jit(solution)/shard_map/ppermute | solution.py:31
  83.8 8.9 %collective-permute-start.22 = (bf16[256,1024]{1,0:T(8,128)(2,1)S(1)}, bf16[256,1024]{1,0:T(8,128)(2,1)S(1)}, u32[]{:S(2)}, u32[]{:S(2)}) collective-permute-start(bf16[256,1024]{1,0:T(8,128)(2,1)S(1)} %get-tuple-element.44.mine), channel_id=1, source_target_pairs={{0,8},{8,0},{16,24},{24,16},{32,40},{40,32},{48,56},{56,48},{64,72... | collective-permute-start | bytes 1572872 | tf_op jit(solution)/shard_map/ppermute | solution.py:43
  99.1 9.1 %collective-permute-start.27 = (bf16[16,128,256]{2,1,0:T(8,128)(2,1)S(1)}, bf16[16,128,256]{2,1,0:T(8,128)(2,1)S(1)}, u32[]{:S(2)}, u32[]{:S(2)}) collective-permute-start(bf16[16,128,256]{2,1,0:T(8,128)(2,1)S(1)} %get-tuple-element.53), channel_id=1, source_target_pairs={{0,8},{8,0},{16,24},{24,16},{32,40},{40,32},{48,56},{56,48},{64,72... | collective-permute-start | bytes 3145736 | tf_op jit(solution)/shard_map/ppermute | solution.py:43
  102.9 14.0 %collective-permute-start.29 = (bf16[4,21,16,256]{3,2,1,0:T(8,128)(2,1)}, bf16[4,21,16,256]{3,2,1,0:T(8,128)(2,1)S(1)}, u32[]{:S(2)}, u32[]{:S(2)}) collective-permute-start(bf16[4,21,16,256]{3,2,1,0:T(8,128)(2,1)} %get-tuple-element.56), channel_id=1, source_target_pairs={{0,64},{8,24},{16,80},{24,40},{32,96},{40,56},{48,112},{56,8},{64,... | collective-permute-start | bytes 2064392 | tf_op jit(solution)/shard_map/ppermute | solution.py:31
  105.7 11.2 %collective-permute-start.30 = (bf16[4,21,16,256]{3,2,1,0:T(8,128)(2,1)}, bf16[4,21,16,256]{3,2,1,0:T(8,128)(2,1)}, u32[]{:S(2)}, u32[]{:S(2)}) collective-permute-start(bf16[4,21,16,256]{3,2,1,0:T(8,128)(2,1)} %get-tuple-element.58), channel_id=1, source_target_pairs={{0,192},{8,56},{16,208},{24,8},{32,224},{40,24},{48,240},{56,40},{... | collective-permute-start | bytes 2064392 | tf_op jit(solution)/shard_map/ppermute | solution.py:31
  109.3 39.8 %all-to-all-start = ((bf16[16,128,256]{2,1,0:T(8,128)(2,1)}), bf16[16,128,256]{2,1,0:T(8,128)(2,1)S(1)}, u32[]{:S(2)}, u32[]{:S(2)}) async-start(bf16[16,128,256]{2,1,0:T(8,128)(2,1)} %broadcast_select_fusion.refs_1_), calls=%async_computation | async-start | bytes 2097152 | tf_op jit(solution)/shard_map/all_to_all | solution.py:433
  112.8 11.9 %collective-permute-start.28 = (bf16[4,22,16,256]{3,2,1,0:T(8,128)(2,1)S(1)}, bf16[4,22,16,256]{3,2,1,0:T(8,128)(2,1)S(1)}, u32[]{:S(2)}, u32[]{:S(2)}) collective-permute-start(bf16[4,22,16,256]{3,2,1,0:T(8,128)(2,1)S(1)} %relay.2._), channel_id=1, source_target_pairs={{0,64},{8,24},{16,80},{24,40},{32,96},{40,56},{48,112},{56,8},{64,... | collective-permute-start | bytes 2162696 | tf_op jit(solution)/shard_map/ppermute | solution.py:31
  119.5 11.0 %collective-permute-start.31 = (bf16[4,22,16,256]{3,2,1,0:T(8,128)(2,1)S(1)}, bf16[4,22,16,256]{3,2,1,0:T(8,128)(2,1)S(1)}, u32[]{:S(2)}, u32[]{:S(2)}) collective-permute-start(bf16[4,22,16,256]{3,2,1,0:T(8,128)(2,1)S(1)} %relay.3), channel_id=1, source_target_pairs={{0,192},{8,56},{16,208},{24,8},{32,224},{40,24},{48,240},{56,40},{... | collective-permute-start | bytes 2162696 | tf_op jit(solution)/shard_map/ppermute | solution.py:31
  131.6 8.2 %collective-permute-start.32 = (bf16[8,6,16,256]{3,2,1,0:T(8,128)(2,1)S(1)}, bf16[8,6,16,256]{3,2,1,0:T(8,128)(2,1)S(1)}, u32[]{:S(2)}, u32[]{:S(2)}) collective-permute-start(bf16[8,6,16,256]{3,2,1,0:T(8,128)(2,1)S(1)} %get-tuple-element.60), channel_id=1, source_target_pairs={{0,16},{8,72},{16,32},{24,88},{32,48},{40,104},{48,0},{56,120},{64... | collective-permute-start | bytes 1179656 | tf_op jit(solution)/shard_map/ppermute | solution.py:31
  132.6 10.7 %collective-permute-start.33 = (bf16[8,6,16,256]{3,2,1,0:T(8,128)(2,1)S(1)}, bf16[8,6,16,256]{3,2,1,0:T(8,128)(2,1)S(1)}, u32[]{:S(2)}, u32[]{:S(2)}) collective-permute-start(bf16[8,6,16,256]{3,2,1,0:T(8,128)(2,1)S(1)} %get-tuple-element.61), channel_id=1, source_target_pairs={{0,48},{8,200},{16,0},{24,216},{32,16},{40,232},{48,32},{56,248},{... | collective-permute-start | bytes 1179656 | tf_op jit(solution)/shard_map/ppermute | solution.py:31
  134.3 10.7 %collective-permute-start.34 = (bf16[8,6,16,256]{3,2,1,0:T(8,128)(2,1)S(1)}, bf16[8,6,16,256]{3,2,1,0:T(8,128)(2,1)S(1)}, u32[]{:S(2)}, u32[]{:S(2)}) collective-permute-start(bf16[8,6,16,256]{3,2,1,0:T(8,128)(2,1)S(1)} %get-tuple-element.62), channel_id=1, source_target_pairs={{0,32},{8,136},{16,48},{24,152},{32,0},{40,168},{48,16},{56,184},{... | collective-permute-start | bytes 1179656 | tf_op jit(solution)/shard_map/ppermute | solution.py:31
  (22 other events, 136.4 us)

commit v3 on v1

--- a/solution.py
+++ b/solution.py
@@ -12,7 +12,7 @@
 F32, BF16 = jnp.float32, jnp.bfloat16
 NX, NY, NZ = 4, 4, 8
 COLS, NNZ, BS, PW = 8, 5, 256, 64
-TOK, KERN, SPLIT = 256, 20, 4
+TOK, KERN = 256, 20
 CORE, XPOS, YPOS, YLO, ZPOS = 40, 41, 42, 43, 44
 HBM = pl.BlockSpec(memory_space=pltpu.MemorySpace.HBM)
 VMEM = pl.BlockSpec(memory_space=pltpu.VMEM)
@@ -190,7 +190,7 @@
 
 
 def backward_kernel(meta, tok, got, mine, up, down, pre, taps, *refs):
-    g0, m1, m3, g1, g3, pgrad, conv, lhs, res, slab, moved = refs
+    *outs, pgrad, conv, lhs, res, slab, moved = refs
     core, x, y = meta[CORE], meta[XPOS], meta[YPOS]
     is_in = core == 0
     slab[...] = jnp.zeros_like(slab)
@@ -241,31 +241,16 @@
             rows = jnp.concatenate(sums + [jnp.zeros((7, BS), F32)], axis=0) * loss_scale
             slab[...] = rows.astype(BF16)
 
-        def emit(out, d, at):
+        for d, out in enumerate(outs):
             start = (here + d) % 4 * far
             for k in range(NNZ):
                 for s in range(4):
-                    out[at, k * 4 + s] = res[k, start + s * near]
-            out[at, KERN] = slab[...]
-
-        emit(g0, 0, c)
-
-        @pl.when(c < SPLIT)
-        def _():
-            emit(m1, 2, c)
-            emit(g1, 1, c)
-            emit(m3, 3, c + SPLIT)
-
-        @pl.when(c >= SPLIT)
-        def _():
-            emit(m3, 2, c - SPLIT)
-            emit(m1, 1, c)
-            emit(g3, 3, c - SPLIT)
+                    out[c, k * 4 + s] = res[k, start + s * near]
+            out[c, KERN] = slab[...]
 
 
 def backward(meta, tok, got, mine, up, down, pre, taps):
-    full, part = (COLS, KERN + 1, 16, BS), (SPLIT, KERN + 1, 16, BS)
-    outs = [(full, BF16)] * 3 + [(part, BF16)] * 2 + [((TOK, COLS * BS), BF16)]
+    outs = [((COLS, KERN + 1, 16, BS), BF16)] * 4 + [((TOK, COLS * BS), BF16)]
     scratch = [
         pltpu.VMEM((TOK, BS), F32),
         pltpu.VMEM((TOK, BS), BF16),
@@ -307,7 +292,8 @@
     )
 
 
-def gather_sum_kernel(meta, parts, out):
+def gather_sum_kernel(meta, parts, out, flag):
+    flag[...] = jnp.zeros_like(flag)
     for b in range(2):
         total = parts[b].astype(F32)
         for z in range(1, NZ):
@@ -315,33 +301,22 @@
         out[:, b * BS : (b + 1) * BS] = total.astype(BF16)
 
 
-def relay_kernel(meta, g1, g3, m1, m3, _, o1, o3):
-    for out, own, got in ((o1, g1, m1), (o3, g3, m3)):
-
-        @pl.loop(0, SPLIT)
-        def _(c):
-            for k in range(KERN):
-                out[c, k] = (own[c, k].astype(F32) + got[c, k].astype(F32)).astype(BF16)
-            out[c, KERN] = own[c, KERN]
-            out[c, KERN + 1] = got[c, KERN]
-
-
-def first_sum_kernel(meta, own, m1, m3, p1, p3, *outs):
+def first_sum_kernel(meta, own, prev, nxt, far, *refs):
+    outs = refs[-4:]
     here = jnp.where(meta[CORE] == 0, meta[XPOS], meta[YPOS])
 
-    for shift, relayed, direct in ((0, p1, m3), (SPLIT, p3, m1)):
-
-        @pl.loop(0, SPLIT)
-        def _(c):
-            at, got = c + shift, c + SPLIT
-            near = relayed[c, KERN].astype(F32) + direct[got, KERN].astype(F32)
-            far = own[at, KERN].astype(F32) + relayed[c, KERN + 1].astype(F32)
-            for d in range(4):
-                s = (here + d) % 4
-                for k in range(NNZ):
-                    total = own[at, k * 4 + s].astype(F32) + relayed[c, k * 4 + s].astype(F32)
-                    outs[d][at, k] = (total + direct[got, k * 4 + s].astype(F32)).astype(BF16)
-                outs[d][at, NNZ] = (far + near).astype(BF16)
+    def total(c, at):
+        a, b, e, f = (r[c, at].astype(F32) for r in (own, prev, nxt, far))
+        return ((a + f) + (b + e)).astype(BF16)
+
+    @pl.loop(0, COLS)
+    def _(c):
+        for d in range(4):
+            for k in range(NNZ):
+                outs[d][c, k] = total(c, k * 4 + (here + d) % 4)
+        slab = total(c, KERN)
+        for out in outs:
+            out[c, NNZ] = slab
 
 
 def second_sum_kernel(meta, own, prev, nxt, far, keep, send):
@@ -414,21 +389,21 @@
     pre, out, top, bot, wts, tok = forward(meta, token_pieces, pieces)
     got = to_partner(out)
     up, down = to_next_chip(bot, 1), to_next_chip(top, -1)
-    g0, m1, m3, g1, g3, pgrad = backward(meta, tok, got, out, up, down, pre, mix_kernel)
-    m1, m3 = first(m1, 1), first(m3, -1)
+    *g, pgrad = backward(meta, tok, got, out, up, down, pre, mix_kernel)
+    parts = (g[0], first(g[1], 1), first(g[3], -1), first(g[2], 2))
 
     keep, send = token_grad(meta, pgrad, wts)
     terms = jnp.where(is_in, keep, to_partner(send))
-    relayed = [((SPLIT, KERN + 2, 16, BS), BF16)] * 2
-    r1, r3 = local(relay_kernel, "relay", relayed, (meta, g1, g3, m1, m3, terms), hbm=(5,))
-    terms = lax.all_to_all(terms, "hid", 0, 0, tiled=True)
-    (grad_tokens,) = local(gather_sum_kernel, "gathersum", [((128, 512), BF16)], (meta, terms))
+    shares = lax.all_to_all(terms, "hid", 0, 0, tiled=True)
+    outs = [((128, 512), BF16), ((8, 128), F32)]
+    grad_tokens, flag = local(gather_sum_kernel, "gathersum", outs, (meta, shares))
 
     h = local(
         first_sum_kernel,
         "firstsum",
         [((COLS, NNZ + 1, 16, BS), BF16)] * 4,
-        (meta, g0, m1, m3, first(r1, 1), first(r3, -1)),
+        (meta, *parts, terms),
+        hbm=(5,),
     )
     last = (h[0], second(h[1], 1), second(h[3], -1), second(h[2], 2))
     shape = ((COLS, NNZ + 2, 8, BS), BF16)
@@ -438,7 +413,7 @@
         place_kernel,
         "place",
         [out_shape, out_shape, ((9, 8 * BS), F32)],
-        (meta, kept, to_partner(sent), grad_tokens),
+        (meta, kept, to_partner(sent), flag),
     )
     grad_tokens = grad_tokens.reshape(1, 2, PW, 512)
     return grad_tokens, win.transpose(0, 2, 1, 3), wout.transpose(0, 2, 1, 3), kern

time: 148 us -> 148 us (level)
  waiting for transfers between devices: 64.4 us -> 70.6 us
  starting transfers between devices: 54.6 us -> 50.5 us
  local copies, waits for them, and re-layouts: 3.63 us -> 0.2 us
    ppermute x16 -> x15, waiting for transfers between devices: 38.5 us -> 44.8 us  [by_core(): return lax.ppermute(value, ('crop', 'rows'), pairs)]
    unnamed x18 -> x8, local copies, waits for them, and re-layouts: 3.44 us -> 0.02 us
    ppermute x5, starting transfers between devices: 12.8 us -> 11 us  [to_partner(): return lax.ppermute(value, 'rows', [(r, r ^ 1) for r in range(16)])]
    ppermute x16 -> x15, starting transfers between devices: 24.7 us -> 23.1 us  [by_core(): return lax.ppermute(value, ('crop', 'rows'), pairs)]
    pallas_call x10 -> x9, Pallas kernels: 21.1 us -> 21.8 us  [local(): pl.pallas_call(kernel, out_shape=shapes, in_specs=[SMEM] + [HBM if i in h...]
  transfers between devices with their start and end apart: 32 -> 31, of which waited for: 16 -> 17; matrix products, arithmetic and copies ran while one was open for 2% -> 2% of each run, Pallas kernels for 3% -> 3%
where the time goes in v3:
time: 148 us
  waiting for transfers between devices  70.6 us (48%)
  starting transfers between devices  50.5 us (34%)
  Pallas kernels  21.8 us (15%)
  other arithmetic  3.58 us (2%)
    ppermute x15, waiting for transfers between devices, by_core(): return lax.ppermute(value, ('crop', 'rows'), pairs)  44.8 us
    ppermute x15, starting transfers between devices, by_core(): return lax.ppermute(value, ('crop', 'rows'), pairs)  23.1 us
    pallas_call x9, Pallas kernels, local(): pl.pallas_call(kernel, out_shape=shapes, in_specs=[SMEM] + [HBM if i in h...  21.8 us
    ppermute x8, waiting for transfers between devices, along_z(): return lax.ppermute(value, 'hid', [(z, (z + step) % NZ) for z in range(NZ)])  17.1 us
    ppermute x5, starting transfers between devices, to_partner(): return lax.ppermute(value, 'rows', [(r, r ^ 1) for r in range(16)])  11 us
    ppermute x8, starting transfers between devices, along_z(): return lax.ppermute(value, 'hid', [(z, (z + step) % NZ) for z in range(NZ)])  10.2 us
    ppermute x2, waiting for transfers between devices, to_next_chip(): return lax.ppermute(value, 'rows', pairs)  8.54 us
    all_to_all x1, starting transfers between devices, on_device(): shares = lax.all_to_all(terms, 'hid', 0, 0, tiled=True)  3.56 us
  transfers between devices with their start and end apart: 31, of which 17 were waited for; matrix products, arithmetic and copies ran while one was open for 2% of the time, Pallas kernels for 3%

profile of v3, /device:TPU:1, one launch (start us, length us, event | category | flops | bytes accessed | tf_op | source)
XLA Modules:
  0.0 147.5 jit_solution(13720523305594209551)
XLA Ops:
  1.9 3.3 %collective-permute-start.9 = (bf16[8,5,16,256]{3,2,1,0:T(8,128)(2,1)S(1)}, bf16[8,5,16,256]{3,2,1,0:T(8,128)(2,1)S(1)}, u32[]{:S(2)}, u32[]{:S(2)}) collective-permute-start(bf16[8,5,16,256]{3,2,1,0:T(8,128)(2,1)S(1)} %select_bitcast_fusion), channel_id=1, source_target_pairs={{0,8},{8,0},{16,24},{24,16},{32,40},{40,32},{48,56},{56,48},{64,72... | collective-permute-start | bytes 983048 | tf_op jit(solution)/shard_map/ppermute | solution.py:41
  8.9 5.7 %collective-permute-start.4 = (bf16[256,512]{1,0:T(8,128)(2,1)S(1)}, bf16[256,512]{1,0:T(8,128)(2,1)S(1)}, u32[]{:S(2)}, u32[]{:S(2)}) collective-permute-start(bf16[256,512]{1,0:T(8,128)(2,1)S(1)} %pad_maximum_fusion.1.refs_0_), channel_id=1, source_target_pairs={{0,7},{1,0},{2,1},{3,2},{4,3},{5,4},{6,5},{7,6},{8,15},{9,8},{10,9... | collective-permute-start | bytes 786440 | tf_op jit(solution)/shard_map/ppermute | solution.py:53
  14.7 4.3 %collective-permute-done.4.refs_3_.refs_4_ = bf16[256,512]{1,0:T(8,128)(2,1)S(1)} collective-permute-done((bf16[256,512]{1,0:T(8,128)(2,1)S(1)}, bf16[256,512]{1,0:T(8,128)(2,1)S(1)}, u32[]{:S(2)}, u32[]{:S(2)}) %collective-permute-start.4) | collective-permute-done | bytes 262176 | tf_op jit(solution)/shard_map/ppermute | solution.py:53
  19.0 3.1 %collective-permute-done.1.refs_2_.refs_1_ = bf16[256,512]{1,0:T(8,128)(2,1)S(1)} collective-permute-done((bf16[256,512]{1,0:T(8,128)(2,1)S(1)}, bf16[256,512]{1,0:T(8,128)(2,1)S(1)}, u32[]{:S(2)}, u32[]{:S(2)}) %collective-permute-start.1) | collective-permute-done | bytes 262176 | tf_op jit(solution)/shard_map/ppermute | solution.py:53
  22.9 2.8 %collective-permute-start.13 = (bf16[2,8,5,16,256]{4,3,2,1,0:T(8,128)(2,1)S(1)}, bf16[2,8,5,16,256]{4,3,2,1,0:T(8,128)(2,1)S(1)}, u32[]{:S(2)}, u32[]{:S(2)}) collective-permute-start(bf16[2,8,5,16,256]{4,3,2,1,0:T(8,128)(2,1)S(1)} %collective-permute-done.10.refs_0_.a.refs_10_), channel_id=1, source_target_pairs={{0,64},{8,200},{16,80},{24,216},{32,96},{40,232},{48,112},{56,248}... | collective-permute-start | bytes 1966088 | tf_op jit(solution)/shard_map/ppermute | solution.py:29
  27.1 4.4 %collective-permute-done.5.refs_2_.refs_5_ = bf16[256,512]{1,0:T(8,128)(2,1)S(1)} collective-permute-done((bf16[256,512]{1,0:T(8,128)(2,1)S(1)}, bf16[256,512]{1,0:T(8,128)(2,1)S(1)}, u32[]{:S(2)}, u32[]{:S(2)}) %collective-permute-start.5) | collective-permute-done | bytes 262176 | tf_op jit(solution)/shard_map/ppermute | solution.py:53
  34.4 3.6 %collective-permute-start.15 = (bf16[1,8,5,16,256]{4,3,2,1,0:T(8,128)(2,1)S(1)}, bf16[1,8,5,16,256]{4,3,2,1,0:T(8,128)(2,1)S(1)}, u32[]{:S(2)}, u32[]{:S(2)}) collective-permute-start(bf16[1,8,5,16,256]{4,3,2,1,0:T(8,128)(2,1)S(1)} %get-tuple-element.30), channel_id=1, source_target_pairs={{0,16},{8,56},{16,32},{24,8},{32,48},{40,24},{48,0},{56,40},{64,80... | collective-permute-start | bytes 983048 | tf_op jit(solution)/shard_map/ppermute | solution.py:29
  39.6 2.4 %collective-permute-done.15.refs_15_ = bf16[1,8,5,16,256]{4,3,2,1,0:T(8,128)(2,1)S(1)} collective-permute-done((bf16[1,8,5,16,256]{4,3,2,1,0:T(8,128)(2,1)S(1)}, bf16[1,8,5,16,256]{4,3,2,1,0:T(8,128)(2,1)S(1)}, u32[]{:S(2)}, u32[]{:S(2)}) %collective-permute-start.15) | collective-permute-done | bytes 327712 | tf_op jit(solution)/shard_map/ppermute | solution.py:29
  43.8 4.5 %collective-permute-done.16.refs_16_ = bf16[1,8,5,16,256]{4,3,2,1,0:T(8,128)(2,1)S(1)} collective-permute-done((bf16[1,8,5,16,256]{4,3,2,1,0:T(8,128)(2,1)S(1)}, bf16[1,8,5,16,256]{4,3,2,1,0:T(8,128)(2,1)S(1)}, u32[]{:S(2)}, u32[]{:S(2)}) %collective-permute-start.16) | collective-permute-done | bytes 327712 | tf_op jit(solution)/shard_map/ppermute | solution.py:29
  51.3 2.5 %collective-permute-done.8.refs_8_ = bf16[128,512]{1,0:T(8,128)(2,1)S(1)} collective-permute-done((bf16[128,512]{1,0:T(8,128)(2,1)S(1)}, bf16[128,512]{1,0:T(8,128)(2,1)S(1)}, u32[]{:S(2)}, u32[]{:S(2)}) %collective-permute-start.8) | collective-permute-done | bytes 131104 | tf_op jit(solution)/shard_map/ppermute | solution.py:53
  55.4 2.1 %collective-permute-done.18.refs_18_ = bf16[1,8,5,16,256]{4,3,2,1,0:T(8,128)(2,1)S(1)} collective-permute-done((bf16[1,8,5,16,256]{4,3,2,1,0:T(8,128)(2,1)S(1)}, bf16[1,8,5,16,256]{4,3,2,1,0:T(8,128)(2,1)S(1)}, u32[]{:S(2)}, u32[]{:S(2)}) %collective-permute-start.18) | collective-permute-done | bytes 327712 | tf_op jit(solution)/shard_map/ppermute | solution.py:29
  57.6 4.3 %forward.1 = (f32[256,2048]{1,0:T(8,128)S(1)}, bf16[256,2048]{1,0:T(8,128)(2,1)S(1)}, bf16[64,2048]{1,0:T(8,128)(2,1)S(1)}, bf16[64,2048]{1,0:T(8,128)(2,1)S(1)}...) custom-call(s32[45]{0:T(128)S(1)} %concatenate.6.meta, ...), custom_call_target="tpu_custom_call" | custom-call | flops 1342177280 | bytes 7340032 | tf_op jit(solution)/shard_map/forward/pallas_call | solution.py:63
  61.8 2.2 %collective-permute-start.19 = (bf16[256,2048]{1,0:T(8,128)(2,1)S(1)}, bf16[256,2048]{1,0:T(8,128)(2,1)S(1)}, u32[]{:S(2)}, u32[]{:S(2)}) collective-permute-start(bf16[256,2048]{1,0:T(8,128)(2,1)S(1)} %get-tuple-element.33.mine), channel_id=1, source_target_pairs={{0,8},{8,0},{16,24},{24,16},{32,40},{40,32},{48,56},{56,48},{64,72... | collective-permute-start | bytes 3145736 | tf_op jit(solution)/shard_map/ppermute | solution.py:41
  66.7 4.6 %collective-permute-done.20.up = bf16[64,2048]{1,0:T(8,128)(2,1)S(1)} collective-permute-done((bf16[64,2048]{1,0:T(8,128)(2,1)S(1)}, bf16[64,2048]{1,0:T(8,128)(2,1)S(1)}, u32[]{:S(2)}, u32[]{:S(2)}) %collective-permute-start.20) | collective-permute-done | bytes 262176 | tf_op jit(solution)/shard_map/ppermute | solution.py:49
  71.3 4.0 %collective-permute-done.21.down = bf16[64,2048]{1,0:T(8,128)(2,1)S(1)} collective-permute-done((bf16[64,2048]{1,0:T(8,128)(2,1)S(1)}, bf16[64,2048]{1,0:T(8,128)(2,1)S(1)}, u32[]{:S(2)}, u32[]{:S(2)}) %collective-permute-start.21) | collective-permute-done | bytes 262176 | tf_op jit(solution)/shard_map/ppermute | solution.py:49
  75.2 9.1 %backward.1 = (bf16[8,21,16,256]{3,2,1,0:T(8,128)(2,1)S(1)}, bf16[8,21,16,256]{3,2,1,0:T(8,128)(2,1)}, bf16[8,21,16,256]{3,2,1,0:T(8,128)(2,1)}, bf16[8,21,16,256]{3,2,1,0:T(8,128)(2,1)}, bf16[256,2048]{1,0:T(8,128)(2,1)S(1)}) custom-call(s32[45]{0:T(128)S(1)} %concatenate.6.meta, bf16[16,256,256]{2,1,0:T(8,128)(2,1)S(1)} %get-tuple-element.32.tok, ...), custom_call_target="tpu_custom_call" | custom-call | flops 1342177280 | bytes 6889472 | tf_op jit(solution)/shard_map/backward/pallas_call | solution.py:63
  84.9 3.4 %collective-permute-start.22 = (bf16[16,128,256]{2,1,0:T(8,128)(2,1)S(1)}, bf16[16,128,256]{2,1,0:T(8,128)(2,1)S(1)}, u32[]{:S(2)}, u32[]{:S(2)}) collective-permute-start(bf16[16,128,256]{2,1,0:T(8,128)(2,1)S(1)} %get-tuple-element.40), channel_id=1, source_target_pairs={{0,8},{8,0},{16,24},{24,16},{32,40},{40,32},{48,56},{56,48},{64,72... | collective-permute-start | bytes 3145736 | tf_op jit(solution)/shard_map/ppermute | solution.py:41
  88.9 5.3 %collective-permute-start.24 = (bf16[8,21,16,256]{3,2,1,0:T(8,128)(2,1)}, bf16[8,21,16,256]{3,2,1,0:T(8,128)(2,1)}, u32[]{:S(2)}, u32[]{:S(2)}) collective-permute-start(bf16[8,21,16,256]{3,2,1,0:T(8,128)(2,1)} %get-tuple-element.44), channel_id=1, source_target_pairs={{0,192},{8,56},{16,208},{24,8},{32,224},{40,24},{48,240},{56,40},{... | collective-permute-start | bytes 4128776 | tf_op jit(solution)/shard_map/ppermute | solution.py:29
  96.6 3.6 %all-to-all-start = ((bf16[16,128,256]{2,1,0:T(8,128)(2,1)}), bf16[16,128,256]{2,1,0:T(8,128)(2,1)S(1)}, u32[]{:S(2)}, u32[]{:S(2)}) async-start(bf16[16,128,256]{2,1,0:T(8,128)(2,1)} %broadcast_select_fusion.refs_0_), calls=%async_computation | async-start | bytes 2097152 | tf_op jit(solution)/shard_map/all_to_all | solution.py:397
  100.1 10.3 %collective-permute-done.23.prev = bf16[8,21,16,256]{3,2,1,0:T(8,128)(2,1)} collective-permute-done((bf16[8,21,16,256]{3,2,1,0:T(8,128)(2,1)}, bf16[8,21,16,256]{3,2,1,0:T(8,128)(2,1)}, u32[]{:S(2)}, u32[]{:S(2)}) %collective-permute-start.23) | collective-permute-done | bytes 1376288 | tf_op jit(solution)/shard_map/ppermute | solution.py:29
  110.5 14.1 %collective-permute-done.24.nxt = bf16[8,21,16,256]{3,2,1,0:T(8,128)(2,1)} collective-permute-done((bf16[8,21,16,256]{3,2,1,0:T(8,128)(2,1)}, bf16[8,21,16,256]{3,2,1,0:T(8,128)(2,1)}, u32[]{:S(2)}, u32[]{:S(2)}) %collective-permute-start.24) | collective-permute-done | bytes 1376288 | tf_op jit(solution)/shard_map/ppermute | solution.py:29
  126.4 2.9 %firstsum.1 = (bf16[8,6,16,256]{3,2,1,0:T(8,128)(2,1)S(1)}, bf16[8,6,16,256]{3,2,1,0:T(8,128)(2,1)S(1)}, bf16[8,6,16,256]{3,2,1,0:T(8,128)(2,1)S(1)}, bf16[8,6,16,256]{3,2,1,0:T(8,128)(2,1)S(1)}) custom-call(s32[45]{0:T(128)S(1)} %concatenate.6.meta, bf16[8,21,16,256]{3,2,1,0:T(8,128)(2,1)S(1)} %get-tuple-element.42.own, ...), custom_call_target="tpu_custom_call" | custom-call | flops 1048576 | bytes 6553600 | tf_op jit(solution)/shard_map/firstsum/pallas_call | solution.py:63
  129.4 2.7 %collective-permute-start.27 = (bf16[8,6,16,256]{3,2,1,0:T(8,128)(2,1)S(1)}, bf16[8,6,16,256]{3,2,1,0:T(8,128)(2,1)S(1)}, u32[]{:S(2)}, u32[]{:S(2)}) collective-permute-start(bf16[8,6,16,256]{3,2,1,0:T(8,128)(2,1)S(1)} %get-tuple-element.48), channel_id=1, source_target_pairs={{0,48},{8,200},{16,0},{24,216},{32,16},{40,232},{48,32},{56,248},{... | collective-permute-start | bytes 1179656 | tf_op jit(solution)/shard_map/ppermute | solution.py:29
  133.3 8.4 %collective-permute-done.26.prev = bf16[8,6,16,256]{3,2,1,0:T(8,128)(2,1)S(1)} collective-permute-done((bf16[8,6,16,256]{3,2,1,0:T(8,128)(2,1)S(1)}, bf16[8,6,16,256]{3,2,1,0:T(8,128)(2,1)S(1)}, u32[]{:S(2)}, u32[]{:S(2)}) %collective-permute-start.26) | collective-permute-done | bytes 393248 | tf_op jit(solution)/shard_map/ppermute | solution.py:29
  (66 shorter events, 33.1 us)
Async XLA Ops:
  6.7 15.5 %collective-permute-start.11 = (bf16[2,8,5,16,256]{4,3,2,1,0:T(8,128)(2,1)S(1)}, bf16[2,8,5,16,256]{4,3,2,1,0:T(8,128)(2,1)S(1)}, u32[]{:S(2)}, u32[]{:S(2)}) collective-permute-start(bf16[2,8,5,16,256]{4,3,2,1,0:T(8,128)(2,1)S(1)} %pad_maximum_fusion.src.refs_9_), channel_id=1, source_target_pairs={{0,192},{8,72},{16,208},{24,88},{32,224},{40,104},{48,240},{56,120... | collective-permute-start | bytes 1966088 | tf_op jit(solution)/shard_map/ppermute | solution.py:29
  6.8 15.4 %collective-permute-start.10 = (bf16[2,8,5,16,256]{4,3,2,1,0:T(8,128)(2,1)S(1)}, bf16[2,8,5,16,256]{4,3,2,1,0:T(8,128)(2,1)S(1)}, u32[]{:S(2)}, u32[]{:S(2)}) collective-permute-start(bf16[2,8,5,16,256]{4,3,2,1,0:T(8,128)(2,1)S(1)} %pad_maximum_fusion.src.refs_9_), channel_id=1, source_target_pairs={{0,16},{8,56},{16,32},{24,8},{32,48},{40,24},{48,0},{56,40},{64,80... | collective-permute-start | bytes 1966088 | tf_op jit(solution)/shard_map/ppermute | solution.py:29
  8.9 10.1 %collective-permute-start.4 = (bf16[256,512]{1,0:T(8,128)(2,1)S(1)}, bf16[256,512]{1,0:T(8,128)(2,1)S(1)}, u32[]{:S(2)}, u32[]{:S(2)}) collective-permute-start(bf16[256,512]{1,0:T(8,128)(2,1)S(1)} %pad_maximum_fusion.1.refs_0_), channel_id=1, source_target_pairs={{0,7},{1,0},{2,1},{3,2},{4,3},{5,4},{6,5},{7,6},{8,15},{9,8},{10,9... | collective-permute-start | bytes 786440 | tf_op jit(solution)/shard_map/ppermute | solution.py:53
  14.5 7.6 %collective-permute-start.1 = (bf16[256,512]{1,0:T(8,128)(2,1)S(1)}, bf16[256,512]{1,0:T(8,128)(2,1)S(1)}, u32[]{:S(2)}, u32[]{:S(2)}) collective-permute-start(bf16[256,512]{1,0:T(8,128)(2,1)S(1)} %pad_maximum_fusion.1.refs_0_), channel_id=1, source_target_pairs={{0,1},{1,2},{2,3},{3,4},{4,5},{5,6},{6,7},{7,0},{8,9},{9,10},{10,1... | collective-permute-start | bytes 786440 | tf_op jit(solution)/shard_map/ppermute | solution.py:53
  22.8 11.0 %collective-permute-start.12 = (bf16[2,8,5,16,256]{4,3,2,1,0:T(8,128)(2,1)S(1)}, bf16[2,8,5,16,256]{4,3,2,1,0:T(8,128)(2,1)S(1)}, u32[]{:S(2)}, u32[]{:S(2)}) collective-permute-start(bf16[2,8,5,16,256]{4,3,2,1,0:T(8,128)(2,1)S(1)} %hold.1), channel_id=1, source_target_pairs={{0,48},{8,24},{16,0},{24,40},{32,16},{40,56},{48,32},{56,8},{64,11... | collective-permute-start | bytes 1966088 | tf_op jit(solution)/shard_map/ppermute | solution.py:29
  22.9 10.9 %collective-permute-start.13 = (bf16[2,8,5,16,256]{4,3,2,1,0:T(8,128)(2,1)S(1)}, bf16[2,8,5,16,256]{4,3,2,1,0:T(8,128)(2,1)S(1)}, u32[]{:S(2)}, u32[]{:S(2)}) collective-permute-start(bf16[2,8,5,16,256]{4,3,2,1,0:T(8,128)(2,1)S(1)} %collective-permute-done.10.refs_0_.a.refs_10_), channel_id=1, source_target_pairs={{0,64},{8,200},{16,80},{24,216},{32,96},{40,232},{48,112},{56,248}... | collective-permute-start | bytes 1966088 | tf_op jit(solution)/shard_map/ppermute | solution.py:29
  34.4 7.6 %collective-permute-start.15 = (bf16[1,8,5,16,256]{4,3,2,1,0:T(8,128)(2,1)S(1)}, bf16[1,8,5,16,256]{4,3,2,1,0:T(8,128)(2,1)S(1)}, u32[]{:S(2)}, u32[]{:S(2)}) collective-permute-start(bf16[1,8,5,16,256]{4,3,2,1,0:T(8,128)(2,1)S(1)} %get-tuple-element.30), channel_id=1, source_target_pairs={{0,16},{8,56},{16,32},{24,8},{32,48},{40,24},{48,0},{56,40},{64,80... | collective-permute-start | bytes 983048 | tf_op jit(solution)/shard_map/ppermute | solution.py:29
  38.0 17.4 %collective-permute-start.14 = (bf16[2,8,5,16,256]{4,3,2,1,0:T(8,128)(2,1)S(1)}, bf16[2,8,5,16,256]{4,3,2,1,0:T(8,128)(2,1)S(1)}, u32[]{:S(2)}, u32[]{:S(2)}) collective-permute-start(bf16[2,8,5,16,256]{4,3,2,1,0:T(8,128)(2,1)S(1)} %collective-permute-done.12.c.refs_12_), channel_id=1, source_target_pairs={{0,192},{8,72},{16,208},{24,88},{32,224},{40,104},{48,240},{56,120... | collective-permute-start | bytes 1966088 | tf_op jit(solution)/shard_map/ppermute | solution.py:29
  38.1 10.2 %collective-permute-start.16 = (bf16[1,8,5,16,256]{4,3,2,1,0:T(8,128)(2,1)S(1)}, bf16[1,8,5,16,256]{4,3,2,1,0:T(8,128)(2,1)S(1)}, u32[]{:S(2)}, u32[]{:S(2)}) collective-permute-start(bf16[1,8,5,16,256]{4,3,2,1,0:T(8,128)(2,1)S(1)} %get-tuple-element.31), channel_id=1, source_target_pairs={{0,48},{8,24},{16,0},{24,40},{32,16},{40,56},{48,32},{56,8},{64,11... | collective-permute-start | bytes 983048 | tf_op jit(solution)/shard_map/ppermute | solution.py:29
  38.1 11.5 %collective-permute-start.6 = (bf16[256,512]{1,0:T(8,128)(2,1)S(1)}, bf16[256,512]{1,0:T(8,128)(2,1)S(1)}, u32[]{:S(2)}, u32[]{:S(2)}) collective-permute-start(bf16[256,512]{1,0:T(8,128)(2,1)S(1)} %collective-permute-done.5.refs_2_.refs_5_), channel_id=1, source_target_pairs={{0,7},{1,0},{2,1},{3,2},{4,3},{5,4},{6,5},{7,6},{8,15},{9,8},{10,9... | collective-permute-start | bytes 786440 | tf_op jit(solution)/shard_map/ppermute | solution.py:53
  38.3 11.7 %collective-permute-start.3 = (bf16[256,512]{1,0:T(8,128)(2,1)S(1)}, bf16[256,512]{1,0:T(8,128)(2,1)S(1)}, u32[]{:S(2)}, u32[]{:S(2)}) collective-permute-start(bf16[256,512]{1,0:T(8,128)(2,1)S(1)} %collective-permute-done.2.refs_1_.refs_2_), channel_id=1, source_target_pairs={{0,1},{1,2},{2,3},{3,4},{4,5},{5,6},{6,7},{7,0},{8,9},{9,10},{10,1... | collective-permute-start | bytes 786440 | tf_op jit(solution)/shard_map/ppermute | solution.py:53
  42.0 13.4 %collective-permute-start.17 = (bf16[1,8,5,16,256]{4,3,2,1,0:T(8,128)(2,1)S(1)}, bf16[1,8,5,16,256]{4,3,2,1,0:T(8,128)(2,1)S(1)}, u32[]{:S(2)}, u32[]{:S(2)}) collective-permute-start(bf16[1,8,5,16,256]{4,3,2,1,0:T(8,128)(2,1)S(1)} %collective-permute-done.15.refs_15_), channel_id=1, source_target_pairs={{0,64},{8,200},{16,80},{24,216},{32,96},{40,232},{48,112},{56,248}... | collective-permute-start | bytes 983048 | tf_op jit(solution)/shard_map/ppermute | solution.py:29
  48.3 9.3 %collective-permute-start.18 = (bf16[1,8,5,16,256]{4,3,2,1,0:T(8,128)(2,1)S(1)}, bf16[1,8,5,16,256]{4,3,2,1,0:T(8,128)(2,1)S(1)}, u32[]{:S(2)}, u32[]{:S(2)}) collective-permute-start(bf16[1,8,5,16,256]{4,3,2,1,0:T(8,128)(2,1)S(1)} %collective-permute-done.16.refs_16_), channel_id=1, source_target_pairs={{0,192},{8,72},{16,208},{24,88},{32,224},{40,104},{48,240},{56,120... | collective-permute-start | bytes 983048 | tf_op jit(solution)/shard_map/ppermute | solution.py:29
  61.8 13.4 %collective-permute-start.19 = (bf16[256,2048]{1,0:T(8,128)(2,1)S(1)}, bf16[256,2048]{1,0:T(8,128)(2,1)S(1)}, u32[]{:S(2)}, u32[]{:S(2)}) collective-permute-start(bf16[256,2048]{1,0:T(8,128)(2,1)S(1)} %get-tuple-element.33.mine), channel_id=1, source_target_pairs={{0,8},{8,0},{16,24},{24,16},{32,40},{40,32},{48,56},{56,48},{64,72... | collective-permute-start | bytes 3145736 | tf_op jit(solution)/shard_map/ppermute | solution.py:41
  64.1 7.2 %collective-permute-start.20 = (bf16[64,2048]{1,0:T(8,128)(2,1)S(1)}, bf16[64,2048]{1,0:T(8,128)(2,1)S(1)}, u32[]{:S(2)}, u32[]{:S(2)}) collective-permute-start(bf16[64,2048]{1,0:T(8,128)(2,1)S(1)} %get-tuple-element.34), channel_id=1, source_target_pairs={{0,24},{8,16},{16,40},{24,32},{32,56},{40,48},{48,72},{56,64},{64,... | collective-permute-start | bytes 786440 | tf_op jit(solution)/shard_map/ppermute | solution.py:49
  65.4 9.8 %collective-permute-start.21 = (bf16[64,2048]{1,0:T(8,128)(2,1)S(1)}, bf16[64,2048]{1,0:T(8,128)(2,1)S(1)}, u32[]{:S(2)}, u32[]{:S(2)}) collective-permute-start(bf16[64,2048]{1,0:T(8,128)(2,1)S(1)} %get-tuple-element.35), channel_id=1, source_target_pairs={{16,8},{24,0},{32,24},{40,16},{48,40},{56,32},{64,56},{72,48},{80,... | collective-permute-start | bytes 786440 | tf_op jit(solution)/shard_map/ppermute | solution.py:49
  84.9 10.6 %collective-permute-start.22 = (bf16[16,128,256]{2,1,0:T(8,128)(2,1)S(1)}, bf16[16,128,256]{2,1,0:T(8,128)(2,1)S(1)}, u32[]{:S(2)}, u32[]{:S(2)}) collective-permute-start(bf16[16,128,256]{2,1,0:T(8,128)(2,1)S(1)} %get-tuple-element.40), channel_id=1, source_target_pairs={{0,8},{8,0},{16,24},{24,16},{32,40},{40,32},{48,56},{56,48},{64,72... | collective-permute-start | bytes 3145736 | tf_op jit(solution)/shard_map/ppermute | solution.py:41
  88.2 22.2 %collective-permute-start.23 = (bf16[8,21,16,256]{3,2,1,0:T(8,128)(2,1)}, bf16[8,21,16,256]{3,2,1,0:T(8,128)(2,1)}, u32[]{:S(2)}, u32[]{:S(2)}) collective-permute-start(bf16[8,21,16,256]{3,2,1,0:T(8,128)(2,1)} %get-tuple-element.43), channel_id=1, source_target_pairs={{0,64},{8,24},{16,80},{24,40},{32,96},{40,56},{48,112},{56,8},{64,... | collective-permute-start | bytes 4128776 | tf_op jit(solution)/shard_map/ppermute | solution.py:29
  88.9 35.6 %collective-permute-start.24 = (bf16[8,21,16,256]{3,2,1,0:T(8,128)(2,1)}, bf16[8,21,16,256]{3,2,1,0:T(8,128)(2,1)}, u32[]{:S(2)}, u32[]{:S(2)}) collective-permute-start(bf16[8,21,16,256]{3,2,1,0:T(8,128)(2,1)} %get-tuple-element.44), channel_id=1, source_target_pairs={{0,192},{8,56},{16,208},{24,8},{32,224},{40,24},{48,240},{56,40},{... | collective-permute-start | bytes 4128776 | tf_op jit(solution)/shard_map/ppermute | solution.py:29
  94.3 32.1 %collective-permute-start.25 = (bf16[8,21,16,256]{3,2,1,0:T(8,128)(2,1)}, bf16[8,21,16,256]{3,2,1,0:T(8,128)(2,1)}, u32[]{:S(2)}, u32[]{:S(2)}) collective-permute-start(bf16[8,21,16,256]{3,2,1,0:T(8,128)(2,1)} %get-tuple-element.45), channel_id=1, source_target_pairs={{0,128},{8,40},{16,144},{24,56},{32,160},{40,8},{48,176},{56,24},{... | collective-permute-start | bytes 4128776 | tf_op jit(solution)/shard_map/ppermute | solution.py:29
  96.6 48.0 %all-to-all-start = ((bf16[16,128,256]{2,1,0:T(8,128)(2,1)}), bf16[16,128,256]{2,1,0:T(8,128)(2,1)S(1)}, u32[]{:S(2)}, u32[]{:S(2)}) async-start(bf16[16,128,256]{2,1,0:T(8,128)(2,1)} %broadcast_select_fusion.refs_0_), calls=%async_computation | async-start | bytes 2097152 | tf_op jit(solution)/shard_map/all_to_all | solution.py:397
  129.3 12.4 %collective-permute-start.26 = (bf16[8,6,16,256]{3,2,1,0:T(8,128)(2,1)S(1)}, bf16[8,6,16,256]{3,2,1,0:T(8,128)(2,1)S(1)}, u32[]{:S(2)}, u32[]{:S(2)}) collective-permute-start(bf16[8,6,16,256]{3,2,1,0:T(8,128)(2,1)S(1)} %get-tuple-element.47), channel_id=1, source_target_pairs={{0,16},{8,72},{16,32},{24,88},{32,48},{40,104},{48,0},{56,120},{64... | collective-permute-start | bytes 1179656 | tf_op jit(solution)/shard_map/ppermute | solution.py:29
  129.4 12.3 %collective-permute-start.27 = (bf16[8,6,16,256]{3,2,1,0:T(8,128)(2,1)S(1)}, bf16[8,6,16,256]{3,2,1,0:T(8,128)(2,1)S(1)}, u32[]{:S(2)}, u32[]{:S(2)}) collective-permute-start(bf16[8,6,16,256]{3,2,1,0:T(8,128)(2,1)S(1)} %get-tuple-element.48), channel_id=1, source_target_pairs={{0,48},{8,200},{16,0},{24,216},{32,16},{40,232},{48,32},{56,248},{... | collective-permute-start | bytes 1179656 | tf_op jit(solution)/shard_map/ppermute | solution.py:29
  132.1 9.7 %collective-permute-start.28 = (bf16[8,6,16,256]{3,2,1,0:T(8,128)(2,1)S(1)}, bf16[8,6,16,256]{3,2,1,0:T(8,128)(2,1)S(1)}, u32[]{:S(2)}, u32[]{:S(2)}) collective-permute-start(bf16[8,6,16,256]{3,2,1,0:T(8,128)(2,1)S(1)} %get-tuple-element.49), channel_id=1, source_target_pairs={{0,32},{8,136},{16,48},{24,152},{32,0},{40,168},{48,16},{56,184},{... | collective-permute-start | bytes 1179656 | tf_op jit(solution)/shard_map/ppermute | solution.py:29
  (11 other events, 77.6 us)

commit v4 on v3

--- a/solution.py
+++ b/solution.py
@@ -12,7 +12,7 @@
 F32, BF16 = jnp.float32, jnp.bfloat16
 NX, NY, NZ = 4, 4, 8
 COLS, NNZ, BS, PW = 8, 5, 256, 64
-TOK, KERN = 256, 20
+TOK, KERN, SLABS = 256, 20, 56
 CORE, XPOS, YPOS, YLO, ZPOS = 40, 41, 42, 43, 44
 HBM = pl.BlockSpec(memory_space=pltpu.MemorySpace.HBM)
 VMEM = pl.BlockSpec(memory_space=pltpu.VMEM)
@@ -57,16 +57,18 @@
     return lax.dot_general(a, b, (dims, ((), ())), preferred_element_type=F32)
 
 
-def local(kernel, name, outs, args, scratch=(), flops=2**20, hbm=()):
-    shapes = [jax.ShapeDtypeStruct(s, t) for s, t in outs]
+def local(kernel, name, outs, args, scratch=(), flops=2**20, hbm=(), hbm_out=()):
+    shapes = [
+        pltpu.HBM(s, t) if i in hbm_out else jax.ShapeDtypeStruct(s, t) for i, (s, t) in enumerate(outs)
+    ]
     size = sum(a.size * a.dtype.itemsize for a in args[1:])
     return pl.pallas_call(
         kernel,
         out_shape=shapes,
         in_specs=[SMEM] + [HBM if i in hbm else VMEM for i in range(1, len(args))],
-        out_specs=[VMEM] * len(outs),
+        out_specs=[HBM if i in hbm_out else VMEM for i in range(len(outs))],
         scratch_shapes=list(scratch),
-        compiler_params=pltpu.CompilerParams(vmem_limit_bytes=14 * 2**20),
+        compiler_params=pltpu.CompilerParams(vmem_limit_bytes=20 * 2**20),
         cost_estimate=pl.CostEstimate(flops=flops, transcendentals=0, bytes_accessed=size),
         name=name,
     )(*args)
@@ -74,6 +76,46 @@
 
 def lanes(c):
     return pl.ds(pl.multiple_of(c * BS, BS), BS)
+
+
+def split_kernel(meta, *refs):
+    sources, (mine, theirs, *held, sems) = refs[:4], refs[4:]
+    copies = [pltpu.make_async_copy(a, b, sems.at[i]) for i, (a, b) in enumerate(zip(sources, held))]
+    for copy in copies:
+        copy.start()
+    for copy in copies:
+        copy.wait()
+    w_in, w_out, tok, cot = held
+    is_in = meta[CORE] == 0
+
+    def put(at, a, b):
+        mine[at] = jnp.where(is_in, a, b).astype(BF16)
+        theirs[at] = jnp.where(is_in, b, a).astype(BF16)
+
+    for k in range(NNZ):
+        a, b = (jnp.swapaxes(w[:, k].astype(F32), 0, 1) for w in (w_in, w_out))
+        for c in range(COLS):
+            put(c * NNZ + k, a[c], b[c])
+    for p in range(2):
+        for r in range(8):
+            part = (slice(r * 16, r * 16 + 16), slice(p * BS, p * BS + BS))
+            put(COLS * NNZ + p * 8 + r, tok[part].astype(F32), cot[part].astype(F32))
+
+
+def join_kernel(meta, mine, got, own, rows):
+    for s in range(2):
+        here = meta[CORE] == s
+
+        def take(at):
+            return jnp.where(here, mine[at].astype(F32), got[at].astype(F32)).astype(BF16)
+
+        for c in range(COLS):
+            for k in range(NNZ):
+                own[s, c, k] = take(c * NNZ + k)
+        for p in range(2):
+            for r in range(8):
+                at = s * 128 + r * 16
+                rows[at : at + 16, p * BS : p * BS + BS] = take(COLS * NNZ + p * 8 + r)
 
 
 def start_tokens(meta, pieces, buf, sem):
@@ -190,7 +232,7 @@
 
 
 def backward_kernel(meta, tok, got, mine, up, down, pre, taps, *refs):
-    *outs, pgrad, conv, lhs, res, slab, moved = refs
+    *outs, pgrad, conv, lhs, res, slab, moved, stage, sems = refs
     core, x, y = meta[CORE], meta[XPOS], meta[YPOS]
     is_in = core == 0
     slab[...] = jnp.zeros_like(slab)
@@ -245,8 +287,12 @@
             start = (here + d) % 4 * far
             for k in range(NNZ):
                 for s in range(4):
-                    out[c, k * 4 + s] = res[k, start + s * near]
-            out[c, KERN] = slab[...]
+                    stage[d, c, k * 4 + s] = res[k, start + s * near]
+            stage[d, c, KERN] = slab[...]
+            pltpu.make_async_copy(stage.at[d, c], out.at[c], sems.at[d]).start()
+
+    for d, out in enumerate(outs):
+        pltpu.make_async_copy(stage.at[d], out, sems.at[d]).wait()
 
 
 def backward(meta, tok, got, mine, up, down, pre, taps):
@@ -257,10 +303,18 @@
         pltpu.VMEM((NNZ, 16, 16, BS), BF16),
         pltpu.VMEM((16, BS), BF16),
         pltpu.VMEM((18, PW, BS), F32),
+        pltpu.VMEM((4, COLS, KERN + 1, 16, BS), BF16),
+        pltpu.SemaphoreType.DMA((4,)),
     ]
     args = (meta, tok, got, mine, up, down, pre, taps)
     return local(
-        backward_kernel, "backward", outs, args, scratch, flops=2 * TOK * BS * BS * NNZ * COLS
+        backward_kernel,
+        "backward",
+        outs,
+        args,
+        scratch,
+        flops=2 * TOK * BS * BS * NNZ * COLS,
+        hbm_out=range(4),
     )
 
 
@@ -269,7 +323,7 @@
     def _():
         acc[...] = jnp.zeros_like(acc)
 
-        @pl.loop(0, COLS)
+        @pl.loop(0, COLS, unroll=2)
         def _(c):
             for k in range(NNZ):
                 wt = wts[c, k].reshape(BS, BS)
@@ -301,20 +355,25 @@
         out[:, b * BS : (b + 1) * BS] = total.astype(BF16)
 
 
-def first_sum_kernel(meta, own, prev, nxt, far, *refs):
-    outs = refs[-4:]
+def first_sum_kernel(meta, *refs):
+    parts, outs, (held, sems) = refs[:4], refs[5:9], refs[9:]
     here = jnp.where(meta[CORE] == 0, meta[XPOS], meta[YPOS])
-
-    def total(c, at):
-        a, b, e, f = (r[c, at].astype(F32) for r in (own, prev, nxt, far))
-        return ((a + f) + (b + e)).astype(BF16)
+    for c in range(COLS):
+        for i, part in enumerate(parts):
+            pltpu.make_async_copy(part.at[c], held.at[c, i], sems.at[c]).start()
 
     @pl.loop(0, COLS)
     def _(c):
+        pltpu.make_async_copy(held.at[c], held.at[c], sems.at[c]).wait()
+
+        def total(at):
+            a, b, e, f = (held[c, i, at].astype(F32) for i in range(4))
+            return ((a + f) + (b + e)).astype(BF16)
+
         for d in range(4):
             for k in range(NNZ):
-                outs[d][c, k] = total(c, k * 4 + (here + d) % 4)
-        slab = total(c, KERN)
+                outs[d][c, k] = total(k * 4 + (here + d) % 4)
+        slab = total(KERN)
         for out in outs:
             out[c, NNZ] = slab
 
@@ -359,14 +418,14 @@
     place = jnp.stack([core, x, crop * 2 + ylo, ylo, z]).astype(jnp.int32)
     meta = jnp.concatenate([block_rows.reshape(-1), place])
     is_in = core == 0
-
-    def side(a, b):
-        mine, theirs = jnp.where(is_in, a, b), jnp.where(is_in, b, a)
-        got = to_partner(theirs)
-        return jnp.where(is_in, mine, got), jnp.where(is_in, got, mine)
-
-    own = jnp.stack(side(*(w.transpose(1, 2, 0, 3) for w in (weight_in, weight_out))))
-    t0 = jnp.concatenate(side(tokens.reshape(128, 512), cotangent.reshape(128, 512)))
+    views = [w.transpose(0, 2, 1, 3) for w in (weight_in, weight_out)]
+    rows = [t.reshape(128, 512) for t in (tokens, cotangent)]
+    slabs = [((SLABS, 16, BS), BF16)] * 2
+    held = [pltpu.VMEM(a.shape, BF16) for a in views + rows] + [pltpu.SemaphoreType.DMA((4,))]
+    args = (meta, *(pltpu.with_memory_space_constraint(a, pltpu.HBM) for a in views + rows))
+    mine, theirs = local(split_kernel, "split", slabs, args, held, hbm=range(1, 5))
+    shapes = [((2, COLS, NNZ, 16, BS), BF16), ((TOK, 2 * BS), BF16)]
+    own, t0 = local(join_kernel, "join", shapes, (meta, mine, to_partner(theirs)))
 
     wa = by_core(own, (0, 1), (0, -1))
     wb = by_core(own, (-1, 0), (1, 0))
@@ -403,7 +462,8 @@
         "firstsum",
         [((COLS, NNZ + 1, 16, BS), BF16)] * 4,
         (meta, *parts, terms),
-        hbm=(5,),
+        [pltpu.VMEM((COLS, 4, KERN + 1, 16, BS), BF16), pltpu.SemaphoreType.DMA((COLS,))],
+        hbm=range(1, 6),
     )
     last = (h[0], second(h[1], 1), second(h[3], -1), second(h[2], 2))
     shape = ((COLS, NNZ + 2, 8, BS), BF16)

time: 148 us -> 149 us (level)
  other arithmetic: 3.58 us -> 1.08 us
  Pallas kernels: 21.8 us -> 24.2 us
    pallas_call x9 -> x11, Pallas kernels: 21.8 us -> 24.2 us  [local(): pl.pallas_call(kernel, out_shape=shapes, in_specs=[SMEM] + [HBM if i in h...]
    select_n x3 -> x0, other arithmetic: 2.25 us -> none  [the longest x2 2.22 us: side(): mine, theirs = (jnp.where(is_in, a, b), jnp.where(is_in, b, a))]
    ppermute x5 -> x4, starting transfers between devices: 11 us -> 10.3 us  [to_partner(): return lax.ppermute(value, 'rows', [(r, r ^ 1) for r in range(16)])]
  transfers between devices with their start and end apart: 31 -> 30, of which waited for: 17 -> 17; matrix products, arithmetic and copies ran while one was open for 2% -> 1% of each run, Pallas kernels for 3% -> 4%
where the time goes in v4:
time: 149 us
  waiting for transfers between devices  72 us (48%)
  starting transfers between devices  50 us (34%)
  Pallas kernels  24.2 us (16%)
    ppermute x15, waiting for transfers between devices, by_core(): return lax.ppermute(value, ('crop', 'rows'), pairs)  44.6 us
    pallas_call x11, Pallas kernels, local(): pl.pallas_call(kernel, out_shape=shapes, in_specs=[SMEM] + [HBM if i in h...  24.2 us
    ppermute x15, starting transfers between devices, by_core(): return lax.ppermute(value, ('crop', 'rows'), pairs)  23.3 us
    ppermute x8, waiting for transfers between devices, along_z(): return lax.ppermute(value, 'hid', [(z, (z + step) % NZ) for z in range(NZ)])  17.4 us
    ppermute x4, starting transfers between devices, to_partner(): return lax.ppermute(value, 'rows', [(r, r ^ 1) for r in range(16)])  10.3 us
    ppermute x8, starting transfers between devices, along_z(): return lax.ppermute(value, 'hid', [(z, (z + step) % NZ) for z in range(NZ)])  10.1 us
    ppermute x2, waiting for transfers between devices, to_next_chip(): return lax.ppermute(value, 'rows', pairs)  8.54 us
    all_to_all x1, starting transfers between devices, on_device(): shares = lax.all_to_all(terms, 'hid', 0, 0, tiled=True)  3.69 us
  transfers between devices with their start and end apart: 30, of which 17 were waited for; matrix products, arithmetic and copies ran while one was open for 1% of the time, Pallas kernels for 4%

profile of v4, /device:TPU:1, one launch (start us, length us, event | category | flops | bytes accessed | tf_op | source)
XLA Modules:
  0.0 149.0 jit_solution(5596573718022057004)
XLA Ops:
  3.6 3.3 %collective-permute-start = (bf16[56,16,256]{2,1,0:T(8,128)(2,1)S(1)}, bf16[56,16,256]{2,1,0:T(8,128)(2,1)S(1)}, u32[]{:S(2)}, u32[]{:S(2)}) collective-permute-start(bf16[56,16,256]{2,1,0:T(8,128)(2,1)S(1)} %get-tuple-element.35), channel_id=1, source_target_pairs={{0,8},{8,0},{16,24},{24,16},{32,40},{40,32},{48,56},{56,48},{64,72... | collective-permute-start | bytes 1376264 | tf_op jit(solution)/shard_map/ppermute | solution.py:41
  11.3 5.6 %collective-permute-start.4 = (bf16[256,512]{1,0:T(8,128)(2,1)S(1)}, bf16[256,512]{1,0:T(8,128)(2,1)S(1)}, u32[]{:S(2)}, u32[]{:S(2)}) collective-permute-start(bf16[256,512]{1,0:T(8,128)(2,1)S(1)} %get-tuple-element.36.refs_0_), channel_id=1, source_target_pairs={{0,7},{1,0},{2,1},{3,2},{4,3},{5,4},{6,5},{7,6},{8,15},{9,8},{10,9... | collective-permute-start | bytes 786440 | tf_op jit(solution)/shard_map/ppermute | solution.py:53
  16.9 4.5 %collective-permute-done.4.refs_3_.refs_4_ = bf16[256,512]{1,0:T(8,128)(2,1)S(1)} collective-permute-done((bf16[256,512]{1,0:T(8,128)(2,1)S(1)}, bf16[256,512]{1,0:T(8,128)(2,1)S(1)}, u32[]{:S(2)}, u32[]{:S(2)}) %collective-permute-start.4) | collective-permute-done | bytes 262176 | tf_op jit(solution)/shard_map/ppermute | solution.py:53
  21.3 3.1 %collective-permute-done.1.refs_2_.refs_1_ = bf16[256,512]{1,0:T(8,128)(2,1)S(1)} collective-permute-done((bf16[256,512]{1,0:T(8,128)(2,1)S(1)}, bf16[256,512]{1,0:T(8,128)(2,1)S(1)}, u32[]{:S(2)}, u32[]{:S(2)}) %collective-permute-start.1) | collective-permute-done | bytes 262176 | tf_op jit(solution)/shard_map/ppermute | solution.py:53
  25.2 2.8 %collective-permute-start.12 = (bf16[2,8,5,16,256]{4,3,2,1,0:T(8,128)(2,1)S(1)}, bf16[2,8,5,16,256]{4,3,2,1,0:T(8,128)(2,1)S(1)}, u32[]{:S(2)}, u32[]{:S(2)}) collective-permute-start(bf16[2,8,5,16,256]{4,3,2,1,0:T(8,128)(2,1)S(1)} %collective-permute-done.9.refs_0_.a.refs_10_), channel_id=1, source_target_pairs={{0,64},{8,200},{16,80},{24,216},{32,96},{40,232},{48,112},{56,248}... | collective-permute-start | bytes 1966088 | tf_op jit(solution)/shard_map/ppermute | solution.py:29
  29.4 4.4 %collective-permute-done.5.refs_2_.refs_5_ = bf16[256,512]{1,0:T(8,128)(2,1)S(1)} collective-permute-done((bf16[256,512]{1,0:T(8,128)(2,1)S(1)}, bf16[256,512]{1,0:T(8,128)(2,1)S(1)}, u32[]{:S(2)}, u32[]{:S(2)}) %collective-permute-start.5) | collective-permute-done | bytes 262176 | tf_op jit(solution)/shard_map/ppermute | solution.py:53
  36.7 3.5 %collective-permute-start.14 = (bf16[1,8,5,16,256]{4,3,2,1,0:T(8,128)(2,1)S(1)}, bf16[1,8,5,16,256]{4,3,2,1,0:T(8,128)(2,1)S(1)}, u32[]{:S(2)}, u32[]{:S(2)}) collective-permute-start(bf16[1,8,5,16,256]{4,3,2,1,0:T(8,128)(2,1)S(1)} %get-tuple-element.38), channel_id=1, source_target_pairs={{0,16},{8,56},{16,32},{24,8},{32,48},{40,24},{48,0},{56,40},{64,80... | collective-permute-start | bytes 983048 | tf_op jit(solution)/shard_map/ppermute | solution.py:29
  41.9 2.3 %collective-permute-done.14.refs_15_ = bf16[1,8,5,16,256]{4,3,2,1,0:T(8,128)(2,1)S(1)} collective-permute-done((bf16[1,8,5,16,256]{4,3,2,1,0:T(8,128)(2,1)S(1)}, bf16[1,8,5,16,256]{4,3,2,1,0:T(8,128)(2,1)S(1)}, u32[]{:S(2)}, u32[]{:S(2)}) %collective-permute-start.14) | collective-permute-done | bytes 327712 | tf_op jit(solution)/shard_map/ppermute | solution.py:29
  46.1 4.5 %collective-permute-done.15.refs_16_ = bf16[1,8,5,16,256]{4,3,2,1,0:T(8,128)(2,1)S(1)} collective-permute-done((bf16[1,8,5,16,256]{4,3,2,1,0:T(8,128)(2,1)S(1)}, bf16[1,8,5,16,256]{4,3,2,1,0:T(8,128)(2,1)S(1)}, u32[]{:S(2)}, u32[]{:S(2)}) %collective-permute-start.15) | collective-permute-done | bytes 327712 | tf_op jit(solution)/shard_map/ppermute | solution.py:29
  53.6 2.5 %collective-permute-done.8.refs_8_ = bf16[128,512]{1,0:T(8,128)(2,1)S(1)} collective-permute-done((bf16[128,512]{1,0:T(8,128)(2,1)S(1)}, bf16[128,512]{1,0:T(8,128)(2,1)S(1)}, u32[]{:S(2)}, u32[]{:S(2)}) %collective-permute-start.8) | collective-permute-done | bytes 131104 | tf_op jit(solution)/shard_map/ppermute | solution.py:53
  57.9 2.2 %collective-permute-done.17.refs_18_ = bf16[1,8,5,16,256]{4,3,2,1,0:T(8,128)(2,1)S(1)} collective-permute-done((bf16[1,8,5,16,256]{4,3,2,1,0:T(8,128)(2,1)S(1)}, bf16[1,8,5,16,256]{4,3,2,1,0:T(8,128)(2,1)S(1)}, u32[]{:S(2)}, u32[]{:S(2)}) %collective-permute-start.17) | collective-permute-done | bytes 327712 | tf_op jit(solution)/shard_map/ppermute | solution.py:29
  60.1 4.3 %forward.1 = (f32[256,2048]{1,0:T(8,128)S(1)}, bf16[256,2048]{1,0:T(8,128)(2,1)S(1)}, bf16[64,2048]{1,0:T(8,128)(2,1)S(1)}, bf16[64,2048]{1,0:T(8,128)(2,1)S(1)}...) custom-call(s32[45]{0:T(128)S(1)} %concatenate.3.meta, ...), custom_call_target="tpu_custom_call" | custom-call | flops 1342177280 | bytes 7340032 | tf_op jit(solution)/shard_map/forward/pallas_call | solution.py:65
  64.3 2.1 %collective-permute-start.18 = (bf16[256,2048]{1,0:T(8,128)(2,1)S(1)}, bf16[256,2048]{1,0:T(8,128)(2,1)S(1)}, u32[]{:S(2)}, u32[]{:S(2)}) collective-permute-start(bf16[256,2048]{1,0:T(8,128)(2,1)S(1)} %get-tuple-element.41.mine), channel_id=1, source_target_pairs={{0,8},{8,0},{16,24},{24,16},{32,40},{40,32},{48,56},{56,48},{64,72... | collective-permute-start | bytes 3145736 | tf_op jit(solution)/shard_map/ppermute | solution.py:41
  69.1 4.6 %collective-permute-done.19.up = bf16[64,2048]{1,0:T(8,128)(2,1)S(1)} collective-permute-done((bf16[64,2048]{1,0:T(8,128)(2,1)S(1)}, bf16[64,2048]{1,0:T(8,128)(2,1)S(1)}, u32[]{:S(2)}, u32[]{:S(2)}) %collective-permute-start.19) | collective-permute-done | bytes 262176 | tf_op jit(solution)/shard_map/ppermute | solution.py:49
  73.7 4.0 %collective-permute-done.20.down = bf16[64,2048]{1,0:T(8,128)(2,1)S(1)} collective-permute-done((bf16[64,2048]{1,0:T(8,128)(2,1)S(1)}, bf16[64,2048]{1,0:T(8,128)(2,1)S(1)}, u32[]{:S(2)}, u32[]{:S(2)}) %collective-permute-start.20) | collective-permute-done | bytes 262176 | tf_op jit(solution)/shard_map/ppermute | solution.py:49
  77.6 7.9 %backward.1 = (bf16[8,21,16,256]{3,2,1,0:T(8,128)(2,1)}, bf16[8,21,16,256]{3,2,1,0:T(8,128)(2,1)}, bf16[8,21,16,256]{3,2,1,0:T(8,128)(2,1)}, bf16[8,21,16,256]{3,2,1,0:T(8,128)(2,1)}, bf16[256,2048]{1,0:T(8,128)(2,1)S(1)}) custom-call(s32[45]{0:T(128)S(1)} %concatenate.3.meta, bf16[16,256,256]{2,1,0:T(8,128)(2,1)S(1)} %get-tuple-element.40.tok, ...), custom_call_target="tpu_custom_call" | custom-call | flops 1342177280 | bytes 6889472 | tf_op jit(solution)/shard_map/backward/pallas_call | solution.py:65
  86.1 2.9 %collective-permute-start.21 = (bf16[16,128,256]{2,1,0:T(8,128)(2,1)S(1)}, bf16[16,128,256]{2,1,0:T(8,128)(2,1)S(1)}, u32[]{:S(2)}, u32[]{:S(2)}) collective-permute-start(bf16[16,128,256]{2,1,0:T(8,128)(2,1)S(1)} %get-tuple-element.48), channel_id=1, source_target_pairs={{0,8},{8,0},{16,24},{24,16},{32,40},{40,32},{48,56},{56,48},{64,72... | collective-permute-start | bytes 3145736 | tf_op jit(solution)/shard_map/ppermute | solution.py:41
  89.7 5.3 %collective-permute-start.23 = (bf16[8,21,16,256]{3,2,1,0:T(8,128)(2,1)}, bf16[8,21,16,256]{3,2,1,0:T(8,128)(2,1)}, u32[]{:S(2)}, u32[]{:S(2)}) collective-permute-start(bf16[8,21,16,256]{3,2,1,0:T(8,128)(2,1)} %get-tuple-element.52), channel_id=1, source_target_pairs={{0,192},{8,56},{16,208},{24,8},{32,224},{40,24},{48,240},{56,40},{... | collective-permute-start | bytes 4128776 | tf_op jit(solution)/shard_map/ppermute | solution.py:29
  97.3 3.7 %all-to-all-start = ((bf16[16,128,256]{2,1,0:T(8,128)(2,1)}), bf16[16,128,256]{2,1,0:T(8,128)(2,1)S(1)}, u32[]{:S(2)}, u32[]{:S(2)}) async-start(bf16[16,128,256]{2,1,0:T(8,128)(2,1)} %broadcast_select_fusion.refs_4_), calls=%async_computation | async-start | bytes 2097152 | tf_op jit(solution)/shard_map/all_to_all | solution.py:456
  101.0 10.2 %collective-permute-done.22.refs_1_ = bf16[8,21,16,256]{3,2,1,0:T(8,128)(2,1)} collective-permute-done((bf16[8,21,16,256]{3,2,1,0:T(8,128)(2,1)}, bf16[8,21,16,256]{3,2,1,0:T(8,128)(2,1)}, u32[]{:S(2)}, u32[]{:S(2)}) %collective-permute-start.22) | collective-permute-done | bytes 1376288 | tf_op jit(solution)/shard_map/ppermute | solution.py:29
  111.2 14.1 %collective-permute-done.23.refs_2_ = bf16[8,21,16,256]{3,2,1,0:T(8,128)(2,1)} collective-permute-done((bf16[8,21,16,256]{3,2,1,0:T(8,128)(2,1)}, bf16[8,21,16,256]{3,2,1,0:T(8,128)(2,1)}, u32[]{:S(2)}, u32[]{:S(2)}) %collective-permute-start.23) | collective-permute-done | bytes 1376288 | tf_op jit(solution)/shard_map/ppermute | solution.py:29
  127.2 3.7 %firstsum.1 = (bf16[8,6,16,256]{3,2,1,0:T(8,128)(2,1)S(1)}, bf16[8,6,16,256]{3,2,1,0:T(8,128)(2,1)S(1)}, bf16[8,6,16,256]{3,2,1,0:T(8,128)(2,1)S(1)}, bf16[8,6,16,256]{3,2,1,0:T(8,128)(2,1)S(1)}) custom-call(s32[45]{0:T(128)S(1)} %concatenate.3.meta, bf16[8,21,16,256]{3,2,1,0:T(8,128)(2,1)S(1)} %copy-done, ...), custom_call_target="tpu_custom_call" | custom-call | flops 1048576 | bytes 6553600 | tf_op jit(solution)/shard_map/firstsum/pallas_call | solution.py:65
  130.9 2.7 %collective-permute-start.26 = (bf16[8,6,16,256]{3,2,1,0:T(8,128)(2,1)S(1)}, bf16[8,6,16,256]{3,2,1,0:T(8,128)(2,1)S(1)}, u32[]{:S(2)}, u32[]{:S(2)}) collective-permute-start(bf16[8,6,16,256]{3,2,1,0:T(8,128)(2,1)S(1)} %get-tuple-element.56), channel_id=1, source_target_pairs={{0,48},{8,200},{16,0},{24,216},{32,16},{40,232},{48,32},{56,248},{... | collective-permute-start | bytes 1179656 | tf_op jit(solution)/shard_map/ppermute | solution.py:29
  134.9 8.4 %collective-permute-done.25.prev = bf16[8,6,16,256]{3,2,1,0:T(8,128)(2,1)S(1)} collective-permute-done((bf16[8,6,16,256]{3,2,1,0:T(8,128)(2,1)S(1)}, bf16[8,6,16,256]{3,2,1,0:T(8,128)(2,1)S(1)}, u32[]{:S(2)}, u32[]{:S(2)}) %collective-permute-start.25) | collective-permute-done | bytes 393248 | tf_op jit(solution)/shard_map/ppermute | solution.py:29
  (56 shorter events, 35.8 us)
Async XLA Ops:
  9.2 15.3 %collective-permute-start.10 = (bf16[2,8,5,16,256]{4,3,2,1,0:T(8,128)(2,1)S(1)}, bf16[2,8,5,16,256]{4,3,2,1,0:T(8,128)(2,1)S(1)}, u32[]{:S(2)}, u32[]{:S(2)}) collective-permute-start(bf16[2,8,5,16,256]{4,3,2,1,0:T(8,128)(2,1)S(1)} %get-tuple-element.37.src.refs_9_), channel_id=1, source_target_pairs={{0,192},{8,72},{16,208},{24,88},{32,224},{40,104},{48,240},{56,120... | collective-permute-start | bytes 1966088 | tf_op jit(solution)/shard_map/ppermute | solution.py:29
  9.2 15.2 %collective-permute-start.9 = (bf16[2,8,5,16,256]{4,3,2,1,0:T(8,128)(2,1)S(1)}, bf16[2,8,5,16,256]{4,3,2,1,0:T(8,128)(2,1)S(1)}, u32[]{:S(2)}, u32[]{:S(2)}) collective-permute-start(bf16[2,8,5,16,256]{4,3,2,1,0:T(8,128)(2,1)S(1)} %get-tuple-element.37.src.refs_9_), channel_id=1, source_target_pairs={{0,16},{8,56},{16,32},{24,8},{32,48},{40,24},{48,0},{56,40},{64,80... | collective-permute-start | bytes 1966088 | tf_op jit(solution)/shard_map/ppermute | solution.py:29
  11.3 10.1 %collective-permute-start.4 = (bf16[256,512]{1,0:T(8,128)(2,1)S(1)}, bf16[256,512]{1,0:T(8,128)(2,1)S(1)}, u32[]{:S(2)}, u32[]{:S(2)}) collective-permute-start(bf16[256,512]{1,0:T(8,128)(2,1)S(1)} %get-tuple-element.36.refs_0_), channel_id=1, source_target_pairs={{0,7},{1,0},{2,1},{3,2},{4,3},{5,4},{6,5},{7,6},{8,15},{9,8},{10,9... | collective-permute-start | bytes 786440 | tf_op jit(solution)/shard_map/ppermute | solution.py:53
  16.9 7.6 %collective-permute-start.1 = (bf16[256,512]{1,0:T(8,128)(2,1)S(1)}, bf16[256,512]{1,0:T(8,128)(2,1)S(1)}, u32[]{:S(2)}, u32[]{:S(2)}) collective-permute-start(bf16[256,512]{1,0:T(8,128)(2,1)S(1)} %get-tuple-element.36.refs_0_), channel_id=1, source_target_pairs={{0,1},{1,2},{2,3},{3,4},{4,5},{5,6},{6,7},{7,0},{8,9},{9,10},{10,1... | collective-permute-start | bytes 786440 | tf_op jit(solution)/shard_map/ppermute | solution.py:53
  25.1 11.0 %collective-permute-start.11 = (bf16[2,8,5,16,256]{4,3,2,1,0:T(8,128)(2,1)S(1)}, bf16[2,8,5,16,256]{4,3,2,1,0:T(8,128)(2,1)S(1)}, u32[]{:S(2)}, u32[]{:S(2)}) collective-permute-start(bf16[2,8,5,16,256]{4,3,2,1,0:T(8,128)(2,1)S(1)} %hold.1), channel_id=1, source_target_pairs={{0,48},{8,24},{16,0},{24,40},{32,16},{40,56},{48,32},{56,8},{64,11... | collective-permute-start | bytes 1966088 | tf_op jit(solution)/shard_map/ppermute | solution.py:29
  25.2 10.9 %collective-permute-start.12 = (bf16[2,8,5,16,256]{4,3,2,1,0:T(8,128)(2,1)S(1)}, bf16[2,8,5,16,256]{4,3,2,1,0:T(8,128)(2,1)S(1)}, u32[]{:S(2)}, u32[]{:S(2)}) collective-permute-start(bf16[2,8,5,16,256]{4,3,2,1,0:T(8,128)(2,1)S(1)} %collective-permute-done.9.refs_0_.a.refs_10_), channel_id=1, source_target_pairs={{0,64},{8,200},{16,80},{24,216},{32,96},{40,232},{48,112},{56,248}... | collective-permute-start | bytes 1966088 | tf_op jit(solution)/shard_map/ppermute | solution.py:29
  36.7 7.5 %collective-permute-start.14 = (bf16[1,8,5,16,256]{4,3,2,1,0:T(8,128)(2,1)S(1)}, bf16[1,8,5,16,256]{4,3,2,1,0:T(8,128)(2,1)S(1)}, u32[]{:S(2)}, u32[]{:S(2)}) collective-permute-start(bf16[1,8,5,16,256]{4,3,2,1,0:T(8,128)(2,1)S(1)} %get-tuple-element.38), channel_id=1, source_target_pairs={{0,16},{8,56},{16,32},{24,8},{32,48},{40,24},{48,0},{56,40},{64,80... | collective-permute-start | bytes 983048 | tf_op jit(solution)/shard_map/ppermute | solution.py:29
  40.1 17.7 %collective-permute-start.13 = (bf16[2,8,5,16,256]{4,3,2,1,0:T(8,128)(2,1)S(1)}, bf16[2,8,5,16,256]{4,3,2,1,0:T(8,128)(2,1)S(1)}, u32[]{:S(2)}, u32[]{:S(2)}) collective-permute-start(bf16[2,8,5,16,256]{4,3,2,1,0:T(8,128)(2,1)S(1)} %collective-permute-done.11.c.refs_12_), channel_id=1, source_target_pairs={{0,192},{8,72},{16,208},{24,88},{32,224},{40,104},{48,240},{56,120... | collective-permute-start | bytes 1966088 | tf_op jit(solution)/shard_map/ppermute | solution.py:29
  40.4 10.2 %collective-permute-start.15 = (bf16[1,8,5,16,256]{4,3,2,1,0:T(8,128)(2,1)S(1)}, bf16[1,8,5,16,256]{4,3,2,1,0:T(8,128)(2,1)S(1)}, u32[]{:S(2)}, u32[]{:S(2)}) collective-permute-start(bf16[1,8,5,16,256]{4,3,2,1,0:T(8,128)(2,1)S(1)} %get-tuple-element.39), channel_id=1, source_target_pairs={{0,48},{8,24},{16,0},{24,40},{32,16},{40,56},{48,32},{56,8},{64,11... | collective-permute-start | bytes 983048 | tf_op jit(solution)/shard_map/ppermute | solution.py:29
  40.4 11.5 %collective-permute-start.6 = (bf16[256,512]{1,0:T(8,128)(2,1)S(1)}, bf16[256,512]{1,0:T(8,128)(2,1)S(1)}, u32[]{:S(2)}, u32[]{:S(2)}) collective-permute-start(bf16[256,512]{1,0:T(8,128)(2,1)S(1)} %collective-permute-done.5.refs_2_.refs_5_), channel_id=1, source_target_pairs={{0,7},{1,0},{2,1},{3,2},{4,3},{5,4},{6,5},{7,6},{8,15},{9,8},{10,9... | collective-permute-start | bytes 786440 | tf_op jit(solution)/shard_map/ppermute | solution.py:53
  40.5 12.0 %collective-permute-start.3 = (bf16[256,512]{1,0:T(8,128)(2,1)S(1)}, bf16[256,512]{1,0:T(8,128)(2,1)S(1)}, u32[]{:S(2)}, u32[]{:S(2)}) collective-permute-start(bf16[256,512]{1,0:T(8,128)(2,1)S(1)} %collective-permute-done.2.refs_1_.refs_2_), channel_id=1, source_target_pairs={{0,1},{1,2},{2,3},{3,4},{4,5},{5,6},{6,7},{7,0},{8,9},{9,10},{10,1... | collective-permute-start | bytes 786440 | tf_op jit(solution)/shard_map/ppermute | solution.py:53
  44.2 13.7 %collective-permute-start.16 = (bf16[1,8,5,16,256]{4,3,2,1,0:T(8,128)(2,1)S(1)}, bf16[1,8,5,16,256]{4,3,2,1,0:T(8,128)(2,1)S(1)}, u32[]{:S(2)}, u32[]{:S(2)}) collective-permute-start(bf16[1,8,5,16,256]{4,3,2,1,0:T(8,128)(2,1)S(1)} %collective-permute-done.14.refs_15_), channel_id=1, source_target_pairs={{0,64},{8,200},{16,80},{24,216},{32,96},{40,232},{48,112},{56,248}... | collective-permute-start | bytes 983048 | tf_op jit(solution)/shard_map/ppermute | solution.py:29
  50.6 9.5 %collective-permute-start.17 = (bf16[1,8,5,16,256]{4,3,2,1,0:T(8,128)(2,1)S(1)}, bf16[1,8,5,16,256]{4,3,2,1,0:T(8,128)(2,1)S(1)}, u32[]{:S(2)}, u32[]{:S(2)}) collective-permute-start(bf16[1,8,5,16,256]{4,3,2,1,0:T(8,128)(2,1)S(1)} %collective-permute-done.15.refs_16_), channel_id=1, source_target_pairs={{0,192},{8,72},{16,208},{24,88},{32,224},{40,104},{48,240},{56,120... | collective-permute-start | bytes 983048 | tf_op jit(solution)/shard_map/ppermute | solution.py:29
  64.3 13.3 %collective-permute-start.18 = (bf16[256,2048]{1,0:T(8,128)(2,1)S(1)}, bf16[256,2048]{1,0:T(8,128)(2,1)S(1)}, u32[]{:S(2)}, u32[]{:S(2)}) collective-permute-start(bf16[256,2048]{1,0:T(8,128)(2,1)S(1)} %get-tuple-element.41.mine), channel_id=1, source_target_pairs={{0,8},{8,0},{16,24},{24,16},{32,40},{40,32},{48,56},{56,48},{64,72... | collective-permute-start | bytes 3145736 | tf_op jit(solution)/shard_map/ppermute | solution.py:41
  66.5 7.2 %collective-permute-start.19 = (bf16[64,2048]{1,0:T(8,128)(2,1)S(1)}, bf16[64,2048]{1,0:T(8,128)(2,1)S(1)}, u32[]{:S(2)}, u32[]{:S(2)}) collective-permute-start(bf16[64,2048]{1,0:T(8,128)(2,1)S(1)} %get-tuple-element.42), channel_id=1, source_target_pairs={{0,24},{8,16},{16,40},{24,32},{32,56},{40,48},{48,72},{56,64},{64,... | collective-permute-start | bytes 786440 | tf_op jit(solution)/shard_map/ppermute | solution.py:49
  67.8 9.8 %collective-permute-start.20 = (bf16[64,2048]{1,0:T(8,128)(2,1)S(1)}, bf16[64,2048]{1,0:T(8,128)(2,1)S(1)}, u32[]{:S(2)}, u32[]{:S(2)}) collective-permute-start(bf16[64,2048]{1,0:T(8,128)(2,1)S(1)} %get-tuple-element.43), channel_id=1, source_target_pairs={{16,8},{24,0},{32,24},{40,16},{48,40},{56,32},{64,56},{72,48},{80,... | collective-permute-start | bytes 786440 | tf_op jit(solution)/shard_map/ppermute | solution.py:49
  86.1 10.1 %collective-permute-start.21 = (bf16[16,128,256]{2,1,0:T(8,128)(2,1)S(1)}, bf16[16,128,256]{2,1,0:T(8,128)(2,1)S(1)}, u32[]{:S(2)}, u32[]{:S(2)}) collective-permute-start(bf16[16,128,256]{2,1,0:T(8,128)(2,1)S(1)} %get-tuple-element.48), channel_id=1, source_target_pairs={{0,8},{8,0},{16,24},{24,16},{32,40},{40,32},{48,56},{56,48},{64,72... | collective-permute-start | bytes 3145736 | tf_op jit(solution)/shard_map/ppermute | solution.py:41
  89.0 22.2 %collective-permute-start.22 = (bf16[8,21,16,256]{3,2,1,0:T(8,128)(2,1)}, bf16[8,21,16,256]{3,2,1,0:T(8,128)(2,1)}, u32[]{:S(2)}, u32[]{:S(2)}) collective-permute-start(bf16[8,21,16,256]{3,2,1,0:T(8,128)(2,1)} %get-tuple-element.51), channel_id=1, source_target_pairs={{0,64},{8,24},{16,80},{24,40},{32,96},{40,56},{48,112},{56,8},{64,... | collective-permute-start | bytes 4128776 | tf_op jit(solution)/shard_map/ppermute | solution.py:29
  89.7 35.6 %collective-permute-start.23 = (bf16[8,21,16,256]{3,2,1,0:T(8,128)(2,1)}, bf16[8,21,16,256]{3,2,1,0:T(8,128)(2,1)}, u32[]{:S(2)}, u32[]{:S(2)}) collective-permute-start(bf16[8,21,16,256]{3,2,1,0:T(8,128)(2,1)} %get-tuple-element.52), channel_id=1, source_target_pairs={{0,192},{8,56},{16,208},{24,8},{32,224},{40,24},{48,240},{56,40},{... | collective-permute-start | bytes 4128776 | tf_op jit(solution)/shard_map/ppermute | solution.py:29
  95.0 32.1 %collective-permute-start.24 = (bf16[8,21,16,256]{3,2,1,0:T(8,128)(2,1)}, bf16[8,21,16,256]{3,2,1,0:T(8,128)(2,1)}, u32[]{:S(2)}, u32[]{:S(2)}) collective-permute-start(bf16[8,21,16,256]{3,2,1,0:T(8,128)(2,1)} %get-tuple-element.53), channel_id=1, source_target_pairs={{0,128},{8,40},{16,144},{24,56},{32,160},{40,8},{48,176},{56,24},{... | collective-permute-start | bytes 4128776 | tf_op jit(solution)/shard_map/ppermute | solution.py:29
  97.3 48.8 %all-to-all-start = ((bf16[16,128,256]{2,1,0:T(8,128)(2,1)}), bf16[16,128,256]{2,1,0:T(8,128)(2,1)S(1)}, u32[]{:S(2)}, u32[]{:S(2)}) async-start(bf16[16,128,256]{2,1,0:T(8,128)(2,1)} %broadcast_select_fusion.refs_4_), calls=%async_computation | async-start | bytes 2097152 | tf_op jit(solution)/shard_map/all_to_all | solution.py:456
  130.8 12.4 %collective-permute-start.25 = (bf16[8,6,16,256]{3,2,1,0:T(8,128)(2,1)S(1)}, bf16[8,6,16,256]{3,2,1,0:T(8,128)(2,1)S(1)}, u32[]{:S(2)}, u32[]{:S(2)}) collective-permute-start(bf16[8,6,16,256]{3,2,1,0:T(8,128)(2,1)S(1)} %get-tuple-element.55), channel_id=1, source_target_pairs={{0,16},{8,72},{16,32},{24,88},{32,48},{40,104},{48,0},{56,120},{64... | collective-permute-start | bytes 1179656 | tf_op jit(solution)/shard_map/ppermute | solution.py:29
  130.9 12.3 %collective-permute-start.26 = (bf16[8,6,16,256]{3,2,1,0:T(8,128)(2,1)S(1)}, bf16[8,6,16,256]{3,2,1,0:T(8,128)(2,1)S(1)}, u32[]{:S(2)}, u32[]{:S(2)}) collective-permute-start(bf16[8,6,16,256]{3,2,1,0:T(8,128)(2,1)S(1)} %get-tuple-element.56), channel_id=1, source_target_pairs={{0,48},{8,200},{16,0},{24,216},{32,16},{40,232},{48,32},{56,248},{... | collective-permute-start | bytes 1179656 | tf_op jit(solution)/shard_map/ppermute | solution.py:29
  133.6 9.7 %collective-permute-start.27 = (bf16[8,6,16,256]{3,2,1,0:T(8,128)(2,1)S(1)}, bf16[8,6,16,256]{3,2,1,0:T(8,128)(2,1)S(1)}, u32[]{:S(2)}, u32[]{:S(2)}) collective-permute-start(bf16[8,6,16,256]{3,2,1,0:T(8,128)(2,1)S(1)} %get-tuple-element.57), channel_id=1, source_target_pairs={{0,32},{8,136},{16,48},{24,152},{32,0},{40,168},{48,16},{56,184},{... | collective-permute-start | bytes 1179656 | tf_op jit(solution)/shard_map/ppermute | solution.py:29
  (8 other events, 85.3 us)

commit v5 on v1

--- a/solution.py
+++ b/solution.py
@@ -57,16 +57,18 @@
     return lax.dot_general(a, b, (dims, ((), ())), preferred_element_type=F32)
 
 
-def local(kernel, name, outs, args, scratch=(), flops=2**20, hbm=()):
-    shapes = [jax.ShapeDtypeStruct(s, t) for s, t in outs]
+def local(kernel, name, outs, args, scratch=(), flops=2**20, hbm=(), hbm_out=()):
+    shapes = [
+        pltpu.HBM(s, t) if i in hbm_out else jax.ShapeDtypeStruct(s, t) for i, (s, t) in enumerate(outs)
+    ]
     size = sum(a.size * a.dtype.itemsize for a in args[1:])
     return pl.pallas_call(
         kernel,
         out_shape=shapes,
         in_specs=[SMEM] + [HBM if i in hbm else VMEM for i in range(1, len(args))],
-        out_specs=[VMEM] * len(outs),
+        out_specs=[HBM if i in hbm_out else VMEM for i in range(len(outs))],
         scratch_shapes=list(scratch),
-        compiler_params=pltpu.CompilerParams(vmem_limit_bytes=14 * 2**20),
+        compiler_params=pltpu.CompilerParams(vmem_limit_bytes=20 * 2**20),
         cost_estimate=pl.CostEstimate(flops=flops, transcendentals=0, bytes_accessed=size),
         name=name,
     )(*args)
@@ -190,7 +192,7 @@
 
 
 def backward_kernel(meta, tok, got, mine, up, down, pre, taps, *refs):
-    g0, m1, m3, g1, g3, pgrad, conv, lhs, res, slab, moved = refs
+    g0, m1, m3, g1, g3, pgrad, conv, lhs, res, slab, moved, stage, sems = refs
     core, x, y = meta[CORE], meta[XPOS], meta[YPOS]
     is_in = core == 0
     slab[...] = jnp.zeros_like(slab)
@@ -245,8 +247,9 @@
             start = (here + d) % 4 * far
             for k in range(NNZ):
                 for s in range(4):
-                    out[at, k * 4 + s] = res[k, start + s * near]
-            out[at, KERN] = slab[...]
+                    stage[d, c, k * 4 + s] = res[k, start + s * near]
+            stage[d, c, KERN] = slab[...]
+            pltpu.make_async_copy(stage.at[d, c], out.at[at], sems.at[d]).start()
 
         emit(g0, 0, c)
 
@@ -261,6 +264,9 @@
             emit(m3, 2, c - SPLIT)
             emit(m1, 1, c)
             emit(g3, 3, c - SPLIT)
+
+    for d in range(4):
+        pltpu.make_async_copy(stage.at[d], g0, sems.at[d]).wait()
 
 
 def backward(meta, tok, got, mine, up, down, pre, taps):
@@ -272,10 +278,18 @@
         pltpu.VMEM((NNZ, 16, 16, BS), BF16),
         pltpu.VMEM((16, BS), BF16),
         pltpu.VMEM((18, PW, BS), F32),
+        pltpu.VMEM((4, COLS, KERN + 1, 16, BS), BF16),
+        pltpu.SemaphoreType.DMA((4,)),
     ]
     args = (meta, tok, got, mine, up, down, pre, taps)
     return local(
-        backward_kernel, "backward", outs, args, scratch, flops=2 * TOK * BS * BS * NNZ * COLS
+        backward_kernel,
+        "backward",
+        outs,
+        args,
+        scratch,
+        flops=2 * TOK * BS * BS * NNZ * COLS,
+        hbm_out=range(5),
     )
 
 
@@ -284,7 +298,7 @@
     def _():
         acc[...] = jnp.zeros_like(acc)
 
-        @pl.loop(0, COLS)
+        @pl.loop(0, COLS, unroll=2)
         def _(c):
             for k in range(NNZ):
                 wt = wts[c, k].reshape(BS, BS)
@@ -307,7 +321,8 @@
     )
 
 
-def gather_sum_kernel(meta, parts, out):
+def gather_sum_kernel(meta, parts, out, flag):
+    flag[...] = jnp.zeros_like(flag)
     for b in range(2):
         total = parts[b].astype(F32)
         for z in range(1, NZ):
@@ -422,7 +437,8 @@
     relayed = [((SPLIT, KERN + 2, 16, BS), BF16)] * 2
     r1, r3 = local(relay_kernel, "relay", relayed, (meta, g1, g3, m1, m3, terms), hbm=(5,))
     terms = lax.all_to_all(terms, "hid", 0, 0, tiled=True)
-    (grad_tokens,) = local(gather_sum_kernel, "gathersum", [((128, 512), BF16)], (meta, terms))
+    outs = [((128, 512), BF16), ((8, 128), F32)]
+    grad_tokens, flag = local(gather_sum_kernel, "gathersum", outs, (meta, terms))
 
     h = local(
         first_sum_kernel,
@@ -438,7 +454,7 @@
         place_kernel,
         "place",
         [out_shape, out_shape, ((9, 8 * BS), F32)],
-        (meta, kept, to_partner(sent), grad_tokens),
+        (meta, kept, to_partner(sent), flag),
     )
     grad_tokens = grad_tokens.reshape(1, 2, PW, 512)
     return grad_tokens, win.transpose(0, 2, 1, 3), wout.transpose(0, 2, 1, 3), kern

time: 148 us -> 145 us (0.980)
  local copies, waits for them, and re-layouts: 3.63 us -> 1.31 us
    unnamed x18 -> x14, local copies, waits for them, and re-layouts: 3.44 us -> 1.13 us
where the time goes in v5:
time: 145 us
  waiting for transfers between devices  64.2 us (44%)
  starting transfers between devices  54.4 us (38%)
  Pallas kernels  20.5 us (14%)
  other arithmetic  3.57 us (2%)
    ppermute x16, waiting for transfers between devices, by_core(): return lax.ppermute(value, ('crop', 'rows'), pairs)  38.3 us
    ppermute x16, starting transfers between devices, by_core(): return lax.ppermute(value, ('crop', 'rows'), pairs)  24.7 us
    pallas_call x10, Pallas kernels, local(): pl.pallas_call(kernel, out_shape=shapes, in_specs=[SMEM] + [HBM if i in h...  20.5 us
    ppermute x8, waiting for transfers between devices, along_z(): return lax.ppermute(value, 'hid', [(z, (z + step) % NZ) for z in range(NZ)])  17.1 us
    ppermute x5, starting transfers between devices, to_partner(): return lax.ppermute(value, 'rows', [(r, r ^ 1) for r in range(16)])  12.5 us
    ppermute x8, starting transfers between devices, along_z(): return lax.ppermute(value, 'hid', [(z, (z + step) % NZ) for z in range(NZ)])  10.2 us
    ppermute x2, waiting for transfers between devices, to_next_chip(): return lax.ppermute(value, 'rows', pairs)  8.54 us
    all_to_all x1, starting transfers between devices, on_device(): terms = lax.all_to_all(terms, 'hid', 0, 0, tiled=True)  4.37 us
  transfers between devices with their start and end apart: 32, of which 16 were waited for; matrix products, arithmetic and copies ran while one was open for 2% of the time, Pallas kernels for 3%

profile of v5, /device:TPU:1, one launch (start us, length us, event | category | flops | bytes accessed | tf_op | source)
XLA Modules:
  0.0 144.9 jit_solution(18198941327109486566)
XLA Ops:
  1.9 3.3 %collective-permute-start.9 = (bf16[8,5,16,256]{3,2,1,0:T(8,128)(2,1)S(1)}, bf16[8,5,16,256]{3,2,1,0:T(8,128)(2,1)S(1)}, u32[]{:S(2)}, u32[]{:S(2)}) collective-permute-start(bf16[8,5,16,256]{3,2,1,0:T(8,128)(2,1)S(1)} %select_bitcast_fusion), channel_id=1, source_target_pairs={{0,8},{8,0},{16,24},{24,16},{32,40},{40,32},{48,56},{56,48},{64,72... | collective-permute-start | bytes 983048 | tf_op jit(solution)/shard_map/ppermute | solution.py:41
  8.9 5.7 %collective-permute-start.4 = (bf16[256,512]{1,0:T(8,128)(2,1)S(1)}, bf16[256,512]{1,0:T(8,128)(2,1)S(1)}, u32[]{:S(2)}, u32[]{:S(2)}) collective-permute-start(bf16[256,512]{1,0:T(8,128)(2,1)S(1)} %pad_maximum_fusion.1.refs_0_), channel_id=1, source_target_pairs={{0,7},{1,0},{2,1},{3,2},{4,3},{5,4},{6,5},{7,6},{8,15},{9,8},{10,9... | collective-permute-start | bytes 786440 | tf_op jit(solution)/shard_map/ppermute | solution.py:53
  14.7 4.3 %collective-permute-done.4.refs_3_.refs_4_ = bf16[256,512]{1,0:T(8,128)(2,1)S(1)} collective-permute-done((bf16[256,512]{1,0:T(8,128)(2,1)S(1)}, bf16[256,512]{1,0:T(8,128)(2,1)S(1)}, u32[]{:S(2)}, u32[]{:S(2)}) %collective-permute-start.4) | collective-permute-done | bytes 262176 | tf_op jit(solution)/shard_map/ppermute | solution.py:53
  19.0 3.1 %collective-permute-done.1.refs_2_.refs_1_ = bf16[256,512]{1,0:T(8,128)(2,1)S(1)} collective-permute-done((bf16[256,512]{1,0:T(8,128)(2,1)S(1)}, bf16[256,512]{1,0:T(8,128)(2,1)S(1)}, u32[]{:S(2)}, u32[]{:S(2)}) %collective-permute-start.1) | collective-permute-done | bytes 262176 | tf_op jit(solution)/shard_map/ppermute | solution.py:53
  22.9 2.8 %collective-permute-start.13 = (bf16[2,8,5,16,256]{4,3,2,1,0:T(8,128)(2,1)S(1)}, bf16[2,8,5,16,256]{4,3,2,1,0:T(8,128)(2,1)S(1)}, u32[]{:S(2)}, u32[]{:S(2)}) collective-permute-start(bf16[2,8,5,16,256]{4,3,2,1,0:T(8,128)(2,1)S(1)} %collective-permute-done.10.refs_0_.a.refs_10_), channel_id=1, source_target_pairs={{0,64},{8,200},{16,80},{24,216},{32,96},{40,232},{48,112},{56,248}... | collective-permute-start | bytes 1966088 | tf_op jit(solution)/shard_map/ppermute | solution.py:29
  27.1 4.4 %collective-permute-done.5.refs_2_.refs_5_ = bf16[256,512]{1,0:T(8,128)(2,1)S(1)} collective-permute-done((bf16[256,512]{1,0:T(8,128)(2,1)S(1)}, bf16[256,512]{1,0:T(8,128)(2,1)S(1)}, u32[]{:S(2)}, u32[]{:S(2)}) %collective-permute-start.5) | collective-permute-done | bytes 262176 | tf_op jit(solution)/shard_map/ppermute | solution.py:53
  34.4 3.6 %collective-permute-start.15 = (bf16[1,8,5,16,256]{4,3,2,1,0:T(8,128)(2,1)S(1)}, bf16[1,8,5,16,256]{4,3,2,1,0:T(8,128)(2,1)S(1)}, u32[]{:S(2)}, u32[]{:S(2)}) collective-permute-start(bf16[1,8,5,16,256]{4,3,2,1,0:T(8,128)(2,1)S(1)} %get-tuple-element.33), channel_id=1, source_target_pairs={{0,16},{8,56},{16,32},{24,8},{32,48},{40,24},{48,0},{56,40},{64,80... | collective-permute-start | bytes 983048 | tf_op jit(solution)/shard_map/ppermute | solution.py:29
  39.6 2.4 %collective-permute-done.15.refs_15_ = bf16[1,8,5,16,256]{4,3,2,1,0:T(8,128)(2,1)S(1)} collective-permute-done((bf16[1,8,5,16,256]{4,3,2,1,0:T(8,128)(2,1)S(1)}, bf16[1,8,5,16,256]{4,3,2,1,0:T(8,128)(2,1)S(1)}, u32[]{:S(2)}, u32[]{:S(2)}) %collective-permute-start.15) | collective-permute-done | bytes 327712 | tf_op jit(solution)/shard_map/ppermute | solution.py:29
  43.8 4.5 %collective-permute-done.16.refs_16_ = bf16[1,8,5,16,256]{4,3,2,1,0:T(8,128)(2,1)S(1)} collective-permute-done((bf16[1,8,5,16,256]{4,3,2,1,0:T(8,128)(2,1)S(1)}, bf16[1,8,5,16,256]{4,3,2,1,0:T(8,128)(2,1)S(1)}, u32[]{:S(2)}, u32[]{:S(2)}) %collective-permute-start.16) | collective-permute-done | bytes 327712 | tf_op jit(solution)/shard_map/ppermute | solution.py:29
  51.3 2.5 %collective-permute-done.8.refs_8_ = bf16[128,512]{1,0:T(8,128)(2,1)S(1)} collective-permute-done((bf16[128,512]{1,0:T(8,128)(2,1)S(1)}, bf16[128,512]{1,0:T(8,128)(2,1)S(1)}, u32[]{:S(2)}, u32[]{:S(2)}) %collective-permute-start.8) | collective-permute-done | bytes 131104 | tf_op jit(solution)/shard_map/ppermute | solution.py:53
  55.4 2.1 %collective-permute-done.18.refs_18_ = bf16[1,8,5,16,256]{4,3,2,1,0:T(8,128)(2,1)S(1)} collective-permute-done((bf16[1,8,5,16,256]{4,3,2,1,0:T(8,128)(2,1)S(1)}, bf16[1,8,5,16,256]{4,3,2,1,0:T(8,128)(2,1)S(1)}, u32[]{:S(2)}, u32[]{:S(2)}) %collective-permute-start.18) | collective-permute-done | bytes 327712 | tf_op jit(solution)/shard_map/ppermute | solution.py:29
  57.6 4.3 %forward.1 = (f32[256,2048]{1,0:T(8,128)S(1)}, bf16[256,2048]{1,0:T(8,128)(2,1)S(1)}, bf16[64,2048]{1,0:T(8,128)(2,1)S(1)}, bf16[64,2048]{1,0:T(8,128)(2,1)S(1)}...) custom-call(s32[45]{0:T(128)S(1)} %concatenate.6.meta, ...), custom_call_target="tpu_custom_call" | custom-call | flops 1342177280 | bytes 7340032 | tf_op jit(solution)/shard_map/forward/pallas_call | solution.py:65
  61.8 2.2 %collective-permute-start.19 = (bf16[256,2048]{1,0:T(8,128)(2,1)S(1)}, bf16[256,2048]{1,0:T(8,128)(2,1)S(1)}, u32[]{:S(2)}, u32[]{:S(2)}) collective-permute-start(bf16[256,2048]{1,0:T(8,128)(2,1)S(1)} %get-tuple-element.36.mine), channel_id=1, source_target_pairs={{0,8},{8,0},{16,24},{24,16},{32,40},{40,32},{48,56},{56,48},{64,72... | collective-permute-start | bytes 3145736 | tf_op jit(solution)/shard_map/ppermute | solution.py:41
  66.7 4.6 %collective-permute-done.20.up = bf16[64,2048]{1,0:T(8,128)(2,1)S(1)} collective-permute-done((bf16[64,2048]{1,0:T(8,128)(2,1)S(1)}, bf16[64,2048]{1,0:T(8,128)(2,1)S(1)}, u32[]{:S(2)}, u32[]{:S(2)}) %collective-permute-start.20) | collective-permute-done | bytes 262176 | tf_op jit(solution)/shard_map/ppermute | solution.py:49
  71.3 4.0 %collective-permute-done.21.down = bf16[64,2048]{1,0:T(8,128)(2,1)S(1)} collective-permute-done((bf16[64,2048]{1,0:T(8,128)(2,1)S(1)}, bf16[64,2048]{1,0:T(8,128)(2,1)S(1)}, u32[]{:S(2)}, u32[]{:S(2)}) %collective-permute-start.21) | collective-permute-done | bytes 262176 | tf_op jit(solution)/shard_map/ppermute | solution.py:49
  75.2 8.1 %backward.1 = (bf16[8,21,16,256]{3,2,1,0:T(8,128)(2,1)}, bf16[8,21,16,256]{3,2,1,0:T(8,128)(2,1)}, bf16[8,21,16,256]{3,2,1,0:T(8,128)(2,1)}, bf16[4,21,16,256]{3...) custom-call(s32[45]{0:T(128)S(1)} %concatenate.6.meta, ...), custom_call_target="tpu_custom_call" | custom-call | flops 1342177280 | bytes 6889472 | tf_op jit(solution)/shard_map/backward/pallas_call | solution.py:65
  83.9 2.8 %collective-permute-start.22 = (bf16[16,128,256]{2,1,0:T(8,128)(2,1)S(1)}, bf16[16,128,256]{2,1,0:T(8,128)(2,1)S(1)}, u32[]{:S(2)}, u32[]{:S(2)}) collective-permute-start(bf16[16,128,256]{2,1,0:T(8,128)(2,1)S(1)} %get-tuple-element.43), channel_id=1, source_target_pairs={{0,8},{8,0},{16,24},{24,16},{32,40},{40,32},{48,56},{56,48},{64,72... | collective-permute-start | bytes 3145736 | tf_op jit(solution)/shard_map/ppermute | solution.py:41
  87.4 5.3 %collective-permute-start.24 = (bf16[8,21,16,256]{3,2,1,0:T(8,128)(2,1)}, bf16[8,21,16,256]{3,2,1,0:T(8,128)(2,1)S(1)}, u32[]{:S(2)}, u32[]{:S(2)}) collective-permute-start(bf16[8,21,16,256]{3,2,1,0:T(8,128)(2,1)} %get-tuple-element.47), channel_id=1, source_target_pairs={{0,192},{8,56},{16,208},{24,8},{32,224},{40,24},{48,240},{56,40},{... | collective-permute-start | bytes 4128776 | tf_op jit(solution)/shard_map/ppermute | solution.py:29
  93.9 4.4 %all-to-all-start = ((bf16[16,128,256]{2,1,0:T(8,128)(2,1)}), bf16[16,128,256]{2,1,0:T(8,128)(2,1)}, u32[]{:S(2)}, u32[]{:S(2)}) async-start(bf16[16,128,256]{2,1,0:T(8,128)(2,1)} %broadcast_select_fusion._), calls=%async_computation | async-start | bytes 2097152 | tf_op jit(solution)/shard_map/all_to_all | solution.py:439
  98.2 10.8 %collective-permute-done.23.m1 = bf16[8,21,16,256]{3,2,1,0:T(8,128)(2,1)S(1)} collective-permute-done((bf16[8,21,16,256]{3,2,1,0:T(8,128)(2,1)}, bf16[8,21,16,256]{3,2,1,0:T(8,128)(2,1)S(1)}, u32[]{:S(2)}, u32[]{:S(2)}) %collective-permute-start.23) | collective-permute-done | bytes 1376288 | tf_op jit(solution)/shard_map/ppermute | solution.py:29
  113.9 9.0 %collective-permute-done.25.p1 = bf16[4,22,16,256]{3,2,1,0:T(8,128)(2,1)S(1)} collective-permute-done((bf16[4,22,16,256]{3,2,1,0:T(8,128)(2,1)S(1)}, bf16[4,22,16,256]{3,2,1,0:T(8,128)(2,1)S(1)}, u32[]{:S(2)}, u32[]{:S(2)}) %collective-permute-start.25) | collective-permute-done | bytes 720928 | tf_op jit(solution)/shard_map/ppermute | solution.py:29
  124.1 2.7 %collective-permute-start.28 = (bf16[8,6,16,256]{3,2,1,0:T(8,128)(2,1)S(1)}, bf16[8,6,16,256]{3,2,1,0:T(8,128)(2,1)S(1)}, u32[]{:S(2)}, u32[]{:S(2)}) collective-permute-start(bf16[8,6,16,256]{3,2,1,0:T(8,128)(2,1)S(1)} %get-tuple-element.54), channel_id=1, source_target_pairs={{0,48},{8,200},{16,0},{24,216},{32,16},{40,232},{48,32},{56,248},{... | collective-permute-start | bytes 1179656 | tf_op jit(solution)/shard_map/ppermute | solution.py:29
  128.0 8.4 %collective-permute-done.27.prev = bf16[8,6,16,256]{3,2,1,0:T(8,128)(2,1)S(1)} collective-permute-done((bf16[8,6,16,256]{3,2,1,0:T(8,128)(2,1)S(1)}, bf16[8,6,16,256]{3,2,1,0:T(8,128)(2,1)S(1)}, u32[]{:S(2)}, u32[]{:S(2)}) %collective-permute-start.27) | collective-permute-done | bytes 393248 | tf_op jit(solution)/shard_map/ppermute | solution.py:29
  137.2 4.0 %collective-permute-start.30 = (bf16[8,7,8,256]{3,2,1,0:T(8,128)(2,1)S(1)}, bf16[8,7,8,256]{3,2,1,0:T(8,128)(2,1)S(1)}, u32[]{:S(2)}, u32[]{:S(2)}) collective-permute-start(bf16[8,7,8,256]{3,2,1,0:T(8,128)(2,1)S(1)} %get-tuple-element.57), channel_id=1, source_target_pairs={{0,8},{8,0},{16,24},{24,16},{32,40},{40,32},{48,56},{56,48},{64,72... | collective-permute-start | bytes 688136 | tf_op jit(solution)/shard_map/ppermute | solution.py:41
  (75 shorter events, 34.7 us)
Async XLA Ops:
  6.7 15.5 %collective-permute-start.11 = (bf16[2,8,5,16,256]{4,3,2,1,0:T(8,128)(2,1)S(1)}, bf16[2,8,5,16,256]{4,3,2,1,0:T(8,128)(2,1)S(1)}, u32[]{:S(2)}, u32[]{:S(2)}) collective-permute-start(bf16[2,8,5,16,256]{4,3,2,1,0:T(8,128)(2,1)S(1)} %pad_maximum_fusion.src.refs_9_), channel_id=1, source_target_pairs={{0,192},{8,72},{16,208},{24,88},{32,224},{40,104},{48,240},{56,120... | collective-permute-start | bytes 1966088 | tf_op jit(solution)/shard_map/ppermute | solution.py:29
  6.8 15.4 %collective-permute-start.10 = (bf16[2,8,5,16,256]{4,3,2,1,0:T(8,128)(2,1)S(1)}, bf16[2,8,5,16,256]{4,3,2,1,0:T(8,128)(2,1)S(1)}, u32[]{:S(2)}, u32[]{:S(2)}) collective-permute-start(bf16[2,8,5,16,256]{4,3,2,1,0:T(8,128)(2,1)S(1)} %pad_maximum_fusion.src.refs_9_), channel_id=1, source_target_pairs={{0,16},{8,56},{16,32},{24,8},{32,48},{40,24},{48,0},{56,40},{64,80... | collective-permute-start | bytes 1966088 | tf_op jit(solution)/shard_map/ppermute | solution.py:29
  8.9 10.1 %collective-permute-start.4 = (bf16[256,512]{1,0:T(8,128)(2,1)S(1)}, bf16[256,512]{1,0:T(8,128)(2,1)S(1)}, u32[]{:S(2)}, u32[]{:S(2)}) collective-permute-start(bf16[256,512]{1,0:T(8,128)(2,1)S(1)} %pad_maximum_fusion.1.refs_0_), channel_id=1, source_target_pairs={{0,7},{1,0},{2,1},{3,2},{4,3},{5,4},{6,5},{7,6},{8,15},{9,8},{10,9... | collective-permute-start | bytes 786440 | tf_op jit(solution)/shard_map/ppermute | solution.py:53
  14.5 7.6 %collective-permute-start.1 = (bf16[256,512]{1,0:T(8,128)(2,1)S(1)}, bf16[256,512]{1,0:T(8,128)(2,1)S(1)}, u32[]{:S(2)}, u32[]{:S(2)}) collective-permute-start(bf16[256,512]{1,0:T(8,128)(2,1)S(1)} %pad_maximum_fusion.1.refs_0_), channel_id=1, source_target_pairs={{0,1},{1,2},{2,3},{3,4},{4,5},{5,6},{6,7},{7,0},{8,9},{9,10},{10,1... | collective-permute-start | bytes 786440 | tf_op jit(solution)/shard_map/ppermute | solution.py:53
  22.8 11.0 %collective-permute-start.12 = (bf16[2,8,5,16,256]{4,3,2,1,0:T(8,128)(2,1)S(1)}, bf16[2,8,5,16,256]{4,3,2,1,0:T(8,128)(2,1)S(1)}, u32[]{:S(2)}, u32[]{:S(2)}) collective-permute-start(bf16[2,8,5,16,256]{4,3,2,1,0:T(8,128)(2,1)S(1)} %hold.1), channel_id=1, source_target_pairs={{0,48},{8,24},{16,0},{24,40},{32,16},{40,56},{48,32},{56,8},{64,11... | collective-permute-start | bytes 1966088 | tf_op jit(solution)/shard_map/ppermute | solution.py:29
  22.9 10.9 %collective-permute-start.13 = (bf16[2,8,5,16,256]{4,3,2,1,0:T(8,128)(2,1)S(1)}, bf16[2,8,5,16,256]{4,3,2,1,0:T(8,128)(2,1)S(1)}, u32[]{:S(2)}, u32[]{:S(2)}) collective-permute-start(bf16[2,8,5,16,256]{4,3,2,1,0:T(8,128)(2,1)S(1)} %collective-permute-done.10.refs_0_.a.refs_10_), channel_id=1, source_target_pairs={{0,64},{8,200},{16,80},{24,216},{32,96},{40,232},{48,112},{56,248}... | collective-permute-start | bytes 1966088 | tf_op jit(solution)/shard_map/ppermute | solution.py:29
  34.4 7.6 %collective-permute-start.15 = (bf16[1,8,5,16,256]{4,3,2,1,0:T(8,128)(2,1)S(1)}, bf16[1,8,5,16,256]{4,3,2,1,0:T(8,128)(2,1)S(1)}, u32[]{:S(2)}, u32[]{:S(2)}) collective-permute-start(bf16[1,8,5,16,256]{4,3,2,1,0:T(8,128)(2,1)S(1)} %get-tuple-element.33), channel_id=1, source_target_pairs={{0,16},{8,56},{16,32},{24,8},{32,48},{40,24},{48,0},{56,40},{64,80... | collective-permute-start | bytes 983048 | tf_op jit(solution)/shard_map/ppermute | solution.py:29
  38.0 17.4 %collective-permute-start.14 = (bf16[2,8,5,16,256]{4,3,2,1,0:T(8,128)(2,1)S(1)}, bf16[2,8,5,16,256]{4,3,2,1,0:T(8,128)(2,1)S(1)}, u32[]{:S(2)}, u32[]{:S(2)}) collective-permute-start(bf16[2,8,5,16,256]{4,3,2,1,0:T(8,128)(2,1)S(1)} %collective-permute-done.12.c.refs_12_), channel_id=1, source_target_pairs={{0,192},{8,72},{16,208},{24,88},{32,224},{40,104},{48,240},{56,120... | collective-permute-start | bytes 1966088 | tf_op jit(solution)/shard_map/ppermute | solution.py:29
  38.1 10.2 %collective-permute-start.16 = (bf16[1,8,5,16,256]{4,3,2,1,0:T(8,128)(2,1)S(1)}, bf16[1,8,5,16,256]{4,3,2,1,0:T(8,128)(2,1)S(1)}, u32[]{:S(2)}, u32[]{:S(2)}) collective-permute-start(bf16[1,8,5,16,256]{4,3,2,1,0:T(8,128)(2,1)S(1)} %get-tuple-element.34), channel_id=1, source_target_pairs={{0,48},{8,24},{16,0},{24,40},{32,16},{40,56},{48,32},{56,8},{64,11... | collective-permute-start | bytes 983048 | tf_op jit(solution)/shard_map/ppermute | solution.py:29
  38.1 11.5 %collective-permute-start.6 = (bf16[256,512]{1,0:T(8,128)(2,1)S(1)}, bf16[256,512]{1,0:T(8,128)(2,1)S(1)}, u32[]{:S(2)}, u32[]{:S(2)}) collective-permute-start(bf16[256,512]{1,0:T(8,128)(2,1)S(1)} %collective-permute-done.5.refs_2_.refs_5_), channel_id=1, source_target_pairs={{0,7},{1,0},{2,1},{3,2},{4,3},{5,4},{6,5},{7,6},{8,15},{9,8},{10,9... | collective-permute-start | bytes 786440 | tf_op jit(solution)/shard_map/ppermute | solution.py:53
  38.3 11.7 %collective-permute-start.3 = (bf16[256,512]{1,0:T(8,128)(2,1)S(1)}, bf16[256,512]{1,0:T(8,128)(2,1)S(1)}, u32[]{:S(2)}, u32[]{:S(2)}) collective-permute-start(bf16[256,512]{1,0:T(8,128)(2,1)S(1)} %collective-permute-done.2.refs_1_.refs_2_), channel_id=1, source_target_pairs={{0,1},{1,2},{2,3},{3,4},{4,5},{5,6},{6,7},{7,0},{8,9},{9,10},{10,1... | collective-permute-start | bytes 786440 | tf_op jit(solution)/shard_map/ppermute | solution.py:53
  42.0 13.4 %collective-permute-start.17 = (bf16[1,8,5,16,256]{4,3,2,1,0:T(8,128)(2,1)S(1)}, bf16[1,8,5,16,256]{4,3,2,1,0:T(8,128)(2,1)S(1)}, u32[]{:S(2)}, u32[]{:S(2)}) collective-permute-start(bf16[1,8,5,16,256]{4,3,2,1,0:T(8,128)(2,1)S(1)} %collective-permute-done.15.refs_15_), channel_id=1, source_target_pairs={{0,64},{8,200},{16,80},{24,216},{32,96},{40,232},{48,112},{56,248}... | collective-permute-start | bytes 983048 | tf_op jit(solution)/shard_map/ppermute | solution.py:29
  48.3 9.3 %collective-permute-start.18 = (bf16[1,8,5,16,256]{4,3,2,1,0:T(8,128)(2,1)S(1)}, bf16[1,8,5,16,256]{4,3,2,1,0:T(8,128)(2,1)S(1)}, u32[]{:S(2)}, u32[]{:S(2)}) collective-permute-start(bf16[1,8,5,16,256]{4,3,2,1,0:T(8,128)(2,1)S(1)} %collective-permute-done.16.refs_16_), channel_id=1, source_target_pairs={{0,192},{8,72},{16,208},{24,88},{32,224},{40,104},{48,240},{56,120... | collective-permute-start | bytes 983048 | tf_op jit(solution)/shard_map/ppermute | solution.py:29
  61.8 13.4 %collective-permute-start.19 = (bf16[256,2048]{1,0:T(8,128)(2,1)S(1)}, bf16[256,2048]{1,0:T(8,128)(2,1)S(1)}, u32[]{:S(2)}, u32[]{:S(2)}) collective-permute-start(bf16[256,2048]{1,0:T(8,128)(2,1)S(1)} %get-tuple-element.36.mine), channel_id=1, source_target_pairs={{0,8},{8,0},{16,24},{24,16},{32,40},{40,32},{48,56},{56,48},{64,72... | collective-permute-start | bytes 3145736 | tf_op jit(solution)/shard_map/ppermute | solution.py:41
  65.4 9.8 %collective-permute-start.21 = (bf16[64,2048]{1,0:T(8,128)(2,1)S(1)}, bf16[64,2048]{1,0:T(8,128)(2,1)S(1)}, u32[]{:S(2)}, u32[]{:S(2)}) collective-permute-start(bf16[64,2048]{1,0:T(8,128)(2,1)S(1)} %get-tuple-element.38), channel_id=1, source_target_pairs={{16,8},{24,0},{32,24},{40,16},{48,40},{56,32},{64,56},{72,48},{80,... | collective-permute-start | bytes 786440 | tf_op jit(solution)/shard_map/ppermute | solution.py:49
  83.9 8.8 %collective-permute-start.22 = (bf16[16,128,256]{2,1,0:T(8,128)(2,1)S(1)}, bf16[16,128,256]{2,1,0:T(8,128)(2,1)S(1)}, u32[]{:S(2)}, u32[]{:S(2)}) collective-permute-start(bf16[16,128,256]{2,1,0:T(8,128)(2,1)S(1)} %get-tuple-element.43), channel_id=1, source_target_pairs={{0,8},{8,0},{16,24},{24,16},{32,40},{40,32},{48,56},{56,48},{64,72... | collective-permute-start | bytes 3145736 | tf_op jit(solution)/shard_map/ppermute | solution.py:41
  86.7 22.3 %collective-permute-start.23 = (bf16[8,21,16,256]{3,2,1,0:T(8,128)(2,1)}, bf16[8,21,16,256]{3,2,1,0:T(8,128)(2,1)S(1)}, u32[]{:S(2)}, u32[]{:S(2)}) collective-permute-start(bf16[8,21,16,256]{3,2,1,0:T(8,128)(2,1)} %get-tuple-element.46), channel_id=1, source_target_pairs={{0,64},{8,24},{16,80},{24,40},{32,96},{40,56},{48,112},{56,8},{64,... | collective-permute-start | bytes 4128776 | tf_op jit(solution)/shard_map/ppermute | solution.py:29
  87.4 21.6 %collective-permute-start.24 = (bf16[8,21,16,256]{3,2,1,0:T(8,128)(2,1)}, bf16[8,21,16,256]{3,2,1,0:T(8,128)(2,1)S(1)}, u32[]{:S(2)}, u32[]{:S(2)}) collective-permute-start(bf16[8,21,16,256]{3,2,1,0:T(8,128)(2,1)} %get-tuple-element.47), channel_id=1, source_target_pairs={{0,192},{8,56},{16,208},{24,8},{32,224},{40,24},{48,240},{56,40},{... | collective-permute-start | bytes 4128776 | tf_op jit(solution)/shard_map/ppermute | solution.py:29
  93.9 47.4 %all-to-all-start = ((bf16[16,128,256]{2,1,0:T(8,128)(2,1)}), bf16[16,128,256]{2,1,0:T(8,128)(2,1)}, u32[]{:S(2)}, u32[]{:S(2)}) async-start(bf16[16,128,256]{2,1,0:T(8,128)(2,1)} %broadcast_select_fusion._), calls=%async_computation | async-start | bytes 2097152 | tf_op jit(solution)/shard_map/all_to_all | solution.py:439
  111.0 11.8 %collective-permute-start.25 = (bf16[4,22,16,256]{3,2,1,0:T(8,128)(2,1)S(1)}, bf16[4,22,16,256]{3,2,1,0:T(8,128)(2,1)S(1)}, u32[]{:S(2)}, u32[]{:S(2)}) collective-permute-start(bf16[4,22,16,256]{3,2,1,0:T(8,128)(2,1)S(1)} %get-tuple-element.50), channel_id=1, source_target_pairs={{0,64},{8,24},{16,80},{24,40},{32,96},{40,56},{48,112},{56,8},{64,... | collective-permute-start | bytes 2162696 | tf_op jit(solution)/shard_map/ppermute | solution.py:29
  112.0 10.9 %collective-permute-start.26 = (bf16[4,22,16,256]{3,2,1,0:T(8,128)(2,1)S(1)}, bf16[4,22,16,256]{3,2,1,0:T(8,128)(2,1)S(1)}, u32[]{:S(2)}, u32[]{:S(2)}) collective-permute-start(bf16[4,22,16,256]{3,2,1,0:T(8,128)(2,1)S(1)} %get-tuple-element.51), channel_id=1, source_target_pairs={{0,192},{8,56},{16,208},{24,8},{32,224},{40,24},{48,240},{56,40},{... | collective-permute-start | bytes 2162696 | tf_op jit(solution)/shard_map/ppermute | solution.py:29
  124.0 12.4 %collective-permute-start.27 = (bf16[8,6,16,256]{3,2,1,0:T(8,128)(2,1)S(1)}, bf16[8,6,16,256]{3,2,1,0:T(8,128)(2,1)S(1)}, u32[]{:S(2)}, u32[]{:S(2)}) collective-permute-start(bf16[8,6,16,256]{3,2,1,0:T(8,128)(2,1)S(1)} %get-tuple-element.53), channel_id=1, source_target_pairs={{0,16},{8,72},{16,32},{24,88},{32,48},{40,104},{48,0},{56,120},{64... | collective-permute-start | bytes 1179656 | tf_op jit(solution)/shard_map/ppermute | solution.py:29
  124.1 12.3 %collective-permute-start.28 = (bf16[8,6,16,256]{3,2,1,0:T(8,128)(2,1)S(1)}, bf16[8,6,16,256]{3,2,1,0:T(8,128)(2,1)S(1)}, u32[]{:S(2)}, u32[]{:S(2)}) collective-permute-start(bf16[8,6,16,256]{3,2,1,0:T(8,128)(2,1)S(1)} %get-tuple-element.54), channel_id=1, source_target_pairs={{0,48},{8,200},{16,0},{24,216},{32,16},{40,232},{48,32},{56,248},{... | collective-permute-start | bytes 1179656 | tf_op jit(solution)/shard_map/ppermute | solution.py:29
  126.7 9.7 %collective-permute-start.29 = (bf16[8,6,16,256]{3,2,1,0:T(8,128)(2,1)S(1)}, bf16[8,6,16,256]{3,2,1,0:T(8,128)(2,1)S(1)}, u32[]{:S(2)}, u32[]{:S(2)}) collective-permute-start(bf16[8,6,16,256]{3,2,1,0:T(8,128)(2,1)S(1)} %get-tuple-element.55), channel_id=1, source_target_pairs={{0,32},{8,136},{16,48},{24,152},{32,0},{40,168},{48,16},{56,184},{... | collective-permute-start | bytes 1179656 | tf_op jit(solution)/shard_map/ppermute | solution.py:29
  (15 other events, 116.5 us)

commit v6 on v5

--- a/solution.py
+++ b/solution.py
@@ -12,7 +12,7 @@
 F32, BF16 = jnp.float32, jnp.bfloat16
 NX, NY, NZ = 4, 4, 8
 COLS, NNZ, BS, PW = 8, 5, 256, 64
-TOK, KERN, SPLIT = 256, 20, 4
+TOK, KERN, SPLIT, PARTS = 256, 20, 4, 2
 CORE, XPOS, YPOS, YLO, ZPOS = 40, 41, 42, 43, 44
 HBM = pl.BlockSpec(memory_space=pltpu.MemorySpace.HBM)
 VMEM = pl.BlockSpec(memory_space=pltpu.VMEM)
@@ -293,7 +293,9 @@
     )
 
 
-def token_grad_kernel(meta, pgrad, wts, keep, send, acc):
+def token_grad_kernel(meta, pgrad, wts, keep, *refs):
+    *sends, acc = refs
+
     @pl.when(meta[CORE] == 0)
     def _():
         acc[...] = jnp.zeros_like(acc)
@@ -304,17 +306,20 @@
                 wt = wts[c, k].reshape(BS, BS)
                 acc[meta[c * NNZ + k]] += dot(pgrad[:, lanes(c)], wt, ((1,), (1,)))
 
-        @pl.loop(0, 16)
-        def _(r):
-            keep[r] = acc[r, :128].astype(BF16)
-            send[r] = acc[r, 128:].astype(BF16)
+        size = 16 // len(sends)
+        for i, send in enumerate(sends):
+
+            @pl.loop(0, size)
+            def _(r):
+                keep[r + i * size] = acc[r + i * size, :128].astype(BF16)
+                send[r] = acc[r + i * size, 128:].astype(BF16)
 
 
 def token_grad(meta, pgrad, wts):
     return local(
         token_grad_kernel,
         "tokengrad",
-        [((16, 128, BS), BF16)] * 2,
+        [((16, 128, BS), BF16)] + [((16 // PARTS, 128, BS), BF16)] * PARTS,
         (meta, pgrad, wts),
         [pltpu.VMEM((16, TOK, BS), F32)],
         flops=2 * TOK * BS * BS * NNZ * COLS,
@@ -432,8 +437,8 @@
     g0, m1, m3, g1, g3, pgrad = backward(meta, tok, got, out, up, down, pre, mix_kernel)
     m1, m3 = first(m1, 1), first(m3, -1)
 
-    keep, send = token_grad(meta, pgrad, wts)
-    terms = jnp.where(is_in, keep, to_partner(send))
+    keep, *sends = token_grad(meta, pgrad, wts)
+    terms = jnp.where(is_in, keep, jnp.concatenate([to_partner(send) for send in sends]))
     relayed = [((SPLIT, KERN + 2, 16, BS), BF16)] * 2
     r1, r3 = local(relay_kernel, "relay", relayed, (meta, g1, g3, m1, m3, terms), hbm=(5,))
     terms = lax.all_to_all(terms, "hid", 0, 0, tiled=True)

time: 145 us -> 142 us (0.979)
  waiting for transfers between devices: 64.2 us -> 61.2 us
    ppermute x16, waiting for transfers between devices: 38.3 us -> 33.2 us  [by_core(): return lax.ppermute(value, ('crop', 'rows'), pairs)]
    ppermute x5 -> x6, waiting for transfers between devices: 0.17 us -> 2.35 us  [to_partner(): return lax.ppermute(value, 'rows', [(r, r ^ 1) for r in range(16)])]
    ppermute x5 -> x6, starting transfers between devices: 12.5 us -> 11.6 us  [to_partner(): return lax.ppermute(value, 'rows', [(r, r ^ 1) for r in range(16)])]
  transfers between devices with their start and end apart: 32 -> 33, of which waited for: 16 -> 18; matrix products, arithmetic and copies ran while one was open for 2% -> 2% of each run, Pallas kernels for 3% -> 4%
where the time goes in v6:
time: 142 us; the launch traced here: 141 us
  waiting for transfers between devices  61.2 us (43%)
  starting transfers between devices  53.7 us (38%)
  Pallas kernels  20.5 us (14%)
  other arithmetic  3.56 us (3%)
    ppermute x16, waiting for transfers between devices, by_core(): return lax.ppermute(value, ('crop', 'rows'), pairs)  33.2 us
    ppermute x16, starting transfers between devices, by_core(): return lax.ppermute(value, ('crop', 'rows'), pairs)  25 us
    pallas_call x10, Pallas kernels, local(): pl.pallas_call(kernel, out_shape=shapes, in_specs=[SMEM] + [HBM if i in h...  20.5 us
    ppermute x8, waiting for transfers between devices, along_z(): return lax.ppermute(value, 'hid', [(z, (z + step) % NZ) for z in range(NZ)])  17.1 us
    ppermute x6, starting transfers between devices, to_partner(): return lax.ppermute(value, 'rows', [(r, r ^ 1) for r in range(16)])  11.6 us
    ppermute x8, starting transfers between devices, along_z(): return lax.ppermute(value, 'hid', [(z, (z + step) % NZ) for z in range(NZ)])  10.2 us
    ppermute x2, waiting for transfers between devices, to_next_chip(): return lax.ppermute(value, 'rows', pairs)  8.54 us
    all_to_all x1, starting transfers between devices, on_device(): terms = lax.all_to_all(terms, 'hid', 0, 0, tiled=True)  4.37 us
  transfers between devices with their start and end apart: 33, of which 18 were waited for; matrix products, arithmetic and copies ran while one was open for 2% of the time, Pallas kernels for 4%

profile of v6, /device:TPU:1, one launch (start us, length us, event | category | flops | bytes accessed | tf_op | source)
XLA Modules:
  0.0 141.2 jit_solution(15234658850675109465)
XLA Ops:
  1.9 3.3 %collective-permute-start.9 = (bf16[8,5,16,256]{3,2,1,0:T(8,128)(2,1)S(1)}, bf16[8,5,16,256]{3,2,1,0:T(8,128)(2,1)S(1)}, u32[]{:S(2)}, u32[]{:S(2)}) collective-permute-start(bf16[8,5,16,256]{3,2,1,0:T(8,128)(2,1)S(1)} %select_bitcast_fusion), channel_id=1, source_target_pairs={{0,8},{8,0},{16,24},{24,16},{32,40},{40,32},{48,56},{56,48},{64,72... | collective-permute-start | bytes 983048 | tf_op jit(solution)/shard_map/ppermute | solution.py:41
  6.8 2.0 %collective-permute-start.10 = (bf16[2,8,5,16,256]{4,3,2,1,0:T(8,128)(2,1)S(1)}, bf16[2,8,5,16,256]{4,3,2,1,0:T(8,128)(2,1)S(1)}, u32[]{:S(2)}, u32[]{:S(2)}) collective-permute-start(bf16[2,8,5,16,256]{4,3,2,1,0:T(8,128)(2,1)S(1)} %pad_maximum_fusion.src.refs_9_), channel_id=1, source_target_pairs={{0,16},{8,56},{16,32},{24,8},{32,48},{40,24},{48,0},{56,40},{64,80... | collective-permute-start | bytes 1966088 | tf_op jit(solution)/shard_map/ppermute | solution.py:29
  8.9 5.7 %collective-permute-start.4 = (bf16[256,512]{1,0:T(8,128)(2,1)S(1)}, bf16[256,512]{1,0:T(8,128)(2,1)S(1)}, u32[]{:S(2)}, u32[]{:S(2)}) collective-permute-start(bf16[256,512]{1,0:T(8,128)(2,1)S(1)} %pad_maximum_fusion.1.refs_0_), channel_id=1, source_target_pairs={{0,7},{1,0},{2,1},{3,2},{4,3},{5,4},{6,5},{7,6},{8,15},{9,8},{10,9... | collective-permute-start | bytes 786440 | tf_op jit(solution)/shard_map/ppermute | solution.py:53
  14.7 4.3 %collective-permute-done.4.refs_3_.refs_4_ = bf16[256,512]{1,0:T(8,128)(2,1)S(1)} collective-permute-done((bf16[256,512]{1,0:T(8,128)(2,1)S(1)}, bf16[256,512]{1,0:T(8,128)(2,1)S(1)}, u32[]{:S(2)}, u32[]{:S(2)}) %collective-permute-start.4) | collective-permute-done | bytes 262176 | tf_op jit(solution)/shard_map/ppermute | solution.py:53
  19.0 3.1 %collective-permute-done.1.refs_2_.refs_1_ = bf16[256,512]{1,0:T(8,128)(2,1)S(1)} collective-permute-done((bf16[256,512]{1,0:T(8,128)(2,1)S(1)}, bf16[256,512]{1,0:T(8,128)(2,1)S(1)}, u32[]{:S(2)}, u32[]{:S(2)}) %collective-permute-start.1) | collective-permute-done | bytes 262176 | tf_op jit(solution)/shard_map/ppermute | solution.py:53
  22.9 2.8 %collective-permute-start.13 = (bf16[2,8,5,16,256]{4,3,2,1,0:T(8,128)(2,1)S(1)}, bf16[2,8,5,16,256]{4,3,2,1,0:T(8,128)(2,1)S(1)}, u32[]{:S(2)}, u32[]{:S(2)}) collective-permute-start(bf16[2,8,5,16,256]{4,3,2,1,0:T(8,128)(2,1)S(1)} %collective-permute-done.10.refs_0_.a.refs_10_), channel_id=1, source_target_pairs={{0,64},{8,200},{16,80},{24,216},{32,96},{40,232},{48,112},{56,248}... | collective-permute-start | bytes 1966088 | tf_op jit(solution)/shard_map/ppermute | solution.py:29
  27.1 4.4 %collective-permute-done.5.refs_2_.refs_5_ = bf16[256,512]{1,0:T(8,128)(2,1)S(1)} collective-permute-done((bf16[256,512]{1,0:T(8,128)(2,1)S(1)}, bf16[256,512]{1,0:T(8,128)(2,1)S(1)}, u32[]{:S(2)}, u32[]{:S(2)}) %collective-permute-start.5) | collective-permute-done | bytes 262176 | tf_op jit(solution)/shard_map/ppermute | solution.py:53
  34.4 3.6 %collective-permute-start.15 = (bf16[1,8,5,16,256]{4,3,2,1,0:T(8,128)(2,1)S(1)}, bf16[1,8,5,16,256]{4,3,2,1,0:T(8,128)(2,1)S(1)}, u32[]{:S(2)}, u32[]{:S(2)}) collective-permute-start(bf16[1,8,5,16,256]{4,3,2,1,0:T(8,128)(2,1)S(1)} %get-tuple-element.34), channel_id=1, source_target_pairs={{0,16},{8,56},{16,32},{24,8},{32,48},{40,24},{48,0},{56,40},{64,80... | collective-permute-start | bytes 983048 | tf_op jit(solution)/shard_map/ppermute | solution.py:29
  39.6 2.4 %collective-permute-done.15.refs_15_ = bf16[1,8,5,16,256]{4,3,2,1,0:T(8,128)(2,1)S(1)} collective-permute-done((bf16[1,8,5,16,256]{4,3,2,1,0:T(8,128)(2,1)S(1)}, bf16[1,8,5,16,256]{4,3,2,1,0:T(8,128)(2,1)S(1)}, u32[]{:S(2)}, u32[]{:S(2)}) %collective-permute-start.15) | collective-permute-done | bytes 327712 | tf_op jit(solution)/shard_map/ppermute | solution.py:29
  43.8 4.5 %collective-permute-done.16.refs_16_ = bf16[1,8,5,16,256]{4,3,2,1,0:T(8,128)(2,1)S(1)} collective-permute-done((bf16[1,8,5,16,256]{4,3,2,1,0:T(8,128)(2,1)S(1)}, bf16[1,8,5,16,256]{4,3,2,1,0:T(8,128)(2,1)S(1)}, u32[]{:S(2)}, u32[]{:S(2)}) %collective-permute-start.16) | collective-permute-done | bytes 327712 | tf_op jit(solution)/shard_map/ppermute | solution.py:29
  51.3 2.5 %collective-permute-done.8.refs_8_ = bf16[128,512]{1,0:T(8,128)(2,1)S(1)} collective-permute-done((bf16[128,512]{1,0:T(8,128)(2,1)S(1)}, bf16[128,512]{1,0:T(8,128)(2,1)S(1)}, u32[]{:S(2)}, u32[]{:S(2)}) %collective-permute-start.8) | collective-permute-done | bytes 131104 | tf_op jit(solution)/shard_map/ppermute | solution.py:53
  55.4 2.1 %collective-permute-done.18.refs_18_ = bf16[1,8,5,16,256]{4,3,2,1,0:T(8,128)(2,1)S(1)} collective-permute-done((bf16[1,8,5,16,256]{4,3,2,1,0:T(8,128)(2,1)S(1)}, bf16[1,8,5,16,256]{4,3,2,1,0:T(8,128)(2,1)S(1)}, u32[]{:S(2)}, u32[]{:S(2)}) %collective-permute-start.18) | collective-permute-done | bytes 327712 | tf_op jit(solution)/shard_map/ppermute | solution.py:29
  57.6 4.3 %forward.1 = (f32[256,2048]{1,0:T(8,128)S(1)}, bf16[256,2048]{1,0:T(8,128)(2,1)S(1)}, bf16[64,2048]{1,0:T(8,128)(2,1)S(1)}, bf16[64,2048]{1,0:T(8,128)(2,1)S(1)}...) custom-call(s32[45]{0:T(128)S(1)} %concatenate.9.meta, ...), custom_call_target="tpu_custom_call" | custom-call | flops 1342177280 | bytes 7340032 | tf_op jit(solution)/shard_map/forward/pallas_call | solution.py:65
  61.8 2.2 %collective-permute-start.19 = (bf16[256,2048]{1,0:T(8,128)(2,1)S(1)}, bf16[256,2048]{1,0:T(8,128)(2,1)S(1)}, u32[]{:S(2)}, u32[]{:S(2)}) collective-permute-start(bf16[256,2048]{1,0:T(8,128)(2,1)S(1)} %get-tuple-element.37.mine), channel_id=1, source_target_pairs={{0,8},{8,0},{16,24},{24,16},{32,40},{40,32},{48,56},{56,48},{64,72... | collective-permute-start | bytes 3145736 | tf_op jit(solution)/shard_map/ppermute | solution.py:41
  66.7 4.6 %collective-permute-done.20.up = bf16[64,2048]{1,0:T(8,128)(2,1)S(1)} collective-permute-done((bf16[64,2048]{1,0:T(8,128)(2,1)S(1)}, bf16[64,2048]{1,0:T(8,128)(2,1)S(1)}, u32[]{:S(2)}, u32[]{:S(2)}) %collective-permute-start.20) | collective-permute-done | bytes 262176 | tf_op jit(solution)/shard_map/ppermute | solution.py:49
  71.3 4.0 %collective-permute-done.21.down = bf16[64,2048]{1,0:T(8,128)(2,1)S(1)} collective-permute-done((bf16[64,2048]{1,0:T(8,128)(2,1)S(1)}, bf16[64,2048]{1,0:T(8,128)(2,1)S(1)}, u32[]{:S(2)}, u32[]{:S(2)}) %collective-permute-start.21) | collective-permute-done | bytes 262176 | tf_op jit(solution)/shard_map/ppermute | solution.py:49
  75.2 8.1 %backward.1 = (bf16[8,21,16,256]{3,2,1,0:T(8,128)(2,1)}, bf16[8,21,16,256]{3,2,1,0:T(8,128)(2,1)}, bf16[8,21,16,256]{3,2,1,0:T(8,128)(2,1)}, bf16[4,21,16,256]{3...) custom-call(s32[45]{0:T(128)S(1)} %concatenate.9.meta, ...), custom_call_target="tpu_custom_call" | custom-call | flops 1342177280 | bytes 6889472 | tf_op jit(solution)/shard_map/backward/pallas_call | solution.py:65
  83.8 5.4 %collective-permute-start.25 = (bf16[8,21,16,256]{3,2,1,0:T(8,128)(2,1)}, bf16[8,21,16,256]{3,2,1,0:T(8,128)(2,1)S(1)}, u32[]{:S(2)}, u32[]{:S(2)}) collective-permute-start(bf16[8,21,16,256]{3,2,1,0:T(8,128)(2,1)} %get-tuple-element.49), channel_id=1, source_target_pairs={{0,192},{8,56},{16,208},{24,8},{32,224},{40,24},{48,240},{56,40},{... | collective-permute-start | bytes 4128776 | tf_op jit(solution)/shard_map/ppermute | solution.py:29
  94.9 4.4 %all-to-all-start = ((bf16[16,128,256]{2,1,0:T(8,128)(2,1)}), bf16[16,128,256]{2,1,0:T(8,128)(2,1)}, u32[]{:S(2)}, u32[]{:S(2)}) async-start(bf16[16,128,256]{2,1,0:T(8,128)(2,1)} %maximum_select_fusion._), calls=%async_computation | async-start | bytes 2097152 | tf_op jit(solution)/shard_map/all_to_all | solution.py:444
  99.3 5.7 %collective-permute-done.24.m1 = bf16[8,21,16,256]{3,2,1,0:T(8,128)(2,1)S(1)} collective-permute-done((bf16[8,21,16,256]{3,2,1,0:T(8,128)(2,1)}, bf16[8,21,16,256]{3,2,1,0:T(8,128)(2,1)S(1)}, u32[]{:S(2)}, u32[]{:S(2)}) %collective-permute-start.24) | collective-permute-done | bytes 1376288 | tf_op jit(solution)/shard_map/ppermute | solution.py:29
  110.2 9.0 %collective-permute-done.26.p1 = bf16[4,22,16,256]{3,2,1,0:T(8,128)(2,1)S(1)} collective-permute-done((bf16[4,22,16,256]{3,2,1,0:T(8,128)(2,1)S(1)}, bf16[4,22,16,256]{3,2,1,0:T(8,128)(2,1)S(1)}, u32[]{:S(2)}, u32[]{:S(2)}) %collective-permute-start.26) | collective-permute-done | bytes 720928 | tf_op jit(solution)/shard_map/ppermute | solution.py:29
  120.4 2.7 %collective-permute-start.29 = (bf16[8,6,16,256]{3,2,1,0:T(8,128)(2,1)S(1)}, bf16[8,6,16,256]{3,2,1,0:T(8,128)(2,1)S(1)}, u32[]{:S(2)}, u32[]{:S(2)}) collective-permute-start(bf16[8,6,16,256]{3,2,1,0:T(8,128)(2,1)S(1)} %get-tuple-element.56), channel_id=1, source_target_pairs={{0,48},{8,200},{16,0},{24,216},{32,16},{40,232},{48,32},{56,248},{... | collective-permute-start | bytes 1179656 | tf_op jit(solution)/shard_map/ppermute | solution.py:29
  124.4 8.4 %collective-permute-done.28.prev = bf16[8,6,16,256]{3,2,1,0:T(8,128)(2,1)S(1)} collective-permute-done((bf16[8,6,16,256]{3,2,1,0:T(8,128)(2,1)S(1)}, bf16[8,6,16,256]{3,2,1,0:T(8,128)(2,1)S(1)}, u32[]{:S(2)}, u32[]{:S(2)}) %collective-permute-start.28) | collective-permute-done | bytes 393248 | tf_op jit(solution)/shard_map/ppermute | solution.py:29
  133.6 4.0 %collective-permute-start.31 = (bf16[8,7,8,256]{3,2,1,0:T(8,128)(2,1)S(1)}, bf16[8,7,8,256]{3,2,1,0:T(8,128)(2,1)S(1)}, u32[]{:S(2)}, u32[]{:S(2)}) collective-permute-start(bf16[8,7,8,256]{3,2,1,0:T(8,128)(2,1)S(1)} %get-tuple-element.59), channel_id=1, source_target_pairs={{0,8},{8,0},{16,24},{24,16},{32,40},{40,32},{48,56},{56,48},{64,72... | collective-permute-start | bytes 688136 | tf_op jit(solution)/shard_map/ppermute | solution.py:41
  (77 shorter events, 36.9 us)
Async XLA Ops:
  6.7 15.5 %collective-permute-start.11 = (bf16[2,8,5,16,256]{4,3,2,1,0:T(8,128)(2,1)S(1)}, bf16[2,8,5,16,256]{4,3,2,1,0:T(8,128)(2,1)S(1)}, u32[]{:S(2)}, u32[]{:S(2)}) collective-permute-start(bf16[2,8,5,16,256]{4,3,2,1,0:T(8,128)(2,1)S(1)} %pad_maximum_fusion.src.refs_9_), channel_id=1, source_target_pairs={{0,192},{8,72},{16,208},{24,88},{32,224},{40,104},{48,240},{56,120... | collective-permute-start | bytes 1966088 | tf_op jit(solution)/shard_map/ppermute | solution.py:29
  6.8 15.4 %collective-permute-start.10 = (bf16[2,8,5,16,256]{4,3,2,1,0:T(8,128)(2,1)S(1)}, bf16[2,8,5,16,256]{4,3,2,1,0:T(8,128)(2,1)S(1)}, u32[]{:S(2)}, u32[]{:S(2)}) collective-permute-start(bf16[2,8,5,16,256]{4,3,2,1,0:T(8,128)(2,1)S(1)} %pad_maximum_fusion.src.refs_9_), channel_id=1, source_target_pairs={{0,16},{8,56},{16,32},{24,8},{32,48},{40,24},{48,0},{56,40},{64,80... | collective-permute-start | bytes 1966088 | tf_op jit(solution)/shard_map/ppermute | solution.py:29
  8.9 10.1 %collective-permute-start.4 = (bf16[256,512]{1,0:T(8,128)(2,1)S(1)}, bf16[256,512]{1,0:T(8,128)(2,1)S(1)}, u32[]{:S(2)}, u32[]{:S(2)}) collective-permute-start(bf16[256,512]{1,0:T(8,128)(2,1)S(1)} %pad_maximum_fusion.1.refs_0_), channel_id=1, source_target_pairs={{0,7},{1,0},{2,1},{3,2},{4,3},{5,4},{6,5},{7,6},{8,15},{9,8},{10,9... | collective-permute-start | bytes 786440 | tf_op jit(solution)/shard_map/ppermute | solution.py:53
  14.5 7.6 %collective-permute-start.1 = (bf16[256,512]{1,0:T(8,128)(2,1)S(1)}, bf16[256,512]{1,0:T(8,128)(2,1)S(1)}, u32[]{:S(2)}, u32[]{:S(2)}) collective-permute-start(bf16[256,512]{1,0:T(8,128)(2,1)S(1)} %pad_maximum_fusion.1.refs_0_), channel_id=1, source_target_pairs={{0,1},{1,2},{2,3},{3,4},{4,5},{5,6},{6,7},{7,0},{8,9},{9,10},{10,1... | collective-permute-start | bytes 786440 | tf_op jit(solution)/shard_map/ppermute | solution.py:53
  22.8 11.0 %collective-permute-start.12 = (bf16[2,8,5,16,256]{4,3,2,1,0:T(8,128)(2,1)S(1)}, bf16[2,8,5,16,256]{4,3,2,1,0:T(8,128)(2,1)S(1)}, u32[]{:S(2)}, u32[]{:S(2)}) collective-permute-start(bf16[2,8,5,16,256]{4,3,2,1,0:T(8,128)(2,1)S(1)} %hold.1), channel_id=1, source_target_pairs={{0,48},{8,24},{16,0},{24,40},{32,16},{40,56},{48,32},{56,8},{64,11... | collective-permute-start | bytes 1966088 | tf_op jit(solution)/shard_map/ppermute | solution.py:29
  22.9 10.9 %collective-permute-start.13 = (bf16[2,8,5,16,256]{4,3,2,1,0:T(8,128)(2,1)S(1)}, bf16[2,8,5,16,256]{4,3,2,1,0:T(8,128)(2,1)S(1)}, u32[]{:S(2)}, u32[]{:S(2)}) collective-permute-start(bf16[2,8,5,16,256]{4,3,2,1,0:T(8,128)(2,1)S(1)} %collective-permute-done.10.refs_0_.a.refs_10_), channel_id=1, source_target_pairs={{0,64},{8,200},{16,80},{24,216},{32,96},{40,232},{48,112},{56,248}... | collective-permute-start | bytes 1966088 | tf_op jit(solution)/shard_map/ppermute | solution.py:29
  34.4 7.6 %collective-permute-start.15 = (bf16[1,8,5,16,256]{4,3,2,1,0:T(8,128)(2,1)S(1)}, bf16[1,8,5,16,256]{4,3,2,1,0:T(8,128)(2,1)S(1)}, u32[]{:S(2)}, u32[]{:S(2)}) collective-permute-start(bf16[1,8,5,16,256]{4,3,2,1,0:T(8,128)(2,1)S(1)} %get-tuple-element.34), channel_id=1, source_target_pairs={{0,16},{8,56},{16,32},{24,8},{32,48},{40,24},{48,0},{56,40},{64,80... | collective-permute-start | bytes 983048 | tf_op jit(solution)/shard_map/ppermute | solution.py:29
  38.0 17.4 %collective-permute-start.14 = (bf16[2,8,5,16,256]{4,3,2,1,0:T(8,128)(2,1)S(1)}, bf16[2,8,5,16,256]{4,3,2,1,0:T(8,128)(2,1)S(1)}, u32[]{:S(2)}, u32[]{:S(2)}) collective-permute-start(bf16[2,8,5,16,256]{4,3,2,1,0:T(8,128)(2,1)S(1)} %collective-permute-done.12.c.refs_12_), channel_id=1, source_target_pairs={{0,192},{8,72},{16,208},{24,88},{32,224},{40,104},{48,240},{56,120... | collective-permute-start | bytes 1966088 | tf_op jit(solution)/shard_map/ppermute | solution.py:29
  38.1 10.2 %collective-permute-start.16 = (bf16[1,8,5,16,256]{4,3,2,1,0:T(8,128)(2,1)S(1)}, bf16[1,8,5,16,256]{4,3,2,1,0:T(8,128)(2,1)S(1)}, u32[]{:S(2)}, u32[]{:S(2)}) collective-permute-start(bf16[1,8,5,16,256]{4,3,2,1,0:T(8,128)(2,1)S(1)} %get-tuple-element.35), channel_id=1, source_target_pairs={{0,48},{8,24},{16,0},{24,40},{32,16},{40,56},{48,32},{56,8},{64,11... | collective-permute-start | bytes 983048 | tf_op jit(solution)/shard_map/ppermute | solution.py:29
  38.1 11.5 %collective-permute-start.6 = (bf16[256,512]{1,0:T(8,128)(2,1)S(1)}, bf16[256,512]{1,0:T(8,128)(2,1)S(1)}, u32[]{:S(2)}, u32[]{:S(2)}) collective-permute-start(bf16[256,512]{1,0:T(8,128)(2,1)S(1)} %collective-permute-done.5.refs_2_.refs_5_), channel_id=1, source_target_pairs={{0,7},{1,0},{2,1},{3,2},{4,3},{5,4},{6,5},{7,6},{8,15},{9,8},{10,9... | collective-permute-start | bytes 786440 | tf_op jit(solution)/shard_map/ppermute | solution.py:53
  38.3 11.7 %collective-permute-start.3 = (bf16[256,512]{1,0:T(8,128)(2,1)S(1)}, bf16[256,512]{1,0:T(8,128)(2,1)S(1)}, u32[]{:S(2)}, u32[]{:S(2)}) collective-permute-start(bf16[256,512]{1,0:T(8,128)(2,1)S(1)} %collective-permute-done.2.refs_1_.refs_2_), channel_id=1, source_target_pairs={{0,1},{1,2},{2,3},{3,4},{4,5},{5,6},{6,7},{7,0},{8,9},{9,10},{10,1... | collective-permute-start | bytes 786440 | tf_op jit(solution)/shard_map/ppermute | solution.py:53
  42.0 13.4 %collective-permute-start.17 = (bf16[1,8,5,16,256]{4,3,2,1,0:T(8,128)(2,1)S(1)}, bf16[1,8,5,16,256]{4,3,2,1,0:T(8,128)(2,1)S(1)}, u32[]{:S(2)}, u32[]{:S(2)}) collective-permute-start(bf16[1,8,5,16,256]{4,3,2,1,0:T(8,128)(2,1)S(1)} %collective-permute-done.15.refs_15_), channel_id=1, source_target_pairs={{0,64},{8,200},{16,80},{24,216},{32,96},{40,232},{48,112},{56,248}... | collective-permute-start | bytes 983048 | tf_op jit(solution)/shard_map/ppermute | solution.py:29
  48.3 9.3 %collective-permute-start.18 = (bf16[1,8,5,16,256]{4,3,2,1,0:T(8,128)(2,1)S(1)}, bf16[1,8,5,16,256]{4,3,2,1,0:T(8,128)(2,1)S(1)}, u32[]{:S(2)}, u32[]{:S(2)}) collective-permute-start(bf16[1,8,5,16,256]{4,3,2,1,0:T(8,128)(2,1)S(1)} %collective-permute-done.16.refs_16_), channel_id=1, source_target_pairs={{0,192},{8,72},{16,208},{24,88},{32,224},{40,104},{48,240},{56,120... | collective-permute-start | bytes 983048 | tf_op jit(solution)/shard_map/ppermute | solution.py:29
  61.8 13.4 %collective-permute-start.19 = (bf16[256,2048]{1,0:T(8,128)(2,1)S(1)}, bf16[256,2048]{1,0:T(8,128)(2,1)S(1)}, u32[]{:S(2)}, u32[]{:S(2)}) collective-permute-start(bf16[256,2048]{1,0:T(8,128)(2,1)S(1)} %get-tuple-element.37.mine), channel_id=1, source_target_pairs={{0,8},{8,0},{16,24},{24,16},{32,40},{40,32},{48,56},{56,48},{64,72... | collective-permute-start | bytes 3145736 | tf_op jit(solution)/shard_map/ppermute | solution.py:41
  64.1 7.2 %collective-permute-start.20 = (bf16[64,2048]{1,0:T(8,128)(2,1)S(1)}, bf16[64,2048]{1,0:T(8,128)(2,1)S(1)}, u32[]{:S(2)}, u32[]{:S(2)}) collective-permute-start(bf16[64,2048]{1,0:T(8,128)(2,1)S(1)} %get-tuple-element.38), channel_id=1, source_target_pairs={{0,24},{8,16},{16,40},{24,32},{32,56},{40,48},{48,72},{56,64},{64,... | collective-permute-start | bytes 786440 | tf_op jit(solution)/shard_map/ppermute | solution.py:49
  65.4 9.8 %collective-permute-start.21 = (bf16[64,2048]{1,0:T(8,128)(2,1)S(1)}, bf16[64,2048]{1,0:T(8,128)(2,1)S(1)}, u32[]{:S(2)}, u32[]{:S(2)}) collective-permute-start(bf16[64,2048]{1,0:T(8,128)(2,1)S(1)} %get-tuple-element.39), channel_id=1, source_target_pairs={{16,8},{24,0},{32,24},{40,16},{48,40},{56,32},{64,56},{72,48},{80,... | collective-permute-start | bytes 786440 | tf_op jit(solution)/shard_map/ppermute | solution.py:49
  83.3 21.7 %collective-permute-start.24 = (bf16[8,21,16,256]{3,2,1,0:T(8,128)(2,1)}, bf16[8,21,16,256]{3,2,1,0:T(8,128)(2,1)S(1)}, u32[]{:S(2)}, u32[]{:S(2)}) collective-permute-start(bf16[8,21,16,256]{3,2,1,0:T(8,128)(2,1)} %get-tuple-element.48), channel_id=1, source_target_pairs={{0,64},{8,24},{16,80},{24,40},{32,96},{40,56},{48,112},{56,8},{64,... | collective-permute-start | bytes 4128776 | tf_op jit(solution)/shard_map/ppermute | solution.py:29
  83.8 21.2 %collective-permute-start.25 = (bf16[8,21,16,256]{3,2,1,0:T(8,128)(2,1)}, bf16[8,21,16,256]{3,2,1,0:T(8,128)(2,1)S(1)}, u32[]{:S(2)}, u32[]{:S(2)}) collective-permute-start(bf16[8,21,16,256]{3,2,1,0:T(8,128)(2,1)} %get-tuple-element.49), channel_id=1, source_target_pairs={{0,192},{8,56},{16,208},{24,8},{32,224},{40,24},{48,240},{56,40},{... | collective-permute-start | bytes 4128776 | tf_op jit(solution)/shard_map/ppermute | solution.py:29
  94.9 42.7 %all-to-all-start = ((bf16[16,128,256]{2,1,0:T(8,128)(2,1)}), bf16[16,128,256]{2,1,0:T(8,128)(2,1)}, u32[]{:S(2)}, u32[]{:S(2)}) async-start(bf16[16,128,256]{2,1,0:T(8,128)(2,1)} %maximum_select_fusion._), calls=%async_computation | async-start | bytes 2097152 | tf_op jit(solution)/shard_map/all_to_all | solution.py:444
  107.0 12.2 %collective-permute-start.26 = (bf16[4,22,16,256]{3,2,1,0:T(8,128)(2,1)S(1)}, bf16[4,22,16,256]{3,2,1,0:T(8,128)(2,1)S(1)}, u32[]{:S(2)}, u32[]{:S(2)}) collective-permute-start(bf16[4,22,16,256]{3,2,1,0:T(8,128)(2,1)S(1)} %get-tuple-element.52), channel_id=1, source_target_pairs={{0,64},{8,24},{16,80},{24,40},{32,96},{40,56},{48,112},{56,8},{64,... | collective-permute-start | bytes 2162696 | tf_op jit(solution)/shard_map/ppermute | solution.py:29
  108.3 10.9 %collective-permute-start.27 = (bf16[4,22,16,256]{3,2,1,0:T(8,128)(2,1)S(1)}, bf16[4,22,16,256]{3,2,1,0:T(8,128)(2,1)S(1)}, u32[]{:S(2)}, u32[]{:S(2)}) collective-permute-start(bf16[4,22,16,256]{3,2,1,0:T(8,128)(2,1)S(1)} %get-tuple-element.53), channel_id=1, source_target_pairs={{0,192},{8,56},{16,208},{24,8},{32,224},{40,24},{48,240},{56,40},{... | collective-permute-start | bytes 2162696 | tf_op jit(solution)/shard_map/ppermute | solution.py:29
  120.3 12.4 %collective-permute-start.28 = (bf16[8,6,16,256]{3,2,1,0:T(8,128)(2,1)S(1)}, bf16[8,6,16,256]{3,2,1,0:T(8,128)(2,1)S(1)}, u32[]{:S(2)}, u32[]{:S(2)}) collective-permute-start(bf16[8,6,16,256]{3,2,1,0:T(8,128)(2,1)S(1)} %get-tuple-element.55), channel_id=1, source_target_pairs={{0,16},{8,72},{16,32},{24,88},{32,48},{40,104},{48,0},{56,120},{64... | collective-permute-start | bytes 1179656 | tf_op jit(solution)/shard_map/ppermute | solution.py:29
  120.4 12.3 %collective-permute-start.29 = (bf16[8,6,16,256]{3,2,1,0:T(8,128)(2,1)S(1)}, bf16[8,6,16,256]{3,2,1,0:T(8,128)(2,1)S(1)}, u32[]{:S(2)}, u32[]{:S(2)}) collective-permute-start(bf16[8,6,16,256]{3,2,1,0:T(8,128)(2,1)S(1)} %get-tuple-element.56), channel_id=1, source_target_pairs={{0,48},{8,200},{16,0},{24,216},{32,16},{40,232},{48,32},{56,248},{... | collective-permute-start | bytes 1179656 | tf_op jit(solution)/shard_map/ppermute | solution.py:29
  123.1 9.7 %collective-permute-start.30 = (bf16[8,6,16,256]{3,2,1,0:T(8,128)(2,1)S(1)}, bf16[8,6,16,256]{3,2,1,0:T(8,128)(2,1)S(1)}, u32[]{:S(2)}, u32[]{:S(2)}) collective-permute-start(bf16[8,6,16,256]{3,2,1,0:T(8,128)(2,1)S(1)} %get-tuple-element.57), channel_id=1, source_target_pairs={{0,32},{8,136},{16,48},{24,152},{32,0},{40,168},{48,16},{56,184},{... | collective-permute-start | bytes 1179656 | tf_op jit(solution)/shard_map/ppermute | solution.py:29
  (16 other events, 110.2 us)

commit v7 on v6

--- a/solution.py
+++ b/solution.py
@@ -335,7 +335,12 @@
         out[:, b * BS : (b + 1) * BS] = total.astype(BF16)
 
 
-def relay_kernel(meta, g1, g3, m1, m3, _, o1, o3):
+def relay_kernel(meta, s1, s3, m1, m3, _, o1, o3, g1, g3, sems):
+    copies = [pltpu.make_async_copy(a, b, sems.at[i]) for i, (a, b) in enumerate(((s1, g1), (s3, g3)))]
+    for copy in copies:
+        copy.start()
+    for copy in copies:
+        copy.wait()
     for out, own, got in ((o1, g1, m1), (o3, g3, m3)):
 
         @pl.loop(0, SPLIT)
@@ -440,7 +445,9 @@
     keep, *sends = token_grad(meta, pgrad, wts)
     terms = jnp.where(is_in, keep, jnp.concatenate([to_partner(send) for send in sends]))
     relayed = [((SPLIT, KERN + 2, 16, BS), BF16)] * 2
-    r1, r3 = local(relay_kernel, "relay", relayed, (meta, g1, g3, m1, m3, terms), hbm=(5,))
+    held = [pltpu.VMEM(g1.shape, BF16)] * 2 + [pltpu.SemaphoreType.DMA((2,))]
+    g1, g3 = (pltpu.with_memory_space_constraint(g, pltpu.HBM) for g in (g1, g3))
+    r1, r3 = local(relay_kernel, "relay", relayed, (meta, g1, g3, m1, m3, terms), held, hbm=(1, 2, 5))
     terms = lax.all_to_all(terms, "hid", 0, 0, tiled=True)
     outs = [((128, 512), BF16), ((8, 128), F32)]
     grad_tokens, flag = local(gather_sum_kernel, "gathersum", outs, (meta, terms))

time: 142 us -> 142 us (level)
  transfers between devices with their start and end apart: 33 -> 33, of which waited for: 18 -> 18; matrix products, arithmetic and copies ran while one was open for 2% -> 2% of each run, Pallas kernels for 4% -> 5%
where the time goes in v7:
time: 142 us; the launch traced here: 141 us
  waiting for transfers between devices  61.3 us (43%)
  starting transfers between devices  53.6 us (38%)
  Pallas kernels  21.8 us (15%)
  other arithmetic  3.58 us (3%)
    ppermute x16, waiting for transfers between devices, by_core(): return lax.ppermute(value, ('crop', 'rows'), pairs)  33.3 us
    ppermute x16, starting transfers between devices, by_core(): return lax.ppermute(value, ('crop', 'rows'), pairs)  25 us
    pallas_call x10, Pallas kernels, local(): pl.pallas_call(kernel, out_shape=shapes, in_specs=[SMEM] + [HBM if i in h...  21.8 us
    ppermute x8, waiting for transfers between devices, along_z(): return lax.ppermute(value, 'hid', [(z, (z + step) % NZ) for z in range(NZ)])  17.1 us
    ppermute x6, starting transfers between devices, to_partner(): return lax.ppermute(value, 'rows', [(r, r ^ 1) for r in range(16)])  11.6 us
    ppermute x8, starting transfers between devices, along_z(): return lax.ppermute(value, 'hid', [(z, (z + step) % NZ) for z in range(NZ)])  10.2 us
    ppermute x2, waiting for transfers between devices, to_next_chip(): return lax.ppermute(value, 'rows', pairs)  8.54 us
    all_to_all x1, starting transfers between devices, on_device(): terms = lax.all_to_all(terms, 'hid', 0, 0, tiled=True)  4.26 us
  transfers between devices with their start and end apart: 33, of which 18 were waited for; matrix products, arithmetic and copies ran while one was open for 2% of the time, Pallas kernels for 5%

profile of v7, /device:TPU:1, one launch (start us, length us, event | category | flops | bytes accessed | tf_op | source)
XLA Modules:
  0.0 141.4 jit_solution(4830398438086210359)
XLA Ops:
  1.9 3.3 %collective-permute-start.9 = (bf16[8,5,16,256]{3,2,1,0:T(8,128)(2,1)S(1)}, bf16[8,5,16,256]{3,2,1,0:T(8,128)(2,1)S(1)}, u32[]{:S(2)}, u32[]{:S(2)}) collective-permute-start(bf16[8,5,16,256]{3,2,1,0:T(8,128)(2,1)S(1)} %select_bitcast_fusion), channel_id=1, source_target_pairs={{0,8},{8,0},{16,24},{24,16},{32,40},{40,32},{48,56},{56,48},{64,72... | collective-permute-start | bytes 983048 | tf_op jit(solution)/shard_map/ppermute | solution.py:41
  8.9 5.7 %collective-permute-start.4 = (bf16[256,512]{1,0:T(8,128)(2,1)S(1)}, bf16[256,512]{1,0:T(8,128)(2,1)S(1)}, u32[]{:S(2)}, u32[]{:S(2)}) collective-permute-start(bf16[256,512]{1,0:T(8,128)(2,1)S(1)} %pad_maximum_fusion.1.refs_0_), channel_id=1, source_target_pairs={{0,7},{1,0},{2,1},{3,2},{4,3},{5,4},{6,5},{7,6},{8,15},{9,8},{10,9... | collective-permute-start | bytes 786440 | tf_op jit(solution)/shard_map/ppermute | solution.py:53
  14.7 4.3 %collective-permute-done.4.refs_3_.refs_4_ = bf16[256,512]{1,0:T(8,128)(2,1)S(1)} collective-permute-done((bf16[256,512]{1,0:T(8,128)(2,1)S(1)}, bf16[256,512]{1,0:T(8,128)(2,1)S(1)}, u32[]{:S(2)}, u32[]{:S(2)}) %collective-permute-start.4) | collective-permute-done | bytes 262176 | tf_op jit(solution)/shard_map/ppermute | solution.py:53
  19.0 3.1 %collective-permute-done.1.refs_2_.refs_1_ = bf16[256,512]{1,0:T(8,128)(2,1)S(1)} collective-permute-done((bf16[256,512]{1,0:T(8,128)(2,1)S(1)}, bf16[256,512]{1,0:T(8,128)(2,1)S(1)}, u32[]{:S(2)}, u32[]{:S(2)}) %collective-permute-start.1) | collective-permute-done | bytes 262176 | tf_op jit(solution)/shard_map/ppermute | solution.py:53
  22.9 2.8 %collective-permute-start.13 = (bf16[2,8,5,16,256]{4,3,2,1,0:T(8,128)(2,1)S(1)}, bf16[2,8,5,16,256]{4,3,2,1,0:T(8,128)(2,1)S(1)}, u32[]{:S(2)}, u32[]{:S(2)}) collective-permute-start(bf16[2,8,5,16,256]{4,3,2,1,0:T(8,128)(2,1)S(1)} %collective-permute-done.10.refs_0_.a.refs_10_), channel_id=1, source_target_pairs={{0,64},{8,200},{16,80},{24,216},{32,96},{40,232},{48,112},{56,248}... | collective-permute-start | bytes 1966088 | tf_op jit(solution)/shard_map/ppermute | solution.py:29
  27.1 4.4 %collective-permute-done.5.refs_2_.refs_5_ = bf16[256,512]{1,0:T(8,128)(2,1)S(1)} collective-permute-done((bf16[256,512]{1,0:T(8,128)(2,1)S(1)}, bf16[256,512]{1,0:T(8,128)(2,1)S(1)}, u32[]{:S(2)}, u32[]{:S(2)}) %collective-permute-start.5) | collective-permute-done | bytes 262176 | tf_op jit(solution)/shard_map/ppermute | solution.py:53
  34.4 3.6 %collective-permute-start.15 = (bf16[1,8,5,16,256]{4,3,2,1,0:T(8,128)(2,1)S(1)}, bf16[1,8,5,16,256]{4,3,2,1,0:T(8,128)(2,1)S(1)}, u32[]{:S(2)}, u32[]{:S(2)}) collective-permute-start(bf16[1,8,5,16,256]{4,3,2,1,0:T(8,128)(2,1)S(1)} %get-tuple-element.34), channel_id=1, source_target_pairs={{0,16},{8,56},{16,32},{24,8},{32,48},{40,24},{48,0},{56,40},{64,80... | collective-permute-start | bytes 983048 | tf_op jit(solution)/shard_map/ppermute | solution.py:29
  39.6 2.4 %collective-permute-done.15.refs_15_ = bf16[1,8,5,16,256]{4,3,2,1,0:T(8,128)(2,1)S(1)} collective-permute-done((bf16[1,8,5,16,256]{4,3,2,1,0:T(8,128)(2,1)S(1)}, bf16[1,8,5,16,256]{4,3,2,1,0:T(8,128)(2,1)S(1)}, u32[]{:S(2)}, u32[]{:S(2)}) %collective-permute-start.15) | collective-permute-done | bytes 327712 | tf_op jit(solution)/shard_map/ppermute | solution.py:29
  43.8 4.5 %collective-permute-done.16.refs_16_ = bf16[1,8,5,16,256]{4,3,2,1,0:T(8,128)(2,1)S(1)} collective-permute-done((bf16[1,8,5,16,256]{4,3,2,1,0:T(8,128)(2,1)S(1)}, bf16[1,8,5,16,256]{4,3,2,1,0:T(8,128)(2,1)S(1)}, u32[]{:S(2)}, u32[]{:S(2)}) %collective-permute-start.16) | collective-permute-done | bytes 327712 | tf_op jit(solution)/shard_map/ppermute | solution.py:29
  51.3 2.5 %collective-permute-done.8.refs_8_ = bf16[128,512]{1,0:T(8,128)(2,1)S(1)} collective-permute-done((bf16[128,512]{1,0:T(8,128)(2,1)S(1)}, bf16[128,512]{1,0:T(8,128)(2,1)S(1)}, u32[]{:S(2)}, u32[]{:S(2)}) %collective-permute-start.8) | collective-permute-done | bytes 131104 | tf_op jit(solution)/shard_map/ppermute | solution.py:53
  55.4 2.1 %collective-permute-done.18.refs_18_ = bf16[1,8,5,16,256]{4,3,2,1,0:T(8,128)(2,1)S(1)} collective-permute-done((bf16[1,8,5,16,256]{4,3,2,1,0:T(8,128)(2,1)S(1)}, bf16[1,8,5,16,256]{4,3,2,1,0:T(8,128)(2,1)S(1)}, u32[]{:S(2)}, u32[]{:S(2)}) %collective-permute-start.18) | collective-permute-done | bytes 327712 | tf_op jit(solution)/shard_map/ppermute | solution.py:29
  57.6 4.3 %forward.1 = (f32[256,2048]{1,0:T(8,128)S(1)}, bf16[256,2048]{1,0:T(8,128)(2,1)S(1)}, bf16[64,2048]{1,0:T(8,128)(2,1)S(1)}, bf16[64,2048]{1,0:T(8,128)(2,1)S(1)}...) custom-call(s32[45]{0:T(128)S(1)} %concatenate.9.meta, ...), custom_call_target="tpu_custom_call" | custom-call | flops 1342177280 | bytes 7340032 | tf_op jit(solution)/shard_map/forward/pallas_call | solution.py:65
  61.8 2.2 %collective-permute-start.19 = (bf16[256,2048]{1,0:T(8,128)(2,1)S(1)}, bf16[256,2048]{1,0:T(8,128)(2,1)S(1)}, u32[]{:S(2)}, u32[]{:S(2)}) collective-permute-start(bf16[256,2048]{1,0:T(8,128)(2,1)S(1)} %get-tuple-element.37.mine), channel_id=1, source_target_pairs={{0,8},{8,0},{16,24},{24,16},{32,40},{40,32},{48,56},{56,48},{64,72... | collective-permute-start | bytes 3145736 | tf_op jit(solution)/shard_map/ppermute | solution.py:41
  66.7 4.6 %collective-permute-done.20.up = bf16[64,2048]{1,0:T(8,128)(2,1)S(1)} collective-permute-done((bf16[64,2048]{1,0:T(8,128)(2,1)S(1)}, bf16[64,2048]{1,0:T(8,128)(2,1)S(1)}, u32[]{:S(2)}, u32[]{:S(2)}) %collective-permute-start.20) | collective-permute-done | bytes 262176 | tf_op jit(solution)/shard_map/ppermute | solution.py:49
  71.3 4.0 %collective-permute-done.21.down = bf16[64,2048]{1,0:T(8,128)(2,1)S(1)} collective-permute-done((bf16[64,2048]{1,0:T(8,128)(2,1)S(1)}, bf16[64,2048]{1,0:T(8,128)(2,1)S(1)}, u32[]{:S(2)}, u32[]{:S(2)}) %collective-permute-start.21) | collective-permute-done | bytes 262176 | tf_op jit(solution)/shard_map/ppermute | solution.py:49
  75.2 8.1 %backward.1 = (bf16[8,21,16,256]{3,2,1,0:T(8,128)(2,1)}, bf16[8,21,16,256]{3,2,1,0:T(8,128)(2,1)}, bf16[8,21,16,256]{3,2,1,0:T(8,128)(2,1)}, bf16[4,21,16,256]{3...) custom-call(s32[45]{0:T(128)S(1)} %concatenate.9.meta, ...), custom_call_target="tpu_custom_call" | custom-call | flops 1342177280 | bytes 6889472 | tf_op jit(solution)/shard_map/backward/pallas_call | solution.py:65
  83.8 5.4 %collective-permute-start.25 = (bf16[8,21,16,256]{3,2,1,0:T(8,128)(2,1)}, bf16[8,21,16,256]{3,2,1,0:T(8,128)(2,1)S(1)}, u32[]{:S(2)}, u32[]{:S(2)}) collective-permute-start(bf16[8,21,16,256]{3,2,1,0:T(8,128)(2,1)} %get-tuple-element.49), channel_id=1, source_target_pairs={{0,192},{8,56},{16,208},{24,8},{32,224},{40,24},{48,240},{56,40},{... | collective-permute-start | bytes 4128776 | tf_op jit(solution)/shard_map/ppermute | solution.py:29
  95.0 4.3 %all-to-all-start = ((bf16[16,128,256]{2,1,0:T(8,128)(2,1)}), bf16[16,128,256]{2,1,0:T(8,128)(2,1)}, u32[]{:S(2)}, u32[]{:S(2)}) async-start(bf16[16,128,256]{2,1,0:T(8,128)(2,1)} %maximum_select_fusion._), calls=%async_computation | async-start | bytes 2097152 | tf_op jit(solution)/shard_map/all_to_all | solution.py:451
  99.2 5.8 %collective-permute-done.24.m1 = bf16[8,21,16,256]{3,2,1,0:T(8,128)(2,1)S(1)} collective-permute-done((bf16[8,21,16,256]{3,2,1,0:T(8,128)(2,1)}, bf16[8,21,16,256]{3,2,1,0:T(8,128)(2,1)S(1)}, u32[]{:S(2)}, u32[]{:S(2)}) %collective-permute-start.24) | collective-permute-done | bytes 1376288 | tf_op jit(solution)/shard_map/ppermute | solution.py:29
  105.0 2.2 %relay.1 = (bf16[4,22,16,256]{3,2,1,0:T(8,128)(2,1)S(1)}, bf16[4,22,16,256]{3,2,1,0:T(8,128)(2,1)S(1)}) custom-call(s32[45]{0:T(128)S(1)} %concatenate.9.meta, bf16[4,21,16,256]{3,2,1,0:T(8,128)(2,1)} %get-tuple-element.50.s1, bf16[4,21,16,256]{3,2,1,0:T(8,128)(2,1)} %get-tuple-element.51.s3, bf16[8,21,16,256]{3,2,1,0:T(8,128)(2,1)S(1)} %collective-permute-done.24.m1, ...), custom_call_target="tpu_custom_call" | custom-call | flops 1048576 | bytes 5177344 | tf_op jit(solution)/shard_map/relay/pallas_call | solution.py:65
  110.4 9.0 %collective-permute-done.26.p1 = bf16[4,22,16,256]{3,2,1,0:T(8,128)(2,1)S(1)} collective-permute-done((bf16[4,22,16,256]{3,2,1,0:T(8,128)(2,1)S(1)}, bf16[4,22,16,256]{3,2,1,0:T(8,128)(2,1)S(1)}, u32[]{:S(2)}, u32[]{:S(2)}) %collective-permute-start.26) | collective-permute-done | bytes 720928 | tf_op jit(solution)/shard_map/ppermute | solution.py:29
  120.6 2.7 %collective-permute-start.29 = (bf16[8,6,16,256]{3,2,1,0:T(8,128)(2,1)S(1)}, bf16[8,6,16,256]{3,2,1,0:T(8,128)(2,1)S(1)}, u32[]{:S(2)}, u32[]{:S(2)}) collective-permute-start(bf16[8,6,16,256]{3,2,1,0:T(8,128)(2,1)S(1)} %get-tuple-element.56), channel_id=1, source_target_pairs={{0,48},{8,200},{16,0},{24,216},{32,16},{40,232},{48,32},{56,248},{... | collective-permute-start | bytes 1179656 | tf_op jit(solution)/shard_map/ppermute | solution.py:29
  124.6 8.4 %collective-permute-done.28.prev = bf16[8,6,16,256]{3,2,1,0:T(8,128)(2,1)S(1)} collective-permute-done((bf16[8,6,16,256]{3,2,1,0:T(8,128)(2,1)S(1)}, bf16[8,6,16,256]{3,2,1,0:T(8,128)(2,1)S(1)}, u32[]{:S(2)}, u32[]{:S(2)}) %collective-permute-start.28) | collective-permute-done | bytes 393248 | tf_op jit(solution)/shard_map/ppermute | solution.py:29
  133.8 4.0 %collective-permute-start.31 = (bf16[8,7,8,256]{3,2,1,0:T(8,128)(2,1)S(1)}, bf16[8,7,8,256]{3,2,1,0:T(8,128)(2,1)S(1)}, u32[]{:S(2)}, u32[]{:S(2)}) collective-permute-start(bf16[8,7,8,256]{3,2,1,0:T(8,128)(2,1)S(1)} %get-tuple-element.59), channel_id=1, source_target_pairs={{0,8},{8,0},{16,24},{24,16},{32,40},{40,32},{48,56},{56,48},{64,72... | collective-permute-start | bytes 688136 | tf_op jit(solution)/shard_map/ppermute | solution.py:41
  (73 shorter events, 37.0 us)
Async XLA Ops:
  6.7 15.5 %collective-permute-start.11 = (bf16[2,8,5,16,256]{4,3,2,1,0:T(8,128)(2,1)S(1)}, bf16[2,8,5,16,256]{4,3,2,1,0:T(8,128)(2,1)S(1)}, u32[]{:S(2)}, u32[]{:S(2)}) collective-permute-start(bf16[2,8,5,16,256]{4,3,2,1,0:T(8,128)(2,1)S(1)} %pad_maximum_fusion.src.refs_9_), channel_id=1, source_target_pairs={{0,192},{8,72},{16,208},{24,88},{32,224},{40,104},{48,240},{56,120... | collective-permute-start | bytes 1966088 | tf_op jit(solution)/shard_map/ppermute | solution.py:29
  6.8 15.4 %collective-permute-start.10 = (bf16[2,8,5,16,256]{4,3,2,1,0:T(8,128)(2,1)S(1)}, bf16[2,8,5,16,256]{4,3,2,1,0:T(8,128)(2,1)S(1)}, u32[]{:S(2)}, u32[]{:S(2)}) collective-permute-start(bf16[2,8,5,16,256]{4,3,2,1,0:T(8,128)(2,1)S(1)} %pad_maximum_fusion.src.refs_9_), channel_id=1, source_target_pairs={{0,16},{8,56},{16,32},{24,8},{32,48},{40,24},{48,0},{56,40},{64,80... | collective-permute-start | bytes 1966088 | tf_op jit(solution)/shard_map/ppermute | solution.py:29
  8.9 10.1 %collective-permute-start.4 = (bf16[256,512]{1,0:T(8,128)(2,1)S(1)}, bf16[256,512]{1,0:T(8,128)(2,1)S(1)}, u32[]{:S(2)}, u32[]{:S(2)}) collective-permute-start(bf16[256,512]{1,0:T(8,128)(2,1)S(1)} %pad_maximum_fusion.1.refs_0_), channel_id=1, source_target_pairs={{0,7},{1,0},{2,1},{3,2},{4,3},{5,4},{6,5},{7,6},{8,15},{9,8},{10,9... | collective-permute-start | bytes 786440 | tf_op jit(solution)/shard_map/ppermute | solution.py:53
  14.5 7.6 %collective-permute-start.1 = (bf16[256,512]{1,0:T(8,128)(2,1)S(1)}, bf16[256,512]{1,0:T(8,128)(2,1)S(1)}, u32[]{:S(2)}, u32[]{:S(2)}) collective-permute-start(bf16[256,512]{1,0:T(8,128)(2,1)S(1)} %pad_maximum_fusion.1.refs_0_), channel_id=1, source_target_pairs={{0,1},{1,2},{2,3},{3,4},{4,5},{5,6},{6,7},{7,0},{8,9},{9,10},{10,1... | collective-permute-start | bytes 786440 | tf_op jit(solution)/shard_map/ppermute | solution.py:53
  22.8 11.0 %collective-permute-start.12 = (bf16[2,8,5,16,256]{4,3,2,1,0:T(8,128)(2,1)S(1)}, bf16[2,8,5,16,256]{4,3,2,1,0:T(8,128)(2,1)S(1)}, u32[]{:S(2)}, u32[]{:S(2)}) collective-permute-start(bf16[2,8,5,16,256]{4,3,2,1,0:T(8,128)(2,1)S(1)} %hold.1), channel_id=1, source_target_pairs={{0,48},{8,24},{16,0},{24,40},{32,16},{40,56},{48,32},{56,8},{64,11... | collective-permute-start | bytes 1966088 | tf_op jit(solution)/shard_map/ppermute | solution.py:29
  22.9 10.9 %collective-permute-start.13 = (bf16[2,8,5,16,256]{4,3,2,1,0:T(8,128)(2,1)S(1)}, bf16[2,8,5,16,256]{4,3,2,1,0:T(8,128)(2,1)S(1)}, u32[]{:S(2)}, u32[]{:S(2)}) collective-permute-start(bf16[2,8,5,16,256]{4,3,2,1,0:T(8,128)(2,1)S(1)} %collective-permute-done.10.refs_0_.a.refs_10_), channel_id=1, source_target_pairs={{0,64},{8,200},{16,80},{24,216},{32,96},{40,232},{48,112},{56,248}... | collective-permute-start | bytes 1966088 | tf_op jit(solution)/shard_map/ppermute | solution.py:29
  34.4 7.6 %collective-permute-start.15 = (bf16[1,8,5,16,256]{4,3,2,1,0:T(8,128)(2,1)S(1)}, bf16[1,8,5,16,256]{4,3,2,1,0:T(8,128)(2,1)S(1)}, u32[]{:S(2)}, u32[]{:S(2)}) collective-permute-start(bf16[1,8,5,16,256]{4,3,2,1,0:T(8,128)(2,1)S(1)} %get-tuple-element.34), channel_id=1, source_target_pairs={{0,16},{8,56},{16,32},{24,8},{32,48},{40,24},{48,0},{56,40},{64,80... | collective-permute-start | bytes 983048 | tf_op jit(solution)/shard_map/ppermute | solution.py:29
  38.0 17.4 %collective-permute-start.14 = (bf16[2,8,5,16,256]{4,3,2,1,0:T(8,128)(2,1)S(1)}, bf16[2,8,5,16,256]{4,3,2,1,0:T(8,128)(2,1)S(1)}, u32[]{:S(2)}, u32[]{:S(2)}) collective-permute-start(bf16[2,8,5,16,256]{4,3,2,1,0:T(8,128)(2,1)S(1)} %collective-permute-done.12.c.refs_12_), channel_id=1, source_target_pairs={{0,192},{8,72},{16,208},{24,88},{32,224},{40,104},{48,240},{56,120... | collective-permute-start | bytes 1966088 | tf_op jit(solution)/shard_map/ppermute | solution.py:29
  38.1 10.2 %collective-permute-start.16 = (bf16[1,8,5,16,256]{4,3,2,1,0:T(8,128)(2,1)S(1)}, bf16[1,8,5,16,256]{4,3,2,1,0:T(8,128)(2,1)S(1)}, u32[]{:S(2)}, u32[]{:S(2)}) collective-permute-start(bf16[1,8,5,16,256]{4,3,2,1,0:T(8,128)(2,1)S(1)} %get-tuple-element.35), channel_id=1, source_target_pairs={{0,48},{8,24},{16,0},{24,40},{32,16},{40,56},{48,32},{56,8},{64,11... | collective-permute-start | bytes 983048 | tf_op jit(solution)/shard_map/ppermute | solution.py:29
  38.1 11.5 %collective-permute-start.6 = (bf16[256,512]{1,0:T(8,128)(2,1)S(1)}, bf16[256,512]{1,0:T(8,128)(2,1)S(1)}, u32[]{:S(2)}, u32[]{:S(2)}) collective-permute-start(bf16[256,512]{1,0:T(8,128)(2,1)S(1)} %collective-permute-done.5.refs_2_.refs_5_), channel_id=1, source_target_pairs={{0,7},{1,0},{2,1},{3,2},{4,3},{5,4},{6,5},{7,6},{8,15},{9,8},{10,9... | collective-permute-start | bytes 786440 | tf_op jit(solution)/shard_map/ppermute | solution.py:53
  38.3 11.7 %collective-permute-start.3 = (bf16[256,512]{1,0:T(8,128)(2,1)S(1)}, bf16[256,512]{1,0:T(8,128)(2,1)S(1)}, u32[]{:S(2)}, u32[]{:S(2)}) collective-permute-start(bf16[256,512]{1,0:T(8,128)(2,1)S(1)} %collective-permute-done.2.refs_1_.refs_2_), channel_id=1, source_target_pairs={{0,1},{1,2},{2,3},{3,4},{4,5},{5,6},{6,7},{7,0},{8,9},{9,10},{10,1... | collective-permute-start | bytes 786440 | tf_op jit(solution)/shard_map/ppermute | solution.py:53
  42.0 13.4 %collective-permute-start.17 = (bf16[1,8,5,16,256]{4,3,2,1,0:T(8,128)(2,1)S(1)}, bf16[1,8,5,16,256]{4,3,2,1,0:T(8,128)(2,1)S(1)}, u32[]{:S(2)}, u32[]{:S(2)}) collective-permute-start(bf16[1,8,5,16,256]{4,3,2,1,0:T(8,128)(2,1)S(1)} %collective-permute-done.15.refs_15_), channel_id=1, source_target_pairs={{0,64},{8,200},{16,80},{24,216},{32,96},{40,232},{48,112},{56,248}... | collective-permute-start | bytes 983048 | tf_op jit(solution)/shard_map/ppermute | solution.py:29
  48.3 9.3 %collective-permute-start.18 = (bf16[1,8,5,16,256]{4,3,2,1,0:T(8,128)(2,1)S(1)}, bf16[1,8,5,16,256]{4,3,2,1,0:T(8,128)(2,1)S(1)}, u32[]{:S(2)}, u32[]{:S(2)}) collective-permute-start(bf16[1,8,5,16,256]{4,3,2,1,0:T(8,128)(2,1)S(1)} %collective-permute-done.16.refs_16_), channel_id=1, source_target_pairs={{0,192},{8,72},{16,208},{24,88},{32,224},{40,104},{48,240},{56,120... | collective-permute-start | bytes 983048 | tf_op jit(solution)/shard_map/ppermute | solution.py:29
  61.8 13.4 %collective-permute-start.19 = (bf16[256,2048]{1,0:T(8,128)(2,1)S(1)}, bf16[256,2048]{1,0:T(8,128)(2,1)S(1)}, u32[]{:S(2)}, u32[]{:S(2)}) collective-permute-start(bf16[256,2048]{1,0:T(8,128)(2,1)S(1)} %get-tuple-element.37.mine), channel_id=1, source_target_pairs={{0,8},{8,0},{16,24},{24,16},{32,40},{40,32},{48,56},{56,48},{64,72... | collective-permute-start | bytes 3145736 | tf_op jit(solution)/shard_map/ppermute | solution.py:41
  64.1 7.2 %collective-permute-start.20 = (bf16[64,2048]{1,0:T(8,128)(2,1)S(1)}, bf16[64,2048]{1,0:T(8,128)(2,1)S(1)}, u32[]{:S(2)}, u32[]{:S(2)}) collective-permute-start(bf16[64,2048]{1,0:T(8,128)(2,1)S(1)} %get-tuple-element.38), channel_id=1, source_target_pairs={{0,24},{8,16},{16,40},{24,32},{32,56},{40,48},{48,72},{56,64},{64,... | collective-permute-start | bytes 786440 | tf_op jit(solution)/shard_map/ppermute | solution.py:49
  65.4 9.8 %collective-permute-start.21 = (bf16[64,2048]{1,0:T(8,128)(2,1)S(1)}, bf16[64,2048]{1,0:T(8,128)(2,1)S(1)}, u32[]{:S(2)}, u32[]{:S(2)}) collective-permute-start(bf16[64,2048]{1,0:T(8,128)(2,1)S(1)} %get-tuple-element.39), channel_id=1, source_target_pairs={{16,8},{24,0},{32,24},{40,16},{48,40},{56,32},{64,56},{72,48},{80,... | collective-permute-start | bytes 786440 | tf_op jit(solution)/shard_map/ppermute | solution.py:49
  83.3 21.7 %collective-permute-start.24 = (bf16[8,21,16,256]{3,2,1,0:T(8,128)(2,1)}, bf16[8,21,16,256]{3,2,1,0:T(8,128)(2,1)S(1)}, u32[]{:S(2)}, u32[]{:S(2)}) collective-permute-start(bf16[8,21,16,256]{3,2,1,0:T(8,128)(2,1)} %get-tuple-element.48), channel_id=1, source_target_pairs={{0,64},{8,24},{16,80},{24,40},{32,96},{40,56},{48,112},{56,8},{64,... | collective-permute-start | bytes 4128776 | tf_op jit(solution)/shard_map/ppermute | solution.py:29
  83.8 21.2 %collective-permute-start.25 = (bf16[8,21,16,256]{3,2,1,0:T(8,128)(2,1)}, bf16[8,21,16,256]{3,2,1,0:T(8,128)(2,1)S(1)}, u32[]{:S(2)}, u32[]{:S(2)}) collective-permute-start(bf16[8,21,16,256]{3,2,1,0:T(8,128)(2,1)} %get-tuple-element.49), channel_id=1, source_target_pairs={{0,192},{8,56},{16,208},{24,8},{32,224},{40,24},{48,240},{56,40},{... | collective-permute-start | bytes 4128776 | tf_op jit(solution)/shard_map/ppermute | solution.py:29
  95.0 42.9 %all-to-all-start = ((bf16[16,128,256]{2,1,0:T(8,128)(2,1)}), bf16[16,128,256]{2,1,0:T(8,128)(2,1)}, u32[]{:S(2)}, u32[]{:S(2)}) async-start(bf16[16,128,256]{2,1,0:T(8,128)(2,1)} %maximum_select_fusion._), calls=%async_computation | async-start | bytes 2097152 | tf_op jit(solution)/shard_map/all_to_all | solution.py:451
  107.2 12.2 %collective-permute-start.26 = (bf16[4,22,16,256]{3,2,1,0:T(8,128)(2,1)S(1)}, bf16[4,22,16,256]{3,2,1,0:T(8,128)(2,1)S(1)}, u32[]{:S(2)}, u32[]{:S(2)}) collective-permute-start(bf16[4,22,16,256]{3,2,1,0:T(8,128)(2,1)S(1)} %get-tuple-element.52), channel_id=1, source_target_pairs={{0,64},{8,24},{16,80},{24,40},{32,96},{40,56},{48,112},{56,8},{64,... | collective-permute-start | bytes 2162696 | tf_op jit(solution)/shard_map/ppermute | solution.py:29
  108.5 10.9 %collective-permute-start.27 = (bf16[4,22,16,256]{3,2,1,0:T(8,128)(2,1)S(1)}, bf16[4,22,16,256]{3,2,1,0:T(8,128)(2,1)S(1)}, u32[]{:S(2)}, u32[]{:S(2)}) collective-permute-start(bf16[4,22,16,256]{3,2,1,0:T(8,128)(2,1)S(1)} %get-tuple-element.53), channel_id=1, source_target_pairs={{0,192},{8,56},{16,208},{24,8},{32,224},{40,24},{48,240},{56,40},{... | collective-permute-start | bytes 2162696 | tf_op jit(solution)/shard_map/ppermute | solution.py:29
  120.5 12.4 %collective-permute-start.28 = (bf16[8,6,16,256]{3,2,1,0:T(8,128)(2,1)S(1)}, bf16[8,6,16,256]{3,2,1,0:T(8,128)(2,1)S(1)}, u32[]{:S(2)}, u32[]{:S(2)}) collective-permute-start(bf16[8,6,16,256]{3,2,1,0:T(8,128)(2,1)S(1)} %get-tuple-element.55), channel_id=1, source_target_pairs={{0,16},{8,72},{16,32},{24,88},{32,48},{40,104},{48,0},{56,120},{64... | collective-permute-start | bytes 1179656 | tf_op jit(solution)/shard_map/ppermute | solution.py:29
  120.6 12.3 %collective-permute-start.29 = (bf16[8,6,16,256]{3,2,1,0:T(8,128)(2,1)S(1)}, bf16[8,6,16,256]{3,2,1,0:T(8,128)(2,1)S(1)}, u32[]{:S(2)}, u32[]{:S(2)}) collective-permute-start(bf16[8,6,16,256]{3,2,1,0:T(8,128)(2,1)S(1)} %get-tuple-element.56), channel_id=1, source_target_pairs={{0,48},{8,200},{16,0},{24,216},{32,16},{40,232},{48,32},{56,248},{... | collective-permute-start | bytes 1179656 | tf_op jit(solution)/shard_map/ppermute | solution.py:29
  123.3 9.7 %collective-permute-start.30 = (bf16[8,6,16,256]{3,2,1,0:T(8,128)(2,1)S(1)}, bf16[8,6,16,256]{3,2,1,0:T(8,128)(2,1)S(1)}, u32[]{:S(2)}, u32[]{:S(2)}) collective-permute-start(bf16[8,6,16,256]{3,2,1,0:T(8,128)(2,1)S(1)} %get-tuple-element.57), channel_id=1, source_target_pairs={{0,32},{8,136},{16,48},{24,152},{32,0},{40,168},{48,16},{56,184},{... | collective-permute-start | bytes 1179656 | tf_op jit(solution)/shard_map/ppermute | solution.py:29
  (14 other events, 100.3 us)

commit v8 on v7

--- a/solution.py
+++ b/solution.py
@@ -131,7 +131,7 @@
     plan = weight_plan(meta, pieces)
     core = meta[CORE]
 
-    @pl.loop(0, COLS)
+    @pl.loop(0, COLS, unroll=2)
     def _(c):
         for k in range(NNZ):
             for src, row, slot in plan:
@@ -148,7 +148,7 @@
 
     @pl.when(core == 0)
     def _():
-        @pl.loop(0, COLS)
+        @pl.loop(0, COLS, unroll=2)
         def _(c):
             p = total(c, ((1,), (0,)))
             pre[:, lanes(c)] = p
@@ -157,7 +157,7 @@
 
     @pl.when(core != 0)
     def _():
-        @pl.loop(0, COLS)
+        @pl.loop(0, COLS, unroll=2)
         def _(c):
             out[:, lanes(c)] = total(c, ((1,), (1,))).astype(BF16)
 

time: 142 us -> 141 us (level)
  no operation moved by 1% of the time
where the time goes in v8:
time: 141 us
  waiting for transfers between devices  61.3 us (43%)
  starting transfers between devices  53.9 us (38%)
  Pallas kernels  21 us (15%)
  other arithmetic  3.58 us (3%)
    ppermute x16, waiting for transfers between devices, by_core(): return lax.ppermute(value, ('crop', 'rows'), pairs)  33.3 us
    ppermute x16, starting transfers between devices, by_core(): return lax.ppermute(value, ('crop', 'rows'), pairs)  25 us
    pallas_call x10, Pallas kernels, local(): pl.pallas_call(kernel, out_shape=shapes, in_specs=[SMEM] + [HBM if i in h...  21 us
    ppermute x8, waiting for transfers between devices, along_z(): return lax.ppermute(value, 'hid', [(z, (z + step) % NZ) for z in range(NZ)])  17.1 us
    ppermute x6, starting transfers between devices, to_partner(): return lax.ppermute(value, 'rows', [(r, r ^ 1) for r in range(16)])  11.8 us
    ppermute x8, starting transfers between devices, along_z(): return lax.ppermute(value, 'hid', [(z, (z + step) % NZ) for z in range(NZ)])  10.2 us
    ppermute x2, waiting for transfers between devices, to_next_chip(): return lax.ppermute(value, 'rows', pairs)  8.54 us
    all_to_all x1, starting transfers between devices, on_device(): terms = lax.all_to_all(terms, 'hid', 0, 0, tiled=True)  4.26 us
  transfers between devices with their start and end apart: 33, of which 18 were waited for; matrix products, arithmetic and copies ran while one was open for 2% of the time, Pallas kernels for 5%

profile of v8, /device:TPU:1, one launch (start us, length us, event | category | flops | bytes accessed | tf_op | source)
XLA Modules:
  0.0 140.9 jit_solution(14060001397663650225)
XLA Ops:
  1.9 3.3 %collective-permute-start.9 = (bf16[8,5,16,256]{3,2,1,0:T(8,128)(2,1)S(1)}, bf16[8,5,16,256]{3,2,1,0:T(8,128)(2,1)S(1)}, u32[]{:S(2)}, u32[]{:S(2)}) collective-permute-start(bf16[8,5,16,256]{3,2,1,0:T(8,128)(2,1)S(1)} %select_bitcast_fusion), channel_id=1, source_target_pairs={{0,8},{8,0},{16,24},{24,16},{32,40},{40,32},{48,56},{56,48},{64,72... | collective-permute-start | bytes 983048 | tf_op jit(solution)/shard_map/ppermute | solution.py:41
  8.9 5.7 %collective-permute-start.4 = (bf16[256,512]{1,0:T(8,128)(2,1)S(1)}, bf16[256,512]{1,0:T(8,128)(2,1)S(1)}, u32[]{:S(2)}, u32[]{:S(2)}) collective-permute-start(bf16[256,512]{1,0:T(8,128)(2,1)S(1)} %pad_maximum_fusion.1.refs_0_), channel_id=1, source_target_pairs={{0,7},{1,0},{2,1},{3,2},{4,3},{5,4},{6,5},{7,6},{8,15},{9,8},{10,9... | collective-permute-start | bytes 786440 | tf_op jit(solution)/shard_map/ppermute | solution.py:53
  14.7 4.3 %collective-permute-done.4.refs_3_.refs_4_ = bf16[256,512]{1,0:T(8,128)(2,1)S(1)} collective-permute-done((bf16[256,512]{1,0:T(8,128)(2,1)S(1)}, bf16[256,512]{1,0:T(8,128)(2,1)S(1)}, u32[]{:S(2)}, u32[]{:S(2)}) %collective-permute-start.4) | collective-permute-done | bytes 262176 | tf_op jit(solution)/shard_map/ppermute | solution.py:53
  19.0 3.1 %collective-permute-done.1.refs_2_.refs_1_ = bf16[256,512]{1,0:T(8,128)(2,1)S(1)} collective-permute-done((bf16[256,512]{1,0:T(8,128)(2,1)S(1)}, bf16[256,512]{1,0:T(8,128)(2,1)S(1)}, u32[]{:S(2)}, u32[]{:S(2)}) %collective-permute-start.1) | collective-permute-done | bytes 262176 | tf_op jit(solution)/shard_map/ppermute | solution.py:53
  22.9 2.8 %collective-permute-start.13 = (bf16[2,8,5,16,256]{4,3,2,1,0:T(8,128)(2,1)S(1)}, bf16[2,8,5,16,256]{4,3,2,1,0:T(8,128)(2,1)S(1)}, u32[]{:S(2)}, u32[]{:S(2)}) collective-permute-start(bf16[2,8,5,16,256]{4,3,2,1,0:T(8,128)(2,1)S(1)} %collective-permute-done.10.refs_0_.a.refs_10_), channel_id=1, source_target_pairs={{0,64},{8,200},{16,80},{24,216},{32,96},{40,232},{48,112},{56,248}... | collective-permute-start | bytes 1966088 | tf_op jit(solution)/shard_map/ppermute | solution.py:29
  27.1 4.4 %collective-permute-done.5.refs_2_.refs_5_ = bf16[256,512]{1,0:T(8,128)(2,1)S(1)} collective-permute-done((bf16[256,512]{1,0:T(8,128)(2,1)S(1)}, bf16[256,512]{1,0:T(8,128)(2,1)S(1)}, u32[]{:S(2)}, u32[]{:S(2)}) %collective-permute-start.5) | collective-permute-done | bytes 262176 | tf_op jit(solution)/shard_map/ppermute | solution.py:53
  34.4 3.6 %collective-permute-start.15 = (bf16[1,8,5,16,256]{4,3,2,1,0:T(8,128)(2,1)S(1)}, bf16[1,8,5,16,256]{4,3,2,1,0:T(8,128)(2,1)S(1)}, u32[]{:S(2)}, u32[]{:S(2)}) collective-permute-start(bf16[1,8,5,16,256]{4,3,2,1,0:T(8,128)(2,1)S(1)} %get-tuple-element.34), channel_id=1, source_target_pairs={{0,16},{8,56},{16,32},{24,8},{32,48},{40,24},{48,0},{56,40},{64,80... | collective-permute-start | bytes 983048 | tf_op jit(solution)/shard_map/ppermute | solution.py:29
  39.6 2.4 %collective-permute-done.15.refs_15_ = bf16[1,8,5,16,256]{4,3,2,1,0:T(8,128)(2,1)S(1)} collective-permute-done((bf16[1,8,5,16,256]{4,3,2,1,0:T(8,128)(2,1)S(1)}, bf16[1,8,5,16,256]{4,3,2,1,0:T(8,128)(2,1)S(1)}, u32[]{:S(2)}, u32[]{:S(2)}) %collective-permute-start.15) | collective-permute-done | bytes 327712 | tf_op jit(solution)/shard_map/ppermute | solution.py:29
  43.8 4.5 %collective-permute-done.16.refs_16_ = bf16[1,8,5,16,256]{4,3,2,1,0:T(8,128)(2,1)S(1)} collective-permute-done((bf16[1,8,5,16,256]{4,3,2,1,0:T(8,128)(2,1)S(1)}, bf16[1,8,5,16,256]{4,3,2,1,0:T(8,128)(2,1)S(1)}, u32[]{:S(2)}, u32[]{:S(2)}) %collective-permute-start.16) | collective-permute-done | bytes 327712 | tf_op jit(solution)/shard_map/ppermute | solution.py:29
  51.3 2.5 %collective-permute-done.8.refs_8_ = bf16[128,512]{1,0:T(8,128)(2,1)S(1)} collective-permute-done((bf16[128,512]{1,0:T(8,128)(2,1)S(1)}, bf16[128,512]{1,0:T(8,128)(2,1)S(1)}, u32[]{:S(2)}, u32[]{:S(2)}) %collective-permute-start.8) | collective-permute-done | bytes 131104 | tf_op jit(solution)/shard_map/ppermute | solution.py:53
  55.4 2.1 %collective-permute-done.18.refs_18_ = bf16[1,8,5,16,256]{4,3,2,1,0:T(8,128)(2,1)S(1)} collective-permute-done((bf16[1,8,5,16,256]{4,3,2,1,0:T(8,128)(2,1)S(1)}, bf16[1,8,5,16,256]{4,3,2,1,0:T(8,128)(2,1)S(1)}, u32[]{:S(2)}, u32[]{:S(2)}) %collective-permute-start.18) | collective-permute-done | bytes 327712 | tf_op jit(solution)/shard_map/ppermute | solution.py:29
  57.6 3.5 %forward.1 = (f32[256,2048]{1,0:T(8,128)S(1)}, bf16[256,2048]{1,0:T(8,128)(2,1)S(1)}, bf16[64,2048]{1,0:T(8,128)(2,1)S(1)}, bf16[64,2048]{1,0:T(8,128)(2,1)S(1)}...) custom-call(s32[45]{0:T(128)S(1)} %concatenate.9.meta, ...), custom_call_target="tpu_custom_call" | custom-call | flops 1342177280 | bytes 7340032 | tf_op jit(solution)/shard_map/forward/pallas_call | solution.py:65
  61.0 2.5 %collective-permute-start.19 = (bf16[256,2048]{1,0:T(8,128)(2,1)S(1)}, bf16[256,2048]{1,0:T(8,128)(2,1)S(1)}, u32[]{:S(2)}, u32[]{:S(2)}) collective-permute-start(bf16[256,2048]{1,0:T(8,128)(2,1)S(1)} %get-tuple-element.37.mine), channel_id=1, source_target_pairs={{0,8},{8,0},{16,24},{24,16},{32,40},{40,32},{48,56},{56,48},{64,72... | collective-permute-start | bytes 3145736 | tf_op jit(solution)/shard_map/ppermute | solution.py:41
  66.1 4.6 %collective-permute-done.20.up = bf16[64,2048]{1,0:T(8,128)(2,1)S(1)} collective-permute-done((bf16[64,2048]{1,0:T(8,128)(2,1)S(1)}, bf16[64,2048]{1,0:T(8,128)(2,1)S(1)}, u32[]{:S(2)}, u32[]{:S(2)}) %collective-permute-start.20) | collective-permute-done | bytes 262176 | tf_op jit(solution)/shard_map/ppermute | solution.py:49
  70.7 4.0 %collective-permute-done.21.down = bf16[64,2048]{1,0:T(8,128)(2,1)S(1)} collective-permute-done((bf16[64,2048]{1,0:T(8,128)(2,1)S(1)}, bf16[64,2048]{1,0:T(8,128)(2,1)S(1)}, u32[]{:S(2)}, u32[]{:S(2)}) %collective-permute-start.21) | collective-permute-done | bytes 262176 | tf_op jit(solution)/shard_map/ppermute | solution.py:49
  74.6 8.1 %backward.1 = (bf16[8,21,16,256]{3,2,1,0:T(8,128)(2,1)}, bf16[8,21,16,256]{3,2,1,0:T(8,128)(2,1)}, bf16[8,21,16,256]{3,2,1,0:T(8,128)(2,1)}, bf16[4,21,16,256]{3...) custom-call(s32[45]{0:T(128)S(1)} %concatenate.9.meta, ...), custom_call_target="tpu_custom_call" | custom-call | flops 1342177280 | bytes 6889472 | tf_op jit(solution)/shard_map/backward/pallas_call | solution.py:65
  83.2 5.4 %collective-permute-start.25 = (bf16[8,21,16,256]{3,2,1,0:T(8,128)(2,1)}, bf16[8,21,16,256]{3,2,1,0:T(8,128)(2,1)S(1)}, u32[]{:S(2)}, u32[]{:S(2)}) collective-permute-start(bf16[8,21,16,256]{3,2,1,0:T(8,128)(2,1)} %get-tuple-element.49), channel_id=1, source_target_pairs={{0,192},{8,56},{16,208},{24,8},{32,224},{40,24},{48,240},{56,40},{... | collective-permute-start | bytes 4128776 | tf_op jit(solution)/shard_map/ppermute | solution.py:29
  94.4 4.3 %all-to-all-start = ((bf16[16,128,256]{2,1,0:T(8,128)(2,1)}), bf16[16,128,256]{2,1,0:T(8,128)(2,1)}, u32[]{:S(2)}, u32[]{:S(2)}) async-start(bf16[16,128,256]{2,1,0:T(8,128)(2,1)} %maximum_select_fusion._), calls=%async_computation | async-start | bytes 2097152 | tf_op jit(solution)/shard_map/all_to_all | solution.py:451
  98.6 5.8 %collective-permute-done.24.m1 = bf16[8,21,16,256]{3,2,1,0:T(8,128)(2,1)S(1)} collective-permute-done((bf16[8,21,16,256]{3,2,1,0:T(8,128)(2,1)}, bf16[8,21,16,256]{3,2,1,0:T(8,128)(2,1)S(1)}, u32[]{:S(2)}, u32[]{:S(2)}) %collective-permute-start.24) | collective-permute-done | bytes 1376288 | tf_op jit(solution)/shard_map/ppermute | solution.py:29
  104.4 2.2 %relay.1 = (bf16[4,22,16,256]{3,2,1,0:T(8,128)(2,1)S(1)}, bf16[4,22,16,256]{3,2,1,0:T(8,128)(2,1)S(1)}) custom-call(s32[45]{0:T(128)S(1)} %concatenate.9.meta, bf16[4,21,16,256]{3,2,1,0:T(8,128)(2,1)} %get-tuple-element.50.s1, bf16[4,21,16,256]{3,2,1,0:T(8,128)(2,1)} %get-tuple-element.51.s3, bf16[8,21,16,256]{3,2,1,0:T(8,128)(2,1)S(1)} %collective-permute-done.24.m1, ...), custom_call_target="tpu_custom_call" | custom-call | flops 1048576 | bytes 5177344 | tf_op jit(solution)/shard_map/relay/pallas_call | solution.py:65
  109.9 9.0 %collective-permute-done.26.p1 = bf16[4,22,16,256]{3,2,1,0:T(8,128)(2,1)S(1)} collective-permute-done((bf16[4,22,16,256]{3,2,1,0:T(8,128)(2,1)S(1)}, bf16[4,22,16,256]{3,2,1,0:T(8,128)(2,1)S(1)}, u32[]{:S(2)}, u32[]{:S(2)}) %collective-permute-start.26) | collective-permute-done | bytes 720928 | tf_op jit(solution)/shard_map/ppermute | solution.py:29
  120.1 2.7 %collective-permute-start.29 = (bf16[8,6,16,256]{3,2,1,0:T(8,128)(2,1)S(1)}, bf16[8,6,16,256]{3,2,1,0:T(8,128)(2,1)S(1)}, u32[]{:S(2)}, u32[]{:S(2)}) collective-permute-start(bf16[8,6,16,256]{3,2,1,0:T(8,128)(2,1)S(1)} %get-tuple-element.56), channel_id=1, source_target_pairs={{0,48},{8,200},{16,0},{24,216},{32,16},{40,232},{48,32},{56,248},{... | collective-permute-start | bytes 1179656 | tf_op jit(solution)/shard_map/ppermute | solution.py:29
  124.0 8.4 %collective-permute-done.28.prev = bf16[8,6,16,256]{3,2,1,0:T(8,128)(2,1)S(1)} collective-permute-done((bf16[8,6,16,256]{3,2,1,0:T(8,128)(2,1)S(1)}, bf16[8,6,16,256]{3,2,1,0:T(8,128)(2,1)S(1)}, u32[]{:S(2)}, u32[]{:S(2)}) %collective-permute-start.28) | collective-permute-done | bytes 393248 | tf_op jit(solution)/shard_map/ppermute | solution.py:29
  133.2 4.0 %collective-permute-start.31 = (bf16[8,7,8,256]{3,2,1,0:T(8,128)(2,1)S(1)}, bf16[8,7,8,256]{3,2,1,0:T(8,128)(2,1)S(1)}, u32[]{:S(2)}, u32[]{:S(2)}) collective-permute-start(bf16[8,7,8,256]{3,2,1,0:T(8,128)(2,1)S(1)} %get-tuple-element.59), channel_id=1, source_target_pairs={{0,8},{8,0},{16,24},{24,16},{32,40},{40,32},{48,56},{56,48},{64,72... | collective-permute-start | bytes 688136 | tf_op jit(solution)/shard_map/ppermute | solution.py:41
  (73 shorter events, 37.0 us)
Async XLA Ops:
  6.7 15.5 %collective-permute-start.11 = (bf16[2,8,5,16,256]{4,3,2,1,0:T(8,128)(2,1)S(1)}, bf16[2,8,5,16,256]{4,3,2,1,0:T(8,128)(2,1)S(1)}, u32[]{:S(2)}, u32[]{:S(2)}) collective-permute-start(bf16[2,8,5,16,256]{4,3,2,1,0:T(8,128)(2,1)S(1)} %pad_maximum_fusion.src.refs_9_), channel_id=1, source_target_pairs={{0,192},{8,72},{16,208},{24,88},{32,224},{40,104},{48,240},{56,120... | collective-permute-start | bytes 1966088 | tf_op jit(solution)/shard_map/ppermute | solution.py:29
  6.8 15.4 %collective-permute-start.10 = (bf16[2,8,5,16,256]{4,3,2,1,0:T(8,128)(2,1)S(1)}, bf16[2,8,5,16,256]{4,3,2,1,0:T(8,128)(2,1)S(1)}, u32[]{:S(2)}, u32[]{:S(2)}) collective-permute-start(bf16[2,8,5,16,256]{4,3,2,1,0:T(8,128)(2,1)S(1)} %pad_maximum_fusion.src.refs_9_), channel_id=1, source_target_pairs={{0,16},{8,56},{16,32},{24,8},{32,48},{40,24},{48,0},{56,40},{64,80... | collective-permute-start | bytes 1966088 | tf_op jit(solution)/shard_map/ppermute | solution.py:29
  8.9 10.1 %collective-permute-start.4 = (bf16[256,512]{1,0:T(8,128)(2,1)S(1)}, bf16[256,512]{1,0:T(8,128)(2,1)S(1)}, u32[]{:S(2)}, u32[]{:S(2)}) collective-permute-start(bf16[256,512]{1,0:T(8,128)(2,1)S(1)} %pad_maximum_fusion.1.refs_0_), channel_id=1, source_target_pairs={{0,7},{1,0},{2,1},{3,2},{4,3},{5,4},{6,5},{7,6},{8,15},{9,8},{10,9... | collective-permute-start | bytes 786440 | tf_op jit(solution)/shard_map/ppermute | solution.py:53
  14.5 7.6 %collective-permute-start.1 = (bf16[256,512]{1,0:T(8,128)(2,1)S(1)}, bf16[256,512]{1,0:T(8,128)(2,1)S(1)}, u32[]{:S(2)}, u32[]{:S(2)}) collective-permute-start(bf16[256,512]{1,0:T(8,128)(2,1)S(1)} %pad_maximum_fusion.1.refs_0_), channel_id=1, source_target_pairs={{0,1},{1,2},{2,3},{3,4},{4,5},{5,6},{6,7},{7,0},{8,9},{9,10},{10,1... | collective-permute-start | bytes 786440 | tf_op jit(solution)/shard_map/ppermute | solution.py:53
  22.8 11.0 %collective-permute-start.12 = (bf16[2,8,5,16,256]{4,3,2,1,0:T(8,128)(2,1)S(1)}, bf16[2,8,5,16,256]{4,3,2,1,0:T(8,128)(2,1)S(1)}, u32[]{:S(2)}, u32[]{:S(2)}) collective-permute-start(bf16[2,8,5,16,256]{4,3,2,1,0:T(8,128)(2,1)S(1)} %hold.1), channel_id=1, source_target_pairs={{0,48},{8,24},{16,0},{24,40},{32,16},{40,56},{48,32},{56,8},{64,11... | collective-permute-start | bytes 1966088 | tf_op jit(solution)/shard_map/ppermute | solution.py:29
  22.9 10.9 %collective-permute-start.13 = (bf16[2,8,5,16,256]{4,3,2,1,0:T(8,128)(2,1)S(1)}, bf16[2,8,5,16,256]{4,3,2,1,0:T(8,128)(2,1)S(1)}, u32[]{:S(2)}, u32[]{:S(2)}) collective-permute-start(bf16[2,8,5,16,256]{4,3,2,1,0:T(8,128)(2,1)S(1)} %collective-permute-done.10.refs_0_.a.refs_10_), channel_id=1, source_target_pairs={{0,64},{8,200},{16,80},{24,216},{32,96},{40,232},{48,112},{56,248}... | collective-permute-start | bytes 1966088 | tf_op jit(solution)/shard_map/ppermute | solution.py:29
  34.4 7.6 %collective-permute-start.15 = (bf16[1,8,5,16,256]{4,3,2,1,0:T(8,128)(2,1)S(1)}, bf16[1,8,5,16,256]{4,3,2,1,0:T(8,128)(2,1)S(1)}, u32[]{:S(2)}, u32[]{:S(2)}) collective-permute-start(bf16[1,8,5,16,256]{4,3,2,1,0:T(8,128)(2,1)S(1)} %get-tuple-element.34), channel_id=1, source_target_pairs={{0,16},{8,56},{16,32},{24,8},{32,48},{40,24},{48,0},{56,40},{64,80... | collective-permute-start | bytes 983048 | tf_op jit(solution)/shard_map/ppermute | solution.py:29
  38.0 17.4 %collective-permute-start.14 = (bf16[2,8,5,16,256]{4,3,2,1,0:T(8,128)(2,1)S(1)}, bf16[2,8,5,16,256]{4,3,2,1,0:T(8,128)(2,1)S(1)}, u32[]{:S(2)}, u32[]{:S(2)}) collective-permute-start(bf16[2,8,5,16,256]{4,3,2,1,0:T(8,128)(2,1)S(1)} %collective-permute-done.12.c.refs_12_), channel_id=1, source_target_pairs={{0,192},{8,72},{16,208},{24,88},{32,224},{40,104},{48,240},{56,120... | collective-permute-start | bytes 1966088 | tf_op jit(solution)/shard_map/ppermute | solution.py:29
  38.1 10.2 %collective-permute-start.16 = (bf16[1,8,5,16,256]{4,3,2,1,0:T(8,128)(2,1)S(1)}, bf16[1,8,5,16,256]{4,3,2,1,0:T(8,128)(2,1)S(1)}, u32[]{:S(2)}, u32[]{:S(2)}) collective-permute-start(bf16[1,8,5,16,256]{4,3,2,1,0:T(8,128)(2,1)S(1)} %get-tuple-element.35), channel_id=1, source_target_pairs={{0,48},{8,24},{16,0},{24,40},{32,16},{40,56},{48,32},{56,8},{64,11... | collective-permute-start | bytes 983048 | tf_op jit(solution)/shard_map/ppermute | solution.py:29
  38.1 11.5 %collective-permute-start.6 = (bf16[256,512]{1,0:T(8,128)(2,1)S(1)}, bf16[256,512]{1,0:T(8,128)(2,1)S(1)}, u32[]{:S(2)}, u32[]{:S(2)}) collective-permute-start(bf16[256,512]{1,0:T(8,128)(2,1)S(1)} %collective-permute-done.5.refs_2_.refs_5_), channel_id=1, source_target_pairs={{0,7},{1,0},{2,1},{3,2},{4,3},{5,4},{6,5},{7,6},{8,15},{9,8},{10,9... | collective-permute-start | bytes 786440 | tf_op jit(solution)/shard_map/ppermute | solution.py:53
  38.3 11.7 %collective-permute-start.3 = (bf16[256,512]{1,0:T(8,128)(2,1)S(1)}, bf16[256,512]{1,0:T(8,128)(2,1)S(1)}, u32[]{:S(2)}, u32[]{:S(2)}) collective-permute-start(bf16[256,512]{1,0:T(8,128)(2,1)S(1)} %collective-permute-done.2.refs_1_.refs_2_), channel_id=1, source_target_pairs={{0,1},{1,2},{2,3},{3,4},{4,5},{5,6},{6,7},{7,0},{8,9},{9,10},{10,1... | collective-permute-start | bytes 786440 | tf_op jit(solution)/shard_map/ppermute | solution.py:53
  42.0 13.4 %collective-permute-start.17 = (bf16[1,8,5,16,256]{4,3,2,1,0:T(8,128)(2,1)S(1)}, bf16[1,8,5,16,256]{4,3,2,1,0:T(8,128)(2,1)S(1)}, u32[]{:S(2)}, u32[]{:S(2)}) collective-permute-start(bf16[1,8,5,16,256]{4,3,2,1,0:T(8,128)(2,1)S(1)} %collective-permute-done.15.refs_15_), channel_id=1, source_target_pairs={{0,64},{8,200},{16,80},{24,216},{32,96},{40,232},{48,112},{56,248}... | collective-permute-start | bytes 983048 | tf_op jit(solution)/shard_map/ppermute | solution.py:29
  48.3 9.3 %collective-permute-start.18 = (bf16[1,8,5,16,256]{4,3,2,1,0:T(8,128)(2,1)S(1)}, bf16[1,8,5,16,256]{4,3,2,1,0:T(8,128)(2,1)S(1)}, u32[]{:S(2)}, u32[]{:S(2)}) collective-permute-start(bf16[1,8,5,16,256]{4,3,2,1,0:T(8,128)(2,1)S(1)} %collective-permute-done.16.refs_16_), channel_id=1, source_target_pairs={{0,192},{8,72},{16,208},{24,88},{32,224},{40,104},{48,240},{56,120... | collective-permute-start | bytes 983048 | tf_op jit(solution)/shard_map/ppermute | solution.py:29
  61.0 13.6 %collective-permute-start.19 = (bf16[256,2048]{1,0:T(8,128)(2,1)S(1)}, bf16[256,2048]{1,0:T(8,128)(2,1)S(1)}, u32[]{:S(2)}, u32[]{:S(2)}) collective-permute-start(bf16[256,2048]{1,0:T(8,128)(2,1)S(1)} %get-tuple-element.37.mine), channel_id=1, source_target_pairs={{0,8},{8,0},{16,24},{24,16},{32,40},{40,32},{48,56},{56,48},{64,72... | collective-permute-start | bytes 3145736 | tf_op jit(solution)/shard_map/ppermute | solution.py:41
  63.5 7.2 %collective-permute-start.20 = (bf16[64,2048]{1,0:T(8,128)(2,1)S(1)}, bf16[64,2048]{1,0:T(8,128)(2,1)S(1)}, u32[]{:S(2)}, u32[]{:S(2)}) collective-permute-start(bf16[64,2048]{1,0:T(8,128)(2,1)S(1)} %get-tuple-element.38), channel_id=1, source_target_pairs={{0,24},{8,16},{16,40},{24,32},{32,56},{40,48},{48,72},{56,64},{64,... | collective-permute-start | bytes 786440 | tf_op jit(solution)/shard_map/ppermute | solution.py:49
  64.8 9.8 %collective-permute-start.21 = (bf16[64,2048]{1,0:T(8,128)(2,1)S(1)}, bf16[64,2048]{1,0:T(8,128)(2,1)S(1)}, u32[]{:S(2)}, u32[]{:S(2)}) collective-permute-start(bf16[64,2048]{1,0:T(8,128)(2,1)S(1)} %get-tuple-element.39), channel_id=1, source_target_pairs={{16,8},{24,0},{32,24},{40,16},{48,40},{56,32},{64,56},{72,48},{80,... | collective-permute-start | bytes 786440 | tf_op jit(solution)/shard_map/ppermute | solution.py:49
  82.7 21.7 %collective-permute-start.24 = (bf16[8,21,16,256]{3,2,1,0:T(8,128)(2,1)}, bf16[8,21,16,256]{3,2,1,0:T(8,128)(2,1)S(1)}, u32[]{:S(2)}, u32[]{:S(2)}) collective-permute-start(bf16[8,21,16,256]{3,2,1,0:T(8,128)(2,1)} %get-tuple-element.48), channel_id=1, source_target_pairs={{0,64},{8,24},{16,80},{24,40},{32,96},{40,56},{48,112},{56,8},{64,... | collective-permute-start | bytes 4128776 | tf_op jit(solution)/shard_map/ppermute | solution.py:29
  83.2 21.2 %collective-permute-start.25 = (bf16[8,21,16,256]{3,2,1,0:T(8,128)(2,1)}, bf16[8,21,16,256]{3,2,1,0:T(8,128)(2,1)S(1)}, u32[]{:S(2)}, u32[]{:S(2)}) collective-permute-start(bf16[8,21,16,256]{3,2,1,0:T(8,128)(2,1)} %get-tuple-element.49), channel_id=1, source_target_pairs={{0,192},{8,56},{16,208},{24,8},{32,224},{40,24},{48,240},{56,40},{... | collective-permute-start | bytes 4128776 | tf_op jit(solution)/shard_map/ppermute | solution.py:29
  94.4 42.9 %all-to-all-start = ((bf16[16,128,256]{2,1,0:T(8,128)(2,1)}), bf16[16,128,256]{2,1,0:T(8,128)(2,1)}, u32[]{:S(2)}, u32[]{:S(2)}) async-start(bf16[16,128,256]{2,1,0:T(8,128)(2,1)} %maximum_select_fusion._), calls=%async_computation | async-start | bytes 2097152 | tf_op jit(solution)/shard_map/all_to_all | solution.py:451
  106.6 12.2 %collective-permute-start.26 = (bf16[4,22,16,256]{3,2,1,0:T(8,128)(2,1)S(1)}, bf16[4,22,16,256]{3,2,1,0:T(8,128)(2,1)S(1)}, u32[]{:S(2)}, u32[]{:S(2)}) collective-permute-start(bf16[4,22,16,256]{3,2,1,0:T(8,128)(2,1)S(1)} %get-tuple-element.52), channel_id=1, source_target_pairs={{0,64},{8,24},{16,80},{24,40},{32,96},{40,56},{48,112},{56,8},{64,... | collective-permute-start | bytes 2162696 | tf_op jit(solution)/shard_map/ppermute | solution.py:29
  108.0 10.9 %collective-permute-start.27 = (bf16[4,22,16,256]{3,2,1,0:T(8,128)(2,1)S(1)}, bf16[4,22,16,256]{3,2,1,0:T(8,128)(2,1)S(1)}, u32[]{:S(2)}, u32[]{:S(2)}) collective-permute-start(bf16[4,22,16,256]{3,2,1,0:T(8,128)(2,1)S(1)} %get-tuple-element.53), channel_id=1, source_target_pairs={{0,192},{8,56},{16,208},{24,8},{32,224},{40,24},{48,240},{56,40},{... | collective-permute-start | bytes 2162696 | tf_op jit(solution)/shard_map/ppermute | solution.py:29
  120.0 12.4 %collective-permute-start.28 = (bf16[8,6,16,256]{3,2,1,0:T(8,128)(2,1)S(1)}, bf16[8,6,16,256]{3,2,1,0:T(8,128)(2,1)S(1)}, u32[]{:S(2)}, u32[]{:S(2)}) collective-permute-start(bf16[8,6,16,256]{3,2,1,0:T(8,128)(2,1)S(1)} %get-tuple-element.55), channel_id=1, source_target_pairs={{0,16},{8,72},{16,32},{24,88},{32,48},{40,104},{48,0},{56,120},{64... | collective-permute-start | bytes 1179656 | tf_op jit(solution)/shard_map/ppermute | solution.py:29
  120.1 12.3 %collective-permute-start.29 = (bf16[8,6,16,256]{3,2,1,0:T(8,128)(2,1)S(1)}, bf16[8,6,16,256]{3,2,1,0:T(8,128)(2,1)S(1)}, u32[]{:S(2)}, u32[]{:S(2)}) collective-permute-start(bf16[8,6,16,256]{3,2,1,0:T(8,128)(2,1)S(1)} %get-tuple-element.56), channel_id=1, source_target_pairs={{0,48},{8,200},{16,0},{24,216},{32,16},{40,232},{48,32},{56,248},{... | collective-permute-start | bytes 1179656 | tf_op jit(solution)/shard_map/ppermute | solution.py:29
  122.7 9.7 %collective-permute-start.30 = (bf16[8,6,16,256]{3,2,1,0:T(8,128)(2,1)S(1)}, bf16[8,6,16,256]{3,2,1,0:T(8,128)(2,1)S(1)}, u32[]{:S(2)}, u32[]{:S(2)}) collective-permute-start(bf16[8,6,16,256]{3,2,1,0:T(8,128)(2,1)S(1)} %get-tuple-element.57), channel_id=1, source_target_pairs={{0,32},{8,136},{16,48},{24,152},{32,0},{40,168},{48,16},{56,184},{... | collective-permute-start | bytes 1179656 | tf_op jit(solution)/shard_map/ppermute | solution.py:29
  (14 other events, 99.8 us)
